TPU v7x, 256 devices: a whole 4x4x8 slice. The times are simulated.
256 devices in a mesh: batch: 4 (over x_lo, core), seq: 64 (over y, z, x_hi).
Axes of the slice: x: 4 (x_hi: 2, x_lo: 2; x = x_hi * 2 + x_lo), y: 4, z: 8, core: 2. Of those that a mesh axis runs over, the one named last changes fastest.
Arguments:
- tokens: bfloat16 [1216, 262144], P('batch', 'seq'), parts along dimension 0, may hold values from -6 to 6
- norm_gain: float32 [2, 304], replicated, may hold values from 0.5 to 1.5
- in_weight: bfloat16 [2, 608, 304], replicated, may hold values from -0.3125 to 0.3125
- in_bias: float32 [2, 608], replicated, may hold values from -3 to 3
- out_weight: bfloat16 [2, 304, 608], replicated, may hold values from -0.25 to 0.25
- out_bias: float32 [2, 304], replicated, may hold values from -3 to 3
Outputs:
- mixed: bfloat16 [1216, 262144], P('batch', 'seq'), parts along dimension 0
There are 4 independent parts, one for each index of `batch`. A program takes and returns all parts, laid end to end along the dimension named above; an argument that names none is the same for every part. Nothing has to cross between parts.
All inputs are finite; a program needn't handle non-finite values.
Results may differ from a plain program's by a relative error of at most 0.0056.
Values may be sent and summed in bfloat16 or wider, within the bound.
No kernel may reach another device: no remote copies, remote signals or barrier semaphores. Data moves between devices by JAX's collectives and lax.ppermute only.
A program may use at most 64 MiB of HBM per device.

v0:
```python
import jax
import jax.numpy as jnp
from jax import lax
from jax.sharding import PartitionSpec as P

TRACK_CH = 16
TRACKS = 19
BLOCKS = 2


def shifted(value, axis, steps):
    count = lax.axis_size(axis)
    pairs = [(source, (source + steps) % count) for source in range(count)]
    return lax.ppermute(value, axis, pairs)


def mix_rows(rotated, gain, in_weight, in_bias, out_weight, out_bias):
    as_float = rotated.astype(jnp.float32)
    mean_square = jnp.mean(as_float * as_float, axis=0, keepdims=True)
    normed = (as_float * gain[:, None] * lax.rsqrt(mean_square + 1e-06)).astype(jnp.bfloat16)
    pre_act = jnp.dot(in_weight, normed, preferred_element_type=jnp.float32) + in_bias[:, None]
    active = jax.nn.gelu(pre_act, approximate=True).astype(jnp.bfloat16)
    summed = (
        as_float
        + jnp.dot(out_weight, active, preferred_element_type=jnp.float32)
        + out_bias[:, None]
    )
    return summed.astype(jnp.bfloat16)


def rotate(current, local_rows):
    short_count = 0
    while short_count + 1 < TRACKS and 2**short_count < local_rows:
        short_count = short_count + 1
    short_slab = current[TRACK_CH : (1 + short_count) * TRACK_CH].reshape(
        short_count, TRACK_CH, local_rows
    )
    pieces = [current[0:TRACK_CH]]
    bundle = jnp.concatenate(
        [short_slab[slot, :, local_rows - 2**slot :] for slot in range(short_count)], 1
    )
    received = shifted(bundle, "seq", 1)
    for slot in range(short_count):
        offset = 2**slot
        begin = offset - 1
        pieces.append(
            jnp.concatenate(
                [received[:, begin : begin + offset], short_slab[slot, :, : local_rows - offset]], 1
            )
        )
    for track_no in range(1 + short_count, TRACKS):
        offset = 2 ** (track_no - 1)
        one_track = current[track_no * TRACK_CH : (track_no + 1) * TRACK_CH]
        distance = offset // local_rows
        pieces.append(shifted(one_track, "seq", distance))
    return jnp.concatenate(pieces, 0)


def shards(tokens, norm_gain, in_weight, in_bias, out_weight, out_bias):
    local_rows = tokens.shape[1]
    current = tokens
    for block_no in range(BLOCKS):
        rotated = rotate(current, local_rows)
        current = mix_rows(
            rotated,
            norm_gain[block_no],
            in_weight[block_no],
            in_bias[block_no],
            out_weight[block_no],
            out_bias[block_no],
        )
    return current


def solution(mesh):
    return jax.shard_map(
        shards,
        mesh=mesh,
        in_specs=(P("batch", "seq"), P(), P(), P(), P(), P()),
        out_specs=P("batch", "seq"),
        check_vma=False,
    )
```

profile of v0, /device:TPU:2, one launch (start us, length us, event | category | flops | bytes accessed | tf_op | source)
XLA Modules:
  0.0 117.8 jit_solution(3728276464569918834)
XLA Ops:
  0.0 1.5 %slice.295 = bf16[192,4096]{1,0:T(8,128)(2,1)S(1)} slice(bf16[304,4096]{1,0:T(8,128)(2,1)} %param.6), slice={[16:208], [0:4096]} | slice | bytes 3145728 | tf_op jit(solution)/shard_map/slice | solution.py:35
  2.3 2.2 %collective-permute-start = (bf16[16,4095]{1,0:T(8,128)(2,1)S(1)}, bf16[16,4095]{1,0:T(8,128)(2,1)S(1)}, u32[]{:S(2)}, u32[]{:S(2)}) collective-permute-start(bf16[16,4095]{1,0:T(8,128)(2,1)S(1)} %concatenate.84), channel_id=1, source_target_pairs={{0,1},{1,2},{2,3},{3,4},{4,5},{5,6},{6,7},{7,8},{8,9},{9,10},{10,1... | collective-permute-start | bytes 393128 | tf_op jit(solution)/shard_map/ppermute | solution.py:14
  4.5 1.3 %fusion.57 = (bf16[16,4096]{1,0:T(8,128)(2,1)S(1)}, bf16[16,4096]{1,0:T(8,128)(2,1)S(1)}, bf16[16,4096]{1,0:T(8,128)(2,1)S(1)}, bf16[16,4096]{1,0:T(8,128)(2,1)S...) fusion(bf16[304,4096]{1,0:T(8,128)(2,1)} %param.6), kind=kLoop, calls=%fused_computation.151 | loop fusion | bytes 1835008 | tf_op jit(solution)/shard_map/slice | solution.py:53
  5.8 3.3 %collective-permute-start.6 = (bf16[16,4096]{1,0:T(8,128)(2,1)S(1)}, bf16[16,4096]{1,0:T(8,128)(2,1)S(1)}, u32[]{:S(2)}, u32[]{:S(2)}) collective-permute-start(bf16[16,4096]{1,0:T(8,128)(2,1)S(1)} %get-tuple-element.18), channel_id=1, source_target_pairs={{0,32},{1,33},{2,34},{3,35},{4,36},{5,37},{6,38},{7,39},{8,40},{9,... | collective-permute-start | bytes 393224 | tf_op jit(solution)/shard_map/ppermute | solution.py:14
  9.1 7.2 %collective-permute-start.4 = (bf16[16,4096]{1,0:T(8,128)(2,1)S(1)}, bf16[16,4096]{1,0:T(8,128)(2,1)S(1)}, u32[]{:S(2)}, u32[]{:S(2)}) collective-permute-start(bf16[16,4096]{1,0:T(8,128)(2,1)S(1)} %get-tuple-element.19), channel_id=1, source_target_pairs={{0,8},{1,9},{2,10},{3,11},{4,12},{5,13},{6,14},{7,15},{8,16},{9,17... | collective-permute-start | bytes 393224 | tf_op jit(solution)/shard_map/ppermute | solution.py:14
  16.3 1.5 %collective-permute-start.3 = (bf16[16,4096]{1,0:T(8,128)(2,1)S(1)}, bf16[16,4096]{1,0:T(8,128)(2,1)S(1)}, u32[]{:S(2)}, u32[]{:S(2)}) collective-permute-start(bf16[16,4096]{1,0:T(8,128)(2,1)S(1)} %get-tuple-element.20), channel_id=1, source_target_pairs={{0,4},{1,5},{2,6},{3,7},{4,8},{5,9},{6,10},{7,11},{8,12},{9,13},{1... | collective-permute-start | bytes 393224 | tf_op jit(solution)/shard_map/ppermute | solution.py:14
  17.7 1.0 collective-permute-start.2
  20.2 0.9 collective-permute-start.1
  22.7 13.3 %collective-permute-done.1 = bf16[16,4096]{1,0:T(8,128)(2,1)S(1)} collective-permute-done((bf16[16,4096]{1,0:T(8,128)(2,1)S(1)}, bf16[16,4096]{1,0:T(8,128)(2,1)S(1)}, u32[]{:S(2)}, u32[]{:S(2)}) %collective-permute-start.1) | collective-permute-done | bytes 131104 | tf_op jit(solution)/shard_map/ppermute | solution.py:14
  36.1 6.5 %collective-permute-done.5 = bf16[16,4096]{1,0:T(8,128)(2,1)S(1)} collective-permute-done((bf16[16,4096]{1,0:T(8,128)(2,1)S(1)}, bf16[16,4096]{1,0:T(8,128)(2,1)S(1)}, u32[]{:S(2)}, u32[]{:S(2)}) %collective-permute-start.5) | collective-permute-done | bytes 131104 | tf_op jit(solution)/shard_map/ppermute | solution.py:14
  42.7 1.4 %copy-done.1 = bf16[304,4096]{1,0:T(8,128)(2,1)} copy-done((bf16[304,4096]{1,0:T(8,128)(2,1)}, bf16[304,4096]{1,0:T(8,128)(2,1)S(1)}, u32[]{:S(2)}) %copy-start.1) | copy-done | bytes 2490392
  44.7 9.9 %fusion.19 = bf16[304,4096]{1,0:T(8,128)(2,1)} fusion(bf16[304,4096]{1,0:T(8,128)(2,1)} %copy-done.1, f32[304]{0:T(512)S(1)} %get-tuple-element.10, f32[608]{0:T(1024)S(1)} %get-tuple-element.6, f32[4096]{0:T(1024)S(1)} %add_rsqrt_fusion.1, f32[304]{0:T(512)S(1)} %get-tuple-element.29, bf16[2,304,608]{2,1,0:T(8,128)(2,1)S(1)} %copy-done.9, ...), kind=kOutput, calls=%fused_computation.29 | convolution fusion | flops 3063152640 | bytes 8273920 | tf_op jit(solution)/shard_map/dot_general | solution.py:25
  54.6 1.5 %slice.429 = bf16[192,4096]{1,0:T(8,128)(2,1)S(1)} slice(bf16[304,4096]{1,0:T(8,128)(2,1)} %fusion.19), slice={[16:208], [0:4096]} | slice | bytes 3145728 | tf_op jit(solution)/shard_map/slice | solution.py:35
  61.6 2.0 %fusion.56 = (bf16[16,4096]{1,0:T(8,128)(2,1)S(1)}, bf16[16,4096]{1,0:T(8,128)(2,1)S(1)}, bf16[16,4096]{1,0:T(8,128)(2,1)S(1)}, bf16[16,4096]{1,0:T(8,128)(2,1)S...) fusion(bf16[304,4096]{1,0:T(8,128)(2,1)} %fusion.19), kind=kLoop, calls=%fused_computation.150 | loop fusion | bytes 1835008 | tf_op jit(solution)/shard_map/slice | solution.py:53
  63.6 1.5 %concatenate.98 = bf16[16,4095]{1,0:T(8,128)(2,1)} concatenate(bf16[16,1]{1,0:T(8,128)(2,1)} %slice_bitcast_fusion.39, bf16[16,2]{1,0:T(8,128)(2,1)} %slice_bitcast_fusion.38, bf16[16,4]{1,0:T(8,128)(2,1)} %slice_bitcast_fusion.37, bf16[16,8]{1,0:T(8,128)(2,1)} %slice_bitcast_fusion.36, bf16[16,16]{1,0:T(8,128)(2,1)} %slice_bitcast_fusion.35, ...), dimensions={1} | concatenate | bytes 262080 | tf_op jit(solution)/shard_map/concatenate | solution.py:39
  65.8 3.1 %collective-permute-start.11 = (bf16[16,4096]{1,0:T(8,128)(2,1)S(1)}, bf16[16,4096]{1,0:T(8,128)(2,1)S(1)}, u32[]{:S(2)}, u32[]{:S(2)}) collective-permute-start(bf16[16,4096]{1,0:T(8,128)(2,1)S(1)} %get-tuple-element.13), channel_id=1, source_target_pairs={{0,8},{1,9},{2,10},{3,11},{4,12},{5,13},{6,14},{7,15},{8,16},{9,17... | collective-permute-start | bytes 393224 | tf_op jit(solution)/shard_map/ppermute | solution.py:14
  69.4 14.3 %collective-permute-done.7 = bf16[16,4095]{1,0:T(8,128)(2,1)S(1)} collective-permute-done((bf16[16,4095]{1,0:T(8,128)(2,1)}, bf16[16,4095]{1,0:T(8,128)(2,1)S(1)}, u32[]{:S(2)}, u32[]{:S(2)}) %collective-permute-start.7) | collective-permute-done | bytes 131072 | tf_op jit(solution)/shard_map/ppermute | solution.py:14
  83.6 0.8 maximum_dynamic-update-slice_fusion.23
  84.5 0.8 maximum_dynamic-update-slice_fusion.22
  87.0 0.8 maximum_dynamic-update-slice_fusion.19
  93.2 1.4 %collective-permute-done.8 = bf16[16,4096]{1,0:T(8,128)(2,1)S(1)} collective-permute-done((bf16[16,4096]{1,0:T(8,128)(2,1)}, bf16[16,4096]{1,0:T(8,128)(2,1)S(1)}, u32[]{:S(2)}, u32[]{:S(2)}) %collective-permute-start.8) | collective-permute-done | bytes 131104 | tf_op jit(solution)/shard_map/ppermute | solution.py:14
  95.2 7.6 %collective-permute-done.9 = bf16[16,4096]{1,0:T(8,128)(2,1)S(1)} collective-permute-done((bf16[16,4096]{1,0:T(8,128)(2,1)S(1)}, bf16[16,4096]{1,0:T(8,128)(2,1)S(1)}, u32[]{:S(2)}, u32[]{:S(2)}) %collective-permute-start.9) | collective-permute-done | bytes 131104 | tf_op jit(solution)/shard_map/ppermute | solution.py:14
  106.2 2.4 %fusion.25 = f32[4096]{0:T(1024)S(1)} fusion(bf16[304,4096]{1,0:T(8,128)(2,1)} %constant_dynamic-update-slice_fusion.6), kind=kLoop, calls=%fused_computation.35 | loop fusion | flops 3731456 | bytes 2506752 | tf_op jit(solution)/shard_map/reduce_sum | solution.py:19
  108.6 9.2 %fusion.18 = bf16[304,4096]{1,0:T(8,128)(2,1)} fusion(bf16[304,4096]{1,0:T(8,128)(2,1)S(1)} %copy-done, f32[304]{0:T(512)S(1)} %copy-done.7, f32[608]{0:T(1024)S(1)} %copy-done.4, f32[4096]{0:T(1024)S(1)} %add_rsqrt_fusion, f32[304]{0:T(512)S(1)} %copy-done.8, bf16[2,304,608]{2,1,0:T(8,128)(2,1)} %param.10, bf16[2,608,304]{1,2,0:T(8,128)(2,1)} %param.8), kind=kOutput, calls=%fused_computation.28 | convolution fusion | flops 3063152640 | bytes 8273920 | tf_op jit(solution)/shard_map/dot_general | solution.py:25
  (146 shorter events, 22.0 us)
Async XLA Ops:
  2.1 16.9 %copy-start.3 = (f32[2,608]{1,0:T(2,128)S(1)}, f32[2,608]{1,0:T(2,128)}, u32[]{:S(2)}) copy-start(f32[2,608]{1,0:T(2,128)} %param.9) | copy-start | bytes 14596
  2.1 17.5 %copy-start.5 = (f32[2,304]{1,0:T(2,128)S(1)}, f32[2,304]{1,0:T(2,128)}, u32[]{:S(2)}) copy-start(f32[2,304]{1,0:T(2,128)} %param.11) | copy-start | bytes 7300
  2.1 17.4 %copy-start.6 = (f32[2,304]{1,0:T(2,128)S(1)}, f32[2,304]{1,0:T(2,128)}, u32[]{:S(2)}) copy-start(f32[2,304]{1,0:T(2,128)} %param.7) | copy-start | bytes 7300
  2.3 17.9 %collective-permute-start = (bf16[16,4095]{1,0:T(8,128)(2,1)S(1)}, bf16[16,4095]{1,0:T(8,128)(2,1)S(1)}, u32[]{:S(2)}, u32[]{:S(2)}) collective-permute-start(bf16[16,4095]{1,0:T(8,128)(2,1)S(1)} %concatenate.84), channel_id=1, source_target_pairs={{0,1},{1,2},{2,3},{3,4},{4,5},{5,6},{6,7},{7,8},{8,9},{9,10},{10,1... | collective-permute-start | bytes 393128 | tf_op jit(solution)/shard_map/ppermute | solution.py:14
  5.8 36.9 %collective-permute-start.6 = (bf16[16,4096]{1,0:T(8,128)(2,1)S(1)}, bf16[16,4096]{1,0:T(8,128)(2,1)S(1)}, u32[]{:S(2)}, u32[]{:S(2)}) collective-permute-start(bf16[16,4096]{1,0:T(8,128)(2,1)S(1)} %get-tuple-element.18), channel_id=1, source_target_pairs={{0,32},{1,33},{2,34},{3,35},{4,36},{5,37},{6,38},{7,39},{8,40},{9,... | collective-permute-start | bytes 393224 | tf_op jit(solution)/shard_map/ppermute | solution.py:14
  9.1 27.1 %collective-permute-start.4 = (bf16[16,4096]{1,0:T(8,128)(2,1)S(1)}, bf16[16,4096]{1,0:T(8,128)(2,1)S(1)}, u32[]{:S(2)}, u32[]{:S(2)}) collective-permute-start(bf16[16,4096]{1,0:T(8,128)(2,1)S(1)} %get-tuple-element.19), channel_id=1, source_target_pairs={{0,8},{1,9},{2,10},{3,11},{4,12},{5,13},{6,14},{7,15},{8,16},{9,17... | collective-permute-start | bytes 393224 | tf_op jit(solution)/shard_map/ppermute | solution.py:14
  16.3 19.8 %collective-permute-start.3 = (bf16[16,4096]{1,0:T(8,128)(2,1)S(1)}, bf16[16,4096]{1,0:T(8,128)(2,1)S(1)}, u32[]{:S(2)}, u32[]{:S(2)}) collective-permute-start(bf16[16,4096]{1,0:T(8,128)(2,1)S(1)} %get-tuple-element.20), channel_id=1, source_target_pairs={{0,4},{1,5},{2,6},{3,7},{4,8},{5,9},{6,10},{7,11},{8,12},{9,13},{1... | collective-permute-start | bytes 393224 | tf_op jit(solution)/shard_map/ppermute | solution.py:14
  17.7 18.3 %collective-permute-start.2 = (bf16[16,4096]{1,0:T(8,128)(2,1)S(1)}, bf16[16,4096]{1,0:T(8,128)(2,1)S(1)}, u32[]{:S(2)}, u32[]{:S(2)}) collective-permute-start(bf16[16,4096]{1,0:T(8,128)(2,1)S(1)} %get-tuple-element.21), channel_id=1, source_target_pairs={{0,2},{1,3},{2,4},{3,5},{4,6},{5,7},{6,8},{7,9},{8,10},{9,11},{10,... | collective-permute-start | bytes 393224 | tf_op jit(solution)/shard_map/ppermute | solution.py:14
  20.2 15.9 %collective-permute-start.1 = (bf16[16,4096]{1,0:T(8,128)(2,1)S(1)}, bf16[16,4096]{1,0:T(8,128)(2,1)S(1)}, u32[]{:S(2)}, u32[]{:S(2)}) collective-permute-start(bf16[16,4096]{1,0:T(8,128)(2,1)S(1)} %get-tuple-element.22), channel_id=1, source_target_pairs={{0,1},{1,2},{2,3},{3,4},{4,5},{5,6},{6,7},{7,8},{8,9},{9,10},{10,1... | collective-permute-start | bytes 393224 | tf_op jit(solution)/shard_map/ppermute | solution.py:14
  22.5 22.2 %copy-start.9 = (bf16[2,304,608]{2,1,0:T(8,128)(2,1)S(1)}, bf16[2,304,608]{2,1,0:T(8,128)(2,1)}, u32[]{:S(2)}) copy-start(bf16[2,304,608]{2,1,0:T(8,128)(2,1)} %param.10) | copy-start | bytes 2217988
  22.5 22.2 %copy-start.10 = (bf16[2,608,304]{1,2,0:T(8,128)(2,1)S(1)}, bf16[2,608,304]{1,2,0:T(8,128)(2,1)}, u32[]{:S(2)}) copy-start(bf16[2,608,304]{1,2,0:T(8,128)(2,1)} %param.8) | copy-start | bytes 2217988
  36.0 6.6 %collective-permute-start.5 = (bf16[16,4096]{1,0:T(8,128)(2,1)S(1)}, bf16[16,4096]{1,0:T(8,128)(2,1)S(1)}, u32[]{:S(2)}, u32[]{:S(2)}) collective-permute-start(bf16[16,4096]{1,0:T(8,128)(2,1)S(1)} %get-tuple-element.24), channel_id=1, source_target_pairs={{0,16},{1,17},{2,18},{3,19},{4,20},{5,21},{6,22},{7,23},{8,24},{9,... | collective-permute-start | bytes 393224 | tf_op jit(solution)/shard_map/ppermute | solution.py:14
  65.2 29.4 %copy-start.2 = (bf16[16,4096]{1,0:T(8,128)(2,1)S(1)}, bf16[16,4096]{1,0:T(8,128)(2,1)}, u32[]{:S(2)}) copy-start(bf16[16,4096]{1,0:T(8,128)(2,1)} %get-tuple-element.15) | copy-start | bytes 393220
  65.2 18.5 %collective-permute-start.7 = (bf16[16,4095]{1,0:T(8,128)(2,1)}, bf16[16,4095]{1,0:T(8,128)(2,1)S(1)}, u32[]{:S(2)}, u32[]{:S(2)}) collective-permute-start(bf16[16,4095]{1,0:T(8,128)(2,1)} %concatenate.98), channel_id=1, source_target_pairs={{0,1},{1,2},{2,3},{3,4},{4,5},{5,6},{6,7},{7,8},{8,9},{9,10},{10,1... | collective-permute-start | bytes 393128 | tf_op jit(solution)/shard_map/ppermute | solution.py:14
  65.2 40.3 %collective-permute-start.13 = (bf16[16,4096]{1,0:T(8,128)(2,1)S(1)}, bf16[16,4096]{1,0:T(8,128)(2,1)S(1)}, u32[]{:S(2)}, u32[]{:S(2)}) collective-permute-start(bf16[16,4096]{1,0:T(8,128)(2,1)S(1)} %get-tuple-element.11), channel_id=1, source_target_pairs={{0,32},{1,33},{2,34},{3,35},{4,36},{5,37},{6,38},{7,39},{8,40},{9,... | collective-permute-start | bytes 393224 | tf_op jit(solution)/shard_map/ppermute | solution.py:14
  65.5 39.4 %collective-permute-start.12 = (bf16[16,4096]{1,0:T(8,128)(2,1)S(1)}, bf16[16,4096]{1,0:T(8,128)(2,1)S(1)}, u32[]{:S(2)}, u32[]{:S(2)}) collective-permute-start(bf16[16,4096]{1,0:T(8,128)(2,1)S(1)} %get-tuple-element.12), channel_id=1, source_target_pairs={{0,16},{1,17},{2,18},{3,19},{4,20},{5,21},{6,22},{7,23},{8,24},{9,... | collective-permute-start | bytes 393224 | tf_op jit(solution)/shard_map/ppermute | solution.py:14
  65.8 38.3 %collective-permute-start.11 = (bf16[16,4096]{1,0:T(8,128)(2,1)S(1)}, bf16[16,4096]{1,0:T(8,128)(2,1)S(1)}, u32[]{:S(2)}, u32[]{:S(2)}) collective-permute-start(bf16[16,4096]{1,0:T(8,128)(2,1)S(1)} %get-tuple-element.13), channel_id=1, source_target_pairs={{0,8},{1,9},{2,10},{3,11},{4,12},{5,13},{6,14},{7,15},{8,16},{9,17... | collective-permute-start | bytes 393224 | tf_op jit(solution)/shard_map/ppermute | solution.py:14
  68.9 34.5 %collective-permute-start.10 = (bf16[16,4096]{1,0:T(8,128)(2,1)S(1)}, bf16[16,4096]{1,0:T(8,128)(2,1)S(1)}, u32[]{:S(2)}, u32[]{:S(2)}) collective-permute-start(bf16[16,4096]{1,0:T(8,128)(2,1)S(1)} %get-tuple-element.14), channel_id=1, source_target_pairs={{0,4},{1,5},{2,6},{3,7},{4,8},{5,9},{6,10},{7,11},{8,12},{9,13},{1... | collective-permute-start | bytes 393224 | tf_op jit(solution)/shard_map/ppermute | solution.py:14
  83.6 10.9 %collective-permute-start.8 = (bf16[16,4096]{1,0:T(8,128)(2,1)}, bf16[16,4096]{1,0:T(8,128)(2,1)S(1)}, u32[]{:S(2)}, u32[]{:S(2)}) collective-permute-start(bf16[16,4096]{1,0:T(8,128)(2,1)} %get-tuple-element.16), channel_id=1, source_target_pairs={{0,1},{1,2},{2,3},{3,4},{4,5},{5,6},{6,7},{7,8},{8,9},{9,10},{10,1... | collective-permute-start | bytes 393224 | tf_op jit(solution)/shard_map/ppermute | solution.py:14
  91.0 17.6 %copy-start.4 = (f32[608]{0:T(1024)S(1)}, f32[608]{0:T(1024)}, u32[]{:S(2)}) copy-start(f32[608]{0:T(1024)} %get-tuple-element.5) | copy-start | bytes 7300
  91.0 17.6 %copy-start.7 = (f32[304]{0:T(512)S(1)}, f32[304]{0:T(512)}, u32[]{:S(2)}) copy-start(f32[304]{0:T(512)} %get-tuple-element.9) | copy-start | bytes 3652
  91.0 17.6 %copy-start.8 = (f32[304]{0:T(512)S(1)}, f32[304]{0:T(512)}, u32[]{:S(2)}) copy-start(f32[304]{0:T(512)} %get-tuple-element.30) | copy-start | bytes 3652
  94.5 8.3 %collective-permute-start.9 = (bf16[16,4096]{1,0:T(8,128)(2,1)S(1)}, bf16[16,4096]{1,0:T(8,128)(2,1)S(1)}, u32[]{:S(2)}, u32[]{:S(2)}) collective-permute-start(bf16[16,4096]{1,0:T(8,128)(2,1)S(1)} %copy-done.2), channel_id=1, source_target_pairs={{0,2},{1,3},{2,4},{3,5},{4,6},{5,7},{6,8},{7,9},{8,10},{9,11},{10,... | collective-permute-start | bytes 393224 | tf_op jit(solution)/shard_map/ppermute | solution.py:14
  106.2 2.5 %copy-start = (bf16[304,4096]{1,0:T(8,128)(2,1)S(1)}, bf16[304,4096]{1,0:T(8,128)(2,1)}, u32[]{:S(2)}) copy-start(bf16[304,4096]{1,0:T(8,128)(2,1)} %constant_dynamic-update-slice_fusion.6) | copy-start | bytes 7471108
  (1 other events, 1.5 us)
where the time goes:
time: 118 us
  waiting for transfers between devices  43.1 us (37%)
  local copies, waits for them, and re-layouts  22.5 us (19%)
  starting transfers between devices  20.2 us (17%)
  matrix products  19.1 us (16%)
  other arithmetic  12.3 us (10%)
    ppermute x14, waiting for transfers between devices, shifted(): return lax.ppermute(value, axis, pairs)  43.1 us
    ppermute x14, starting transfers between devices, shifted(): return lax.ppermute(value, axis, pairs)  20.2 us
    dot_general x2, matrix products, mix_rows(): jnp.dot(out_weight, active, preferred_element_type=jnp.float32)  19.1 us
    unnamed x24, other arithmetic  9.43 us
    squeeze x22, local copies, waits for them, and re-layouts, rotate(): short_slab[slot, :, local_rows - 2 ** slot:]  5.77 us
    unnamed x32, local copies, waits for them, and re-layouts  4.89 us
    slice x2, local copies, waits for them, and re-layouts, rotate(): one_track = current[track_no * TRACK_CH:(track_no + 1) * TRACK_CH]  3.31 us
    slice x2, local copies, waits for them, and re-layouts, rotate(): current[TRACK_CH:(1 + short_count) * TRACK_CH]  3.02 us
  transfers between devices with their start and end apart: 14, of which 5 were waited for; matrix products, arithmetic and copies ran while one was open for 15% of the time, Pallas kernels for 0%

commit v1 on v0

v1 whole, which is shorter than its diff:
```python
import functools

import jax
import jax.numpy as jnp
from jax import lax
from jax.experimental import pallas as pl
from jax.experimental.pallas import tpu as pltpu
from jax.sharding import PartitionSpec as P

TRACK_CH = 16
TRACKS = 19
BLOCKS = 2
LANES = 128
TILE = 512
GELU_A = 0.7978845608028654
GELU_B = 0.7978845608028654 * 0.044715


def shifted(value, axis, steps):
    count = lax.axis_size(axis)
    pairs = [(source, (source + steps) % count) for source in range(count)]
    return lax.ppermute(value, axis, pairs)


def short_tracks(local_rows):
    count = 0
    while count + 1 < TRACKS and 2**count < local_rows:
        count = count + 1
    return count


def pack_halo(track, store, local_rows, short_count):
    lane = lax.broadcasted_iota(jnp.int32, (TRACK_CH, LANES), 1)
    packed = jnp.zeros((TRACK_CH, LANES), jnp.float32)
    for slot in range(short_count):
        offset = 2**slot
        if offset < LANES:
            last = track(1 + slot, local_rows - LANES, local_rows).astype(jnp.float32)
            moved = pltpu.roll(last, (2 * offset - 1) % LANES, 1)
            inside = (lane >= offset - 1) & (lane < 2 * offset - 1)
            packed = jnp.where(inside, moved, packed)
        else:
            store(offset, 2 * offset, track(1 + slot, local_rows - offset, local_rows))
    store(0, LANES, packed.astype(jnp.bfloat16))


def rotated_piece(track, halo, slot, begin, end):
    offset = 2**slot
    if offset < LANES:
        if begin == 0:
            packed = halo(0, LANES).astype(jnp.float32)
            before = pltpu.roll(packed, (LANES + 1 - 2 * offset) % LANES, 1)
            window = jnp.concatenate([before, track(1 + slot, 0, end).astype(jnp.float32)], 1)
        else:
            window = track(1 + slot, begin - LANES, end).astype(jnp.float32)
        return pltpu.roll(window, offset, 1)[:, LANES:]
    parts = []
    if begin < offset:
        parts.append(halo(offset + begin, offset + min(end, offset)))
    if end > offset:
        parts.append(track(1 + slot, max(begin, offset) - offset, end - offset))
    joined = parts[0] if len(parts) == 1 else jnp.concatenate(parts, 1)
    return joined.astype(jnp.float32)


def mix(rotated, gain, w_in, b_in, w_out, b_out):
    mean_square = jnp.mean(rotated * rotated, axis=0, keepdims=True)
    normed = (rotated * gain * lax.rsqrt(mean_square + 1e-06)).astype(jnp.bfloat16)
    pre = jnp.dot(w_in, normed, preferred_element_type=jnp.float32) + b_in
    inner = pre * (GELU_A + GELU_B * (pre * pre))
    half = 0.5 * pre
    active = (half + half * jnp.tanh(inner)).astype(jnp.bfloat16)
    out = jnp.dot(w_out, active, preferred_element_type=jnp.float32)
    return (rotated + out + b_out).astype(jnp.bfloat16)


def halo_kernel(local_rows, short_count, tail, out):
    base = local_rows - tail.shape[1]

    def track(t, begin, end):
        return tail[t * TRACK_CH : (t + 1) * TRACK_CH, begin - base : end - base]

    def store(begin, end, value):
        out[:, begin:end] = value

    pack_halo(track, store, local_rows, short_count)


def block_kernel(short_count, last, *refs):
    far_count = TRACKS - 1 - short_count
    near, halo_in = refs[0], refs[1]
    far = refs[2 : 2 + far_count]
    gain, w_in, b_in, w_out, b_out = refs[2 + far_count : 7 + far_count]
    outs = refs[7 + far_count :]
    local_rows = halo_in.shape[1]
    near_rows = (1 + short_count) * TRACK_CH

    def track(t, begin, end):
        return near[t * TRACK_CH : (t + 1) * TRACK_CH, begin:end]

    def halo(begin, end):
        return halo_in[:, begin:end]

    for begin in range(0, local_rows, TILE):
        end = begin + TILE
        pieces = [track(0, begin, end).astype(jnp.float32)]
        for slot in range(short_count):
            pieces.append(rotated_piece(track, halo, slot, begin, end))
        for ref in far:
            pieces.append(ref[:, begin:end].astype(jnp.float32))
        rotated = jnp.concatenate(pieces, 0)
        mixed = mix(rotated, gain[...], w_in[...], b_in[...], w_out[...], b_out[...])
        if last:
            outs[0][:, begin:end] = mixed
        else:
            outs[0][:, begin:end] = mixed[:near_rows]
            for at in range(far_count):
                top = near_rows + at * TRACK_CH
                outs[2 + at][:, begin:end] = mixed[top : top + TRACK_CH]
    if not last:

        def made(t, begin, end):
            return outs[0][t * TRACK_CH : (t + 1) * TRACK_CH, begin:end]

        def store(begin, end, value):
            outs[1][:, begin:end] = value

        pack_halo(made, store, local_rows, short_count)


VMEM = pl.BlockSpec(memory_space=pltpu.VMEM)


def shards(tokens, norm_gain, in_weight, in_bias, out_weight, out_bias):
    width, local_rows = tokens.shape
    short_count = short_tracks(local_rows)
    far_count = TRACKS - 1 - short_count
    near_rows = (1 + short_count) * TRACK_CH
    one = jax.ShapeDtypeStruct((TRACK_CH, local_rows), jnp.bfloat16)
    near = tokens[:near_rows]
    bundle = pl.pallas_call(
        functools.partial(halo_kernel, local_rows, short_count),
        out_shape=one,
        grid=(1,),
        in_specs=[pl.BlockSpec((near_rows, local_rows // 2), lambda i: (0, 1))],
        out_specs=pl.BlockSpec((TRACK_CH, local_rows), lambda i: (0, 0)),
        name="halo",
    )(tokens)
    far = [tokens[near_rows + at * TRACK_CH : near_rows + (at + 1) * TRACK_CH] for at in range(far_count)]
    for block_no in range(BLOCKS):
        last = block_no == BLOCKS - 1
        halo = shifted(bundle, "seq", 1)
        far = [
            shifted(value, "seq", 2 ** (short_count + at) // local_rows)
            for at, value in enumerate(far)
        ]
        if last:
            out_shape = [jax.ShapeDtypeStruct((width, local_rows), jnp.bfloat16)]
        else:
            out_shape = [jax.ShapeDtypeStruct((near_rows, local_rows), jnp.bfloat16)] + [one] * (1 + far_count)
        outs = pl.pallas_call(
            functools.partial(block_kernel, short_count, last),
            out_shape=out_shape,
            in_specs=[VMEM] * (7 + far_count),
            out_specs=[VMEM] * len(out_shape),
            compiler_params=pltpu.CompilerParams(vmem_limit_bytes=40 << 20),
            name="block",
        )(
            near,
            halo,
            *far,
            norm_gain[block_no][:, None],
            in_weight[block_no],
            in_bias[block_no][:, None],
            out_weight[block_no],
            out_bias[block_no][:, None],
        )
        if last:
            return outs[0]
        near, bundle, far = outs[0], outs[1], outs[2:]


def solution(mesh):
    return jax.shard_map(
        shards,
        mesh=mesh,
        in_specs=(P("batch", "seq"), P(), P(), P(), P(), P()),
        out_specs=P("batch", "seq"),
        check_vma=False,
    )
```

time: 118 us -> 82.1 us (0.70)
  Pallas kernels: 0 us -> 20.6 us
  matrix products: 19.1 us -> 0 us
  waiting for transfers between devices: 43.1 us -> 26.9 us
  other arithmetic: 12.3 us -> 0 us
  local copies, waits for them, and re-layouts: 22.5 us -> 10.8 us
  starting transfers between devices: 20.2 us -> 23.4 us
    pallas_call x0 -> x3, Pallas kernels: none -> 20.6 us  [the longest x2 18.7 us: shards(): pl.pallas_call(functools.partial(block_kernel, short_count, last), out_sh...]
    dot_general x2 -> x0, matrix products: 19.1 us -> none  [mix_rows(): jnp.dot(out_weight, active, preferred_element_type=jnp.float32)]
    ppermute x14, waiting for transfers between devices: 43.1 us -> 26.9 us  [shifted(): return lax.ppermute(value, axis, pairs)]
    unnamed x24 -> x0, other arithmetic: 9.43 us -> none
    squeeze x46 -> x1, local copies, waits for them, and re-layouts: 6.01 us -> 1.18 us  [shards(): out_weight[block_no]]
    slice x30 -> x3, local copies, waits for them, and re-layouts: 9.23 us -> 4.52 us  [the longest x1 2.14 us: shards(): tokens[near_rows + at * TRACK_CH:near_rows + (at + 1) * TRACK_CH]]
    ppermute x14, starting transfers between devices: 20.2 us -> 23.4 us  [shifted(): return lax.ppermute(value, axis, pairs)]
    reduce_sum x2 -> x0, other arithmetic: 2.9 us -> none  [mix_rows(): mean_square = jnp.mean(as_float * as_float, axis=0, keepdims=True)]
  transfers between devices with their start and end apart: 14 -> 14, of which waited for: 5 -> 6; matrix products, arithmetic and copies ran while one was open for 15% -> 7% of each run, Pallas kernels for 0% -> 2%
where the time goes in v1:
time: 82.1 us; the launch traced here: 81.9 us
  waiting for transfers between devices  26.9 us (33%)
  starting transfers between devices  23.4 us (29%)
  Pallas kernels  20.6 us (25%)
  local copies, waits for them, and re-layouts  10.8 us (13%)
    ppermute x14, waiting for transfers between devices, shifted(): return lax.ppermute(value, axis, pairs)  26.9 us
    ppermute x14, starting transfers between devices, shifted(): return lax.ppermute(value, axis, pairs)  23.4 us
    pallas_call x2, Pallas kernels, shards(): pl.pallas_call(functools.partial(block_kernel, short_count, last), out_sh...  18.7 us
    unnamed x14, local copies, waits for them, and re-layouts  4.16 us
    slice x1, local copies, waits for them, and re-layouts, shards(): tokens[near_rows + at * TRACK_CH:near_rows + (at + 1) * TRACK_CH]  2.14 us
    pallas_call x1, Pallas kernels, shards(): pl.pallas_call(functools.partial(halo_kernel, local_rows, short_count), o...  1.9 us
  transfers between devices with their start and end apart: 14, of which 6 were waited for; matrix products, arithmetic and copies ran while one was open for 7% of the time, Pallas kernels for 2%

profile of v1, /device:TPU:2, one launch (start us, length us, event | category | flops | bytes accessed | tf_op | source)
XLA Modules:
  0.0 81.9 jit_solution(11531610398995579578)
XLA Ops:
  0.0 2.1 %fusion = (bf16[16,4096]{1,0:T(8,128)(2,1)}, bf16[16,4096]{1,0:T(8,128)(2,1)}, bf16[16,4096]{1,0:T(8,128)(2,1)}, bf16[16,4096]{1,0:T(8,128)(2,1)}, bf16[16,4096]{1,0:T(8,128)(2,1)}, /*index=5*/bf16[16,4096]{1,0:T(8,128)(2,1)}) fusion(bf16[304,4096]{1,0:T(8,128)(2,1)} %tail.1), kind=kLoop, calls=%fused_computation.8 | loop fusion | bytes 1572864 | tf_op jit(solution)/shard_map/slice | solution.py:149
  2.1 2.1 %collective-permute-start.1 = (bf16[16,4096]{1,0:T(8,128)(2,1)}, bf16[16,4096]{1,0:T(8,128)(2,1)S(1)}, u32[]{:S(2)}, u32[]{:S(2)}) collective-permute-start(bf16[16,4096]{1,0:T(8,128)(2,1)} %get-tuple-element.25), channel_id=1, source_target_pairs={{0,1},{1,2},{2,3},{3,4},{4,5},{5,6},{6,7},{7,8},{8,9},{9,10},{10,1... | collective-permute-start | bytes 393224 | tf_op jit(solution)/shard_map/ppermute | solution.py:22
  4.3 1.9 %collective-permute-start.2 = (bf16[16,4096]{1,0:T(8,128)(2,1)}, bf16[16,4096]{1,0:T(8,128)(2,1)S(1)}, u32[]{:S(2)}, u32[]{:S(2)}) collective-permute-start(bf16[16,4096]{1,0:T(8,128)(2,1)} %get-tuple-element.24), channel_id=1, source_target_pairs={{0,2},{1,3},{2,4},{3,5},{4,6},{5,7},{6,8},{7,9},{8,10},{9,11},{10,... | collective-permute-start | bytes 393224 | tf_op jit(solution)/shard_map/ppermute | solution.py:22
  6.2 3.3 %collective-permute-start.3 = (bf16[16,4096]{1,0:T(8,128)(2,1)}, bf16[16,4096]{1,0:T(8,128)(2,1)}, u32[]{:S(2)}, u32[]{:S(2)}) collective-permute-start(bf16[16,4096]{1,0:T(8,128)(2,1)} %get-tuple-element.23), channel_id=1, source_target_pairs={{0,4},{1,5},{2,6},{3,7},{4,8},{5,9},{6,10},{7,11},{8,12},{9,13},{1... | collective-permute-start | bytes 393224 | tf_op jit(solution)/shard_map/ppermute | solution.py:22
  9.5 4.5 %collective-permute-start.4 = (bf16[16,4096]{1,0:T(8,128)(2,1)}, bf16[16,4096]{1,0:T(8,128)(2,1)}, u32[]{:S(2)}, u32[]{:S(2)}) collective-permute-start(bf16[16,4096]{1,0:T(8,128)(2,1)} %get-tuple-element.22), channel_id=1, source_target_pairs={{0,8},{1,9},{2,10},{3,11},{4,12},{5,13},{6,14},{7,15},{8,16},{9,17... | collective-permute-start | bytes 393224 | tf_op jit(solution)/shard_map/ppermute | solution.py:22
  13.9 1.6 %collective-permute-start.5 = (bf16[16,4096]{1,0:T(8,128)(2,1)}, bf16[16,4096]{1,0:T(8,128)(2,1)}, u32[]{:S(2)}, u32[]{:S(2)}) collective-permute-start(bf16[16,4096]{1,0:T(8,128)(2,1)} %get-tuple-element.26), channel_id=1, source_target_pairs={{0,16},{1,17},{2,18},{3,19},{4,20},{5,21},{6,22},{7,23},{8,24},{9,... | collective-permute-start | bytes 393224 | tf_op jit(solution)/shard_map/ppermute | solution.py:22
  15.5 1.6 %slice.51.refs_0_ = bf16[208,4096]{1,0:T(8,128)(2,1)S(1)} slice(bf16[304,4096]{1,0:T(8,128)(2,1)} %tail.1), slice={[0:208], [0:4096]} | slice | bytes 3407872 | tf_op jit(solution)/shard_map/slice | solution.py:140
  17.1 1.9 %halo.1 = bf16[16,4096]{1,0:T(8,128)(2,1)} custom-call(bf16[304,4096]{1,0:T(8,128)(2,1)} %tail.1), custom_call_target="tpu_custom_call" | custom-call | tf_op jit(solution)/shard_map/halo/pallas_call | solution.py:141
  20.6 3.0 %collective-permute-start.6 = (bf16[16,4096]{1,0:T(8,128)(2,1)}, bf16[16,4096]{1,0:T(8,128)(2,1)S(1)}, u32[]{:S(2)}, u32[]{:S(2)}) collective-permute-start(bf16[16,4096]{1,0:T(8,128)(2,1)} %get-tuple-element.21), channel_id=1, source_target_pairs={{0,32},{1,33},{2,34},{3,35},{4,36},{5,37},{6,38},{7,39},{8,40},{9,... | collective-permute-start | bytes 393224 | tf_op jit(solution)/shard_map/ppermute | solution.py:22
  24.5 1.2 %slice_bitcast_fusion = (bf16[304,608]{1,0:T(8,128)(2,1)S(1)}, bf16[304,608]{1,0:T(8,128)(2,1)S(1)}) fusion(bf16[2,304,608]{2,1,0:T(8,128)(2,1)} %param.10), kind=kLoop, calls=%fused_computation | loop fusion | bytes 1478656 | tf_op jit(solution)/shard_map/squeeze | solution.py:175
  25.7 1.5 %collective-permute-done.3.refs_4_ = bf16[16,4096]{1,0:T(8,128)(2,1)} collective-permute-done((bf16[16,4096]{1,0:T(8,128)(2,1)}, bf16[16,4096]{1,0:T(8,128)(2,1)}, u32[]{:S(2)}, u32[]{:S(2)}) %collective-permute-start.3) | collective-permute-done | bytes 131104 | tf_op jit(solution)/shard_map/ppermute | solution.py:22
  27.1 2.8 %collective-permute-done.6.refs_7_ = bf16[16,4096]{1,0:T(8,128)(2,1)S(1)} collective-permute-done((bf16[16,4096]{1,0:T(8,128)(2,1)}, bf16[16,4096]{1,0:T(8,128)(2,1)S(1)}, u32[]{:S(2)}, u32[]{:S(2)}) %collective-permute-start.6) | collective-permute-done | bytes 131104 | tf_op jit(solution)/shard_map/ppermute | solution.py:22
  29.9 4.6 %collective-permute-done.refs_1_ = bf16[16,4096]{1,0:T(8,128)(2,1)S(1)} collective-permute-done((bf16[16,4096]{1,0:T(8,128)(2,1)}, bf16[16,4096]{1,0:T(8,128)(2,1)S(1)}, u32[]{:S(2)}, u32[]{:S(2)}) %collective-permute-start) | collective-permute-done | bytes 131104 | tf_op jit(solution)/shard_map/ppermute | solution.py:22
  34.5 9.6 %block.2 = (bf16[208,4096]{1,0:T(8,128)(2,1)S(1)}, bf16[16,4096]{1,0:T(8,128)(2,1)}, bf16[16,4096]{1,0:T(8,128)(2,1)}, bf16[16,4096]{1,0:T(8,128)(2,1)}, bf16[16...) custom-call(bf16[208,4096]{1,0:T(8,128)(2,1)S(1)} %slice.51.refs_0_, ...), custom_call_target="tpu_custom_call" | custom-call | tf_op jit(solution)/shard_map/block/pallas_call | solution.py:161
  44.1 1.2 %copy-done = bf16[208,4096]{1,0:T(8,128)(2,1)} copy-done((bf16[208,4096]{1,0:T(8,128)(2,1)}, bf16[208,4096]{1,0:T(8,128)(2,1)S(1)}, u32[]{:S(2)}) %copy-start) | copy-done | bytes 1703960
  45.3 1.5 %collective-permute-start.11 = (bf16[16,4096]{1,0:T(8,128)(2,1)S(1)}, bf16[16,4096]{1,0:T(8,128)(2,1)S(1)}, u32[]{:S(2)}, u32[]{:S(2)}) collective-permute-start(bf16[16,4096]{1,0:T(8,128)(2,1)S(1)} %get-tuple-element.18), channel_id=1, source_target_pairs={{0,8},{1,9},{2,10},{3,11},{4,12},{5,13},{6,14},{7,15},{8,16},{9,17... | collective-permute-start | bytes 393224 | tf_op jit(solution)/shard_map/ppermute | solution.py:22
  46.8 1.2 %collective-permute-start.12 = (bf16[16,4096]{1,0:T(8,128)(2,1)}, bf16[16,4096]{1,0:T(8,128)(2,1)S(1)}, u32[]{:S(2)}, u32[]{:S(2)}) collective-permute-start(bf16[16,4096]{1,0:T(8,128)(2,1)} %get-tuple-element.19), channel_id=1, source_target_pairs={{0,16},{1,17},{2,18},{3,19},{4,20},{5,21},{6,22},{7,23},{8,24},{9,... | collective-permute-start | bytes 393224 | tf_op jit(solution)/shard_map/ppermute | solution.py:22
  48.0 2.9 %collective-permute-start.13 = (bf16[16,4096]{1,0:T(8,128)(2,1)}, bf16[16,4096]{1,0:T(8,128)(2,1)S(1)}, u32[]{:S(2)}, u32[]{:S(2)}) collective-permute-start(bf16[16,4096]{1,0:T(8,128)(2,1)} %get-tuple-element.20), channel_id=1, source_target_pairs={{0,32},{1,33},{2,34},{3,35},{4,36},{5,37},{6,38},{7,39},{8,40},{9,... | collective-permute-start | bytes 393224 | tf_op jit(solution)/shard_map/ppermute | solution.py:22
  51.5 8.8 %collective-permute-done.10.refs_4_ = bf16[16,4096]{1,0:T(8,128)(2,1)S(1)} collective-permute-done((bf16[16,4096]{1,0:T(8,128)(2,1)S(1)}, bf16[16,4096]{1,0:T(8,128)(2,1)S(1)}, u32[]{:S(2)}, u32[]{:S(2)}) %collective-permute-start.10) | collective-permute-done | bytes 131104 | tf_op jit(solution)/shard_map/ppermute | solution.py:22
  60.4 1.2 %copy.18 = bf16[1,608,304]{2,1,0:T(8,128)(2,1)S(1)} copy(bf16[1,608,304]{1,2,0:T(8,128)(2,1)} %get-tuple-element.29) | data formatting | bytes 739328
  62.1 6.8 %collective-permute-done.13.refs_7_ = bf16[16,4096]{1,0:T(8,128)(2,1)S(1)} collective-permute-done((bf16[16,4096]{1,0:T(8,128)(2,1)}, bf16[16,4096]{1,0:T(8,128)(2,1)S(1)}, u32[]{:S(2)}, u32[]{:S(2)}) %collective-permute-start.13) | collective-permute-done | bytes 131104 | tf_op jit(solution)/shard_map/ppermute | solution.py:22
  68.9 2.3 %collective-permute-done.8.refs_2_ = bf16[16,4096]{1,0:T(8,128)(2,1)S(1)} collective-permute-done((bf16[16,4096]{1,0:T(8,128)(2,1)}, bf16[16,4096]{1,0:T(8,128)(2,1)S(1)}, u32[]{:S(2)}, u32[]{:S(2)}) %collective-permute-start.8) | collective-permute-done | bytes 131104 | tf_op jit(solution)/shard_map/ppermute | solution.py:22
  71.3 1.5 %copy-done.1 = bf16[208,4096]{1,0:T(8,128)(2,1)S(1)} copy-done((bf16[208,4096]{1,0:T(8,128)(2,1)S(1)}, bf16[208,4096]{1,0:T(8,128)(2,1)}, u32[]{:S(2)}) %copy-start.1) | copy-done | bytes 1703960
  72.7 9.1 %block.3 = bf16[304,4096]{1,0:T(8,128)(2,1)} custom-call(bf16[208,4096]{1,0:T(8,128)(2,1)S(1)} %copy-done.1, bf16[16,4096]{1,0:T(8,128)(2,1)S(1)} %collective-permute-done.7.refs_1_, bf16[16,4096]{1,0:T(8,128)(2,1)S(1)} %collective-permute-done.8.refs_2_, bf16[16,4096]{1,0:T(8,128)(2,1)S(1)} %collective-permute-done.9.refs_3_, ...), custom_call_target="tpu_custom_call" | custom-call | tf_op jit(solution)/shard_map/block/pallas_call | solution.py:161
  (34 shorter events, 3.5 us)
Async XLA Ops:
  2.1 18.5 %collective-permute-start.1 = (bf16[16,4096]{1,0:T(8,128)(2,1)}, bf16[16,4096]{1,0:T(8,128)(2,1)S(1)}, u32[]{:S(2)}, u32[]{:S(2)}) collective-permute-start(bf16[16,4096]{1,0:T(8,128)(2,1)} %get-tuple-element.25), channel_id=1, source_target_pairs={{0,1},{1,2},{2,3},{3,4},{4,5},{5,6},{6,7},{7,8},{8,9},{9,10},{10,1... | collective-permute-start | bytes 393224 | tf_op jit(solution)/shard_map/ppermute | solution.py:22
  4.3 19.4 %collective-permute-start.2 = (bf16[16,4096]{1,0:T(8,128)(2,1)}, bf16[16,4096]{1,0:T(8,128)(2,1)S(1)}, u32[]{:S(2)}, u32[]{:S(2)}) collective-permute-start(bf16[16,4096]{1,0:T(8,128)(2,1)} %get-tuple-element.24), channel_id=1, source_target_pairs={{0,2},{1,3},{2,4},{3,5},{4,6},{5,7},{6,8},{7,9},{8,10},{9,11},{10,... | collective-permute-start | bytes 393224 | tf_op jit(solution)/shard_map/ppermute | solution.py:22
  6.2 20.9 %collective-permute-start.3 = (bf16[16,4096]{1,0:T(8,128)(2,1)}, bf16[16,4096]{1,0:T(8,128)(2,1)}, u32[]{:S(2)}, u32[]{:S(2)}) collective-permute-start(bf16[16,4096]{1,0:T(8,128)(2,1)} %get-tuple-element.23), channel_id=1, source_target_pairs={{0,4},{1,5},{2,6},{3,7},{4,8},{5,9},{6,10},{7,11},{8,12},{9,13},{1... | collective-permute-start | bytes 393224 | tf_op jit(solution)/shard_map/ppermute | solution.py:22
  9.5 17.7 %collective-permute-start.4 = (bf16[16,4096]{1,0:T(8,128)(2,1)}, bf16[16,4096]{1,0:T(8,128)(2,1)}, u32[]{:S(2)}, u32[]{:S(2)}) collective-permute-start(bf16[16,4096]{1,0:T(8,128)(2,1)} %get-tuple-element.22), channel_id=1, source_target_pairs={{0,8},{1,9},{2,10},{3,11},{4,12},{5,13},{6,14},{7,15},{8,16},{9,17... | collective-permute-start | bytes 393224 | tf_op jit(solution)/shard_map/ppermute | solution.py:22
  13.9 5.1 %copy-start.2 = (bf16[2,608,304]{1,2,0:T(8,128)(2,1)S(1)}, bf16[2,608,304]{1,2,0:T(8,128)(2,1)}, u32[]{:S(2)}) copy-start(bf16[2,608,304]{1,2,0:T(8,128)(2,1)} %param.8) | copy-start | bytes 2217988
  13.9 13.2 %collective-permute-start.5 = (bf16[16,4096]{1,0:T(8,128)(2,1)}, bf16[16,4096]{1,0:T(8,128)(2,1)}, u32[]{:S(2)}, u32[]{:S(2)}) collective-permute-start(bf16[16,4096]{1,0:T(8,128)(2,1)} %get-tuple-element.26), channel_id=1, source_target_pairs={{0,16},{1,17},{2,18},{3,19},{4,20},{5,21},{6,22},{7,23},{8,24},{9,... | collective-permute-start | bytes 393224 | tf_op jit(solution)/shard_map/ppermute | solution.py:22
  17.1 3.0 %copy-start.3 = (f32[2,608]{1,0:T(2,128)S(1)}, f32[2,608]{1,0:T(2,128)}, u32[]{:S(2)}) copy-start(f32[2,608]{1,0:T(2,128)} %param.9) | copy-start | bytes 14596
  17.1 3.2 %copy-start.4 = (f32[2,304]{1,0:T(2,128)S(1)}, f32[2,304]{1,0:T(2,128)}, u32[]{:S(2)}) copy-start(f32[2,304]{1,0:T(2,128)} %param.7) | copy-start | bytes 7300
  17.1 3.4 %copy-start.5 = (f32[2,304]{1,0:T(2,128)S(1)}, f32[2,304]{1,0:T(2,128)}, u32[]{:S(2)}) copy-start(f32[2,304]{1,0:T(2,128)} %param.11) | copy-start | bytes 7300
  20.6 9.3 %collective-permute-start.6 = (bf16[16,4096]{1,0:T(8,128)(2,1)}, bf16[16,4096]{1,0:T(8,128)(2,1)S(1)}, u32[]{:S(2)}, u32[]{:S(2)}) collective-permute-start(bf16[16,4096]{1,0:T(8,128)(2,1)} %get-tuple-element.21), channel_id=1, source_target_pairs={{0,32},{1,33},{2,34},{3,35},{4,36},{5,37},{6,38},{7,39},{8,40},{9,... | collective-permute-start | bytes 393224 | tf_op jit(solution)/shard_map/ppermute | solution.py:22
  23.6 10.9 %collective-permute-start = (bf16[16,4096]{1,0:T(8,128)(2,1)}, bf16[16,4096]{1,0:T(8,128)(2,1)S(1)}, u32[]{:S(2)}, u32[]{:S(2)}) collective-permute-start(bf16[16,4096]{1,0:T(8,128)(2,1)} %halo.1), channel_id=1, source_target_pairs={{0,1},{1,2},{2,3},{3,4},{4,5},{5,6},{6,7},{7,8},{8,9},{9,10},{10,1... | collective-permute-start | bytes 393224 | tf_op jit(solution)/shard_map/ppermute | solution.py:22
  44.1 1.2 %copy-start = (bf16[208,4096]{1,0:T(8,128)(2,1)}, bf16[208,4096]{1,0:T(8,128)(2,1)S(1)}, u32[]{:S(2)}) copy-start(bf16[208,4096]{1,0:T(8,128)(2,1)S(1)} %get-tuple-element.13.refs_0_) | copy-start | bytes 5111812
  45.3 15.0 %collective-permute-start.10 = (bf16[16,4096]{1,0:T(8,128)(2,1)S(1)}, bf16[16,4096]{1,0:T(8,128)(2,1)S(1)}, u32[]{:S(2)}, u32[]{:S(2)}) collective-permute-start(bf16[16,4096]{1,0:T(8,128)(2,1)S(1)} %get-tuple-element.17), channel_id=1, source_target_pairs={{0,4},{1,5},{2,6},{3,7},{4,8},{5,9},{6,10},{7,11},{8,12},{9,13},{1... | collective-permute-start | bytes 393224 | tf_op jit(solution)/shard_map/ppermute | solution.py:22
  45.3 15.0 %collective-permute-start.11 = (bf16[16,4096]{1,0:T(8,128)(2,1)S(1)}, bf16[16,4096]{1,0:T(8,128)(2,1)S(1)}, u32[]{:S(2)}, u32[]{:S(2)}) collective-permute-start(bf16[16,4096]{1,0:T(8,128)(2,1)S(1)} %get-tuple-element.18), channel_id=1, source_target_pairs={{0,8},{1,9},{2,10},{3,11},{4,12},{5,13},{6,14},{7,15},{8,16},{9,17... | collective-permute-start | bytes 393224 | tf_op jit(solution)/shard_map/ppermute | solution.py:22
  46.8 15.3 %collective-permute-start.12 = (bf16[16,4096]{1,0:T(8,128)(2,1)}, bf16[16,4096]{1,0:T(8,128)(2,1)S(1)}, u32[]{:S(2)}, u32[]{:S(2)}) collective-permute-start(bf16[16,4096]{1,0:T(8,128)(2,1)} %get-tuple-element.19), channel_id=1, source_target_pairs={{0,16},{1,17},{2,18},{3,19},{4,20},{5,21},{6,22},{7,23},{8,24},{9,... | collective-permute-start | bytes 393224 | tf_op jit(solution)/shard_map/ppermute | solution.py:22
  48.0 20.9 %collective-permute-start.13 = (bf16[16,4096]{1,0:T(8,128)(2,1)}, bf16[16,4096]{1,0:T(8,128)(2,1)S(1)}, u32[]{:S(2)}, u32[]{:S(2)}) collective-permute-start(bf16[16,4096]{1,0:T(8,128)(2,1)} %get-tuple-element.20), channel_id=1, source_target_pairs={{0,32},{1,33},{2,34},{3,35},{4,36},{5,37},{6,38},{7,39},{8,40},{9,... | collective-permute-start | bytes 393224 | tf_op jit(solution)/shard_map/ppermute | solution.py:22
  50.9 18.0 %collective-permute-start.7 = (bf16[16,4096]{1,0:T(8,128)(2,1)}, bf16[16,4096]{1,0:T(8,128)(2,1)S(1)}, u32[]{:S(2)}, u32[]{:S(2)}) collective-permute-start(bf16[16,4096]{1,0:T(8,128)(2,1)} %get-tuple-element.14), channel_id=1, source_target_pairs={{0,1},{1,2},{2,3},{3,4},{4,5},{5,6},{6,7},{7,8},{8,9},{9,10},{10,1... | collective-permute-start | bytes 393224 | tf_op jit(solution)/shard_map/ppermute | solution.py:22
  60.3 10.9 %collective-permute-start.8 = (bf16[16,4096]{1,0:T(8,128)(2,1)}, bf16[16,4096]{1,0:T(8,128)(2,1)S(1)}, u32[]{:S(2)}, u32[]{:S(2)}) collective-permute-start(bf16[16,4096]{1,0:T(8,128)(2,1)} %get-tuple-element.15), channel_id=1, source_target_pairs={{0,1},{1,2},{2,3},{3,4},{4,5},{5,6},{6,7},{7,8},{8,9},{9,10},{10,1... | collective-permute-start | bytes 393224 | tf_op jit(solution)/shard_map/ppermute | solution.py:22
  60.4 10.9 %collective-permute-start.9 = (bf16[16,4096]{1,0:T(8,128)(2,1)}, bf16[16,4096]{1,0:T(8,128)(2,1)S(1)}, u32[]{:S(2)}, u32[]{:S(2)}) collective-permute-start(bf16[16,4096]{1,0:T(8,128)(2,1)} %get-tuple-element.16), channel_id=1, source_target_pairs={{0,2},{1,3},{2,4},{3,5},{4,6},{5,7},{6,8},{7,9},{8,10},{9,11},{10,... | collective-permute-start | bytes 393224 | tf_op jit(solution)/shard_map/ppermute | solution.py:22
  71.3 1.5 %copy-start.1 = (bf16[208,4096]{1,0:T(8,128)(2,1)S(1)}, bf16[208,4096]{1,0:T(8,128)(2,1)}, u32[]{:S(2)}) copy-start(bf16[208,4096]{1,0:T(8,128)(2,1)} %copy-done) | copy-start | bytes 5111812

commit v2 on v1

v2 whole, which is shorter than its diff:
```python
import functools

import jax
import jax.numpy as jnp
from jax import lax
from jax.experimental import pallas as pl
from jax.experimental.pallas import tpu as pltpu
from jax.sharding import PartitionSpec as P

TRACK_CH = 16
TRACKS = 19
BLOCKS = 2
LANES = 128
NEAR_TILE = 1024
FAR_TILE = 1024
OUT_TILE = 1024
COST = 1
LIMITS = 8, 12, 8
GELU_A = 0.7978845608028654
GELU_B = 0.7978845608028654 * 0.044715
F32, BF16 = jnp.float32, jnp.bfloat16
VMEM = pl.BlockSpec(memory_space=pltpu.VMEM)


def shifted(value, axis, steps):
    count = lax.axis_size(axis)
    pairs = [(source, (source + steps) % count) for source in range(count)]
    return lax.ppermute(value, axis, pairs)


def after(value, *others):
    return lax.optimization_barrier((value, *others))[0]


def short_tracks(local_rows):
    count = 0
    while count + 1 < TRACKS and 2**count < local_rows:
        count = count + 1
    return count


def pack_halo(track, store, local_rows, short_count):
    lane = lax.broadcasted_iota(jnp.int32, (TRACK_CH, LANES), 1)
    packed = jnp.zeros((TRACK_CH, LANES), F32)
    for slot in range(short_count):
        offset = 2**slot
        if offset < LANES:
            last = track(1 + slot, local_rows - LANES, local_rows).astype(F32)
            moved = pltpu.roll(last, (2 * offset - 1) % LANES, 1)
            inside = (lane >= offset - 1) & (lane < 2 * offset - 1)
            packed = jnp.where(inside, moved, packed)
        else:
            store(offset, 2 * offset, track(1 + slot, local_rows - offset, local_rows))
    store(0, LANES, packed.astype(BF16))


def rotated_piece(track, halo, slot, begin, end):
    offset = 2**slot
    if offset < LANES:
        if begin == 0:
            packed = halo(0, LANES).astype(F32)
            before = pltpu.roll(packed, (LANES + 1 - 2 * offset) % LANES, 1)
            window = jnp.concatenate([before, track(1 + slot, 0, end).astype(F32)], 1)
        else:
            window = track(1 + slot, begin - LANES, end).astype(F32)
        return pltpu.roll(window, offset, 1)[:, LANES:].astype(BF16)
    parts = []
    if begin < offset:
        parts.append(halo(offset + begin, offset + min(end, offset)))
    if end > offset:
        parts.append(track(1 + slot, max(begin, offset) - offset, end - offset))
    return parts[0] if len(parts) == 1 else jnp.concatenate(parts, 1)


def split_kernel(first_row, tokens, *refs):
    count = len(refs) // 2
    copies = []
    for at in range(count):
        top = first_row + at * TRACK_CH
        copies.append(
            pltpu.make_async_copy(tokens.at[top : top + TRACK_CH, :], refs[at], refs[count + at])
        )
    for copy in copies:
        copy.start()
    for copy in copies:
        copy.wait()


def halo_kernel(local_rows, short_count, tail, out):
    base = local_rows - tail.shape[1]

    def track(t, begin, end):
        return tail[t * TRACK_CH : (t + 1) * TRACK_CH, begin - base : end - base]

    def store(begin, end, value):
        out[:, begin:end] = value

    pack_halo(track, store, local_rows, short_count)


def near_kernel(short_count, first, *refs):
    near, gain, w_in, *halo_in = refs[:-3]
    rotated, squares, partial = refs[-3:]
    near_rows, width = rotated.shape

    def track(t, begin, end):
        return near[t * TRACK_CH : (t + 1) * TRACK_CH, begin:end]

    def halo(begin, end):
        return halo_in[0][:, begin:end]

    for at in range(0, width, NEAR_TILE):
        begin, end = first + at, first + at + NEAR_TILE
        total = jnp.zeros((8, NEAR_TILE), F32)
        scaled = []
        for t in range(1 + short_count):
            rows = slice(t * TRACK_CH, (t + 1) * TRACK_CH)
            piece = track(0, begin, end) if t == 0 else rotated_piece(track, halo, t - 1, begin, end)
            rotated[rows, at : at + NEAR_TILE] = piece
            piece = piece.astype(F32)
            total = total + (piece[:8] * piece[:8] + piece[8:] * piece[8:])
            scaled.append((piece * gain[rows]).astype(BF16))
        squares[:, at : at + NEAR_TILE] = total
        partial[:, at : at + NEAR_TILE] = jnp.dot(
            w_in[:, :near_rows], jnp.concatenate(scaled, 0), preferred_element_type=F32
        ).astype(BF16)


def far_kernel(near_rows, last, *refs):
    nears = refs[:6]
    far = refs[6:12]
    gain, w_in, b_in, w_out, b_out = refs[12:17]
    outs = refs[17:]
    local_rows = far[0].shape[1]
    half_rows = local_rows // 2
    width = near_rows + len(far) * TRACK_CH
    for begin in range(0, local_rows, FAR_TILE):
        end = begin + FAR_TILE
        rotated, squares, partial = nears[:3] if begin < half_rows else nears[3:]
        at = begin % half_rows
        here = slice(at, at + FAR_TILE)
        parts = [ref[:, begin:end].astype(F32) for ref in far]
        total = squares[:, here]
        for part in parts:
            total = total + (part[:8] * part[:8] + part[8:] * part[8:])
        scale = lax.rsqrt(jnp.sum(total, axis=0, keepdims=True) * (1.0 / width) + 1e-06)
        far_part = jnp.concatenate(parts, 0)
        scaled = (far_part * gain[near_rows:]).astype(BF16)
        pre = partial[:, here].astype(F32) + jnp.dot(w_in[:, near_rows:], scaled, preferred_element_type=F32)
        pre = pre * scale + b_in[...]
        inner = pre * (GELU_A + GELU_B * (pre * pre))
        half = 0.5 * pre
        active = (half + half * jnp.tanh(inner)).astype(BF16)
        if last:
            out = jnp.dot(w_out[...], active, preferred_element_type=F32) + b_out[...]
            outs[0][:near_rows, begin:end] = (rotated[:, here].astype(F32) + out[:near_rows]).astype(BF16)
            outs[0][near_rows:, begin:end] = (far_part + out[near_rows:]).astype(BF16)
        else:
            out = jnp.dot(w_out[near_rows:], active, preferred_element_type=F32)
            mixed = (far_part + out + b_out[near_rows:]).astype(BF16)
            outs[0][:, begin:end] = active
            for track in range(len(far)):
                outs[1 + track][:, begin:end] = mixed[track * TRACK_CH : (track + 1) * TRACK_CH]


def out_kernel(short_count, low, high, active, w_out, b_out, near, bundle):
    near_rows, local_rows = near.shape
    half_rows = local_rows // 2
    for begin in range(0, local_rows, OUT_TILE):
        end = begin + OUT_TILE
        rotated = low if begin < half_rows else high
        at = begin % half_rows
        out = jnp.dot(w_out[:near_rows], active[:, begin:end], preferred_element_type=F32)
        kept = rotated[:, at : at + OUT_TILE].astype(F32)
        near[:, begin:end] = (kept + out + b_out[:near_rows]).astype(BF16)

    def track(t, begin, end):
        return near[t * TRACK_CH : (t + 1) * TRACK_CH, begin:end]

    def store(begin, end, value):
        bundle[:, begin:end] = value

    pack_halo(track, store, local_rows, short_count)


def call(kernel, out_shape, count, name, limit):
    return pl.pallas_call(
        kernel,
        out_shape=out_shape,
        in_specs=[VMEM] * count,
        out_specs=[VMEM] * len(out_shape),
        compiler_params=pltpu.CompilerParams(vmem_limit_bytes=limit << 20),
        cost_estimate=pl.CostEstimate(flops=COST, transcendentals=0, bytes_accessed=COST),
        name=name,
    )


def permuted(value, moves):
    return lax.ppermute(value, "seq", moves)


def routes():
    first, second = [], []
    for y in range(4):
        for z in range(8):
            for x in range(2):
                source = (y * 8 + z) * 2 + x
                middle = (((y + z // 4) % 4) * 8 + (z - 2) % 8) * 2 + x
                first.append((source, middle))
                second.append((middle, (source + 8) % 64))
    return first, second


def first_moves(far):
    to_middle, _ = routes()
    eight = permuted(far[3], to_middle)
    one = shifted(far[0], "seq", 1)
    back = shifted(far[5], "seq", -16)
    four = shifted(far[2], "seq", 4)
    two = shifted(far[1], "seq", 2)
    return eight, one, back, four, two


def last_moves(far, firsts, bundle):
    _, from_middle = routes()
    eight, one, back, four, two = firsts
    eight = permuted(eight, from_middle)
    back = shifted(back, "seq", -16)
    halo = shifted(after(bundle, two), "seq", 1)
    sixteen = shifted(after(far[4], one), "seq", 16)
    return [one, two, four, eight, sixteen, back], halo


def shards(tokens, norm_gain, in_weight, in_bias, out_weight, out_bias):
    width, local_rows = tokens.shape
    half_rows = local_rows // 2
    hidden = in_weight.shape[1]
    short_count = short_tracks(local_rows)
    far_count = TRACKS - 1 - short_count
    near_rows = (1 + short_count) * TRACK_CH
    one = jax.ShapeDtypeStruct((TRACK_CH, local_rows), BF16)
    near_shape = jax.ShapeDtypeStruct((near_rows, local_rows), BF16)
    half_shapes = [
        jax.ShapeDtypeStruct((near_rows, half_rows), BF16),
        jax.ShapeDtypeStruct((8, half_rows), F32),
        jax.ShapeDtypeStruct((hidden, half_rows), BF16),
    ]
    far = pl.pallas_call(
        functools.partial(split_kernel, near_rows),
        out_shape=[one] * far_count,
        in_specs=[pl.BlockSpec(memory_space=pl.ANY)],
        out_specs=[VMEM] * far_count,
        scratch_shapes=[pltpu.SemaphoreType.DMA] * far_count,
        name="split",
    )(tokens)
    bundle = pl.pallas_call(
        functools.partial(halo_kernel, local_rows, short_count),
        out_shape=one,
        grid=(1,),
        in_specs=[pl.BlockSpec((near_rows, local_rows // 2), lambda i: (0, 1))],
        out_specs=pl.BlockSpec((TRACK_CH, local_rows), lambda i: (0, 0)),
        name="halo",
    )(after(tokens, far[0]))
    near = tokens[:near_rows]
    firsts = first_moves(far)
    for block_no in range(BLOCKS):
        last = block_no == BLOCKS - 1
        gain = norm_gain[block_no][:, None]
        w_in, b_in = in_weight[block_no], in_bias[block_no][:, None]
        w_out, b_out = out_weight[block_no], out_bias[block_no][:, None]
        moved, halo = last_moves(far, firsts, bundle)
        high = call(functools.partial(near_kernel, short_count, half_rows), half_shapes, 3, "high", LIMITS[0])(
            after(near, firsts[4]), gain, w_in
        )
        low = call(functools.partial(near_kernel, short_count, 0), half_shapes, 4, "low", LIMITS[0])(
            near, gain, w_in, halo
        )
        out_shape = [jax.ShapeDtypeStruct((width, local_rows), BF16)]
        if not last:
            out_shape = [jax.ShapeDtypeStruct((hidden, local_rows), BF16)] + [one] * far_count
        outs = call(functools.partial(far_kernel, near_rows, last), out_shape, 17, "far", LIMITS[1])(
            *low, *high, *moved, gain, w_in, b_in, w_out, b_out
        )
        if last:
            return outs[0]
        active, far = outs[0], outs[1:]
        firsts = first_moves(far)
        near, bundle = call(
            functools.partial(out_kernel, short_count), [near_shape, one], 5, "out", 20
        )(low[0], high[0], after(active, firsts[4]), w_out, b_out)


def solution(mesh):
    return jax.shard_map(
        shards,
        mesh=mesh,
        in_specs=(P("batch", "seq"), P(), P(), P(), P(), P()),
        out_specs=P("batch", "seq"),
        check_vma=False,
    )
```

time: 82.1 us -> 73.3 us (0.89)
  waiting for transfers between devices: 26.9 us -> 2.03 us
  starting transfers between devices: 23.4 us -> 36.6 us
  Pallas kernels: 20.6 us -> 26.7 us
  local copies, waits for them, and re-layouts: 10.8 us -> 7.08 us
    ppermute x14, waiting for transfers between devices: 26.9 us -> 2.02 us  [shifted(): return lax.ppermute(value, axis, pairs)]
    ppermute x0 -> x4, starting transfers between devices: none -> 13.9 us  [permuted(): return lax.ppermute(value, 'seq', moves)]
    pallas_call x2 -> x8, Pallas kernels: 18.7 us -> 24.8 us  [the longest x2 15.5 us: shards(): call(functools.partial(far_kernel, near_rows, last), out_shape, 17, 'far'...]
    unnamed x14 -> x8, local copies, waits for them, and re-layouts: 4.16 us -> 1.52 us
    slice x2 -> x1, local copies, waits for them, and re-layouts: 2.95 us -> 1.92 us  [shards(): w_in, b_in = (in_weight[block_no], in_bias[block_no][:, None])]
  transfers between devices with their start and end apart: 14 -> 18, of which waited for: 6 -> 2; matrix products, arithmetic and copies ran while one was open for 7% -> 10% of each run, Pallas kernels for 2% -> 12%
where the time goes in v2:
time: 73.3 us; the launch traced here: 72.6 us
  starting transfers between devices  36.6 us (50%)
  Pallas kernels  26.7 us (36%)
  local copies, waits for them, and re-layouts  7.08 us (10%)
  waiting for transfers between devices  2.03 us (3%)
    ppermute x14, starting transfers between devices, shifted(): return lax.ppermute(value, axis, pairs)  22.6 us
    pallas_call x2, Pallas kernels, shards(): call(functools.partial(far_kernel, near_rows, last), out_shape, 17, 'far'...  15.5 us
    ppermute x4, starting transfers between devices, permuted(): return lax.ppermute(value, 'seq', moves)  13.9 us
    pallas_call x2, Pallas kernels, shards(): call(functools.partial(near_kernel, short_count, 0), half_shapes, 4, 'low...  2.91 us
    pallas_call x1, Pallas kernels, shards(): call(functools.partial(out_kernel, short_count), [near_shape, one], 5, 'o...  2.25 us
    pallas_call x1, Pallas kernels, shards(): pl.pallas_call(functools.partial(split_kernel, near_rows), out_shape=[one...  2.15 us
    ppermute x14, waiting for transfers between devices, shifted(): return lax.ppermute(value, axis, pairs)  2.02 us
    pallas_call x2, Pallas kernels, shards(): call(functools.partial(near_kernel, short_count, half_rows), half_shapes,...  1.93 us
  transfers between devices with their start and end apart: 18, of which 2 were waited for; matrix products, arithmetic and copies ran while one was open for 10% of the time, Pallas kernels for 12%

profile of v2, /device:TPU:2, one launch (start us, length us, event | category | flops | bytes accessed | tf_op | source)
XLA Modules:
  0.0 72.6 jit_solution(9424704211246278332)
XLA Ops:
  0.0 2.1 %split.1 = (bf16[16,4096]{1,0:T(8,128)(2,1)}, bf16[16,4096]{1,0:T(8,128)(2,1)}, bf16[16,4096]{1,0:T(8,128)(2,1)}, bf16[16,4096]{1,0:T(8,128)(2,1)}, bf16[16,4096]{1,0:T(8,128)(2,1)}, /*index=5*/bf16[16,4096]{1,0:T(8,128)(2,1)}) custom-call(bf16[304,4096]{1,0:T(8,128)(2,1)} %tail), custom_call_target="tpu_custom_call" | custom-call | tf_op jit(solution)/shard_map/split/pallas_call | solution.py:248
  2.2 2.0 %collective-permute-start = (bf16[16,4096]{1,0:T(8,128)(2,1)}, bf16[16,4096]{1,0:T(8,128)(2,1)S(1)}, u32[]{:S(2)}, u32[]{:S(2)}) collective-permute-start(bf16[16,4096]{1,0:T(8,128)(2,1)} %get-tuple-element.42), channel_id=1, source_target_pairs={{0,2},{1,3},{2,4},{3,5},{4,6},{5,7},{6,8},{7,9},{8,10},{9,11},{10,... | collective-permute-start | bytes 393224 | tf_op jit(solution)/shard_map/ppermute | solution.py:28
  4.2 2.1 %collective-permute-start.2 = (bf16[16,4096]{1,0:T(8,128)(2,1)}, bf16[16,4096]{1,0:T(8,128)(2,1)S(1)}, u32[]{:S(2)}, u32[]{:S(2)}) collective-permute-start(bf16[16,4096]{1,0:T(8,128)(2,1)} %get-tuple-element.40), channel_id=1, source_target_pairs={{0,1},{1,2},{2,3},{3,4},{4,5},{5,6},{6,7},{7,8},{8,9},{9,10},{10,1... | collective-permute-start | bytes 393224 | tf_op jit(solution)/shard_map/ppermute | solution.py:28
  6.3 5.4 %collective-permute-start.4 = (bf16[16,4096]{1,0:T(8,128)(2,1)}, bf16[16,4096]{1,0:T(8,128)(2,1)}, u32[]{:S(2)}, u32[]{:S(2)}) collective-permute-start(bf16[16,4096]{1,0:T(8,128)(2,1)} %get-tuple-element.52), channel_id=1, source_target_pairs={{0,12},{1,13},{2,14},{3,15},{4,0},{5,1},{6,2},{7,3},{8,20},{9,21},... | collective-permute-start | bytes 393224 | tf_op jit(solution)/shard_map/ppermute | solution.py:199
  11.7 3.0 %collective-permute-start.7 = (bf16[16,4096]{1,0:T(8,128)(2,1)}, bf16[16,4096]{1,0:T(8,128)(2,1)}, u32[]{:S(2)}, u32[]{:S(2)}) collective-permute-start(bf16[16,4096]{1,0:T(8,128)(2,1)} %get-tuple-element.55), channel_id=1, source_target_pairs={{0,48},{1,49},{2,50},{3,51},{4,52},{5,53},{6,54},{7,55},{8,56},{9,... | collective-permute-start | bytes 393224 | tf_op jit(solution)/shard_map/ppermute | solution.py:28
  14.7 1.6 %slice.33.refs_0_ = bf16[208,4096]{1,0:T(8,128)(2,1)S(1)} slice(bf16[304,4096]{1,0:T(8,128)(2,1)} %tail), slice={[0:208], [0:4096]} | slice | bytes 3407872 | tf_op jit(solution)/shard_map/slice | solution.py:264
  16.3 1.9 %halo.1 = bf16[16,4096]{1,0:T(8,128)(2,1)} custom-call(bf16[304,4096]{1,0:T(8,128)(2,1)} %tail), custom_call_target="tpu_custom_call" | custom-call | tf_op jit(solution)/shard_map/halo/pallas_call | solution.py:256
  18.2 1.9 %fusion = (bf16[1,608,304]{1,2,0:T(8,128)(2,1)}, bf16[1,608,304]{1,2,0:T(8,128)(2,1)S(1)}) fusion(bf16[2,608,304]{1,2,0:T(8,128)(2,1)} %param.8), kind=kLoop, calls=%fused_computation.8 | loop fusion | bytes 1478656 | tf_op jit(solution)/shard_map/slice | solution.py:269
  20.9 1.9 %collective-permute-start.1 = (bf16[16,4096]{1,0:T(8,128)(2,1)}, bf16[16,4096]{1,0:T(8,128)(2,1)S(1)}, u32[]{:S(2)}, u32[]{:S(2)}) collective-permute-start(bf16[16,4096]{1,0:T(8,128)(2,1)} %halo.1), channel_id=1, source_target_pairs={{0,1},{1,2},{2,3},{3,4},{4,5},{5,6},{6,7},{7,8},{8,9},{9,10},{10,1... | collective-permute-start | bytes 393224 | tf_op jit(solution)/shard_map/ppermute | solution.py:28
  22.9 3.2 %collective-permute-start.5 = (bf16[16,4096]{1,0:T(8,128)(2,1)}, bf16[16,4096]{1,0:T(8,128)(2,1)S(1)}, u32[]{:S(2)}, u32[]{:S(2)}) collective-permute-start(bf16[16,4096]{1,0:T(8,128)(2,1)} %collective-permute-done.4), channel_id=1, source_target_pairs={{12,8},{13,9},{14,10},{15,11},{0,12},{1,13},{2,14},{3,15},{20,16},... | collective-permute-start | bytes 393224 | tf_op jit(solution)/shard_map/ppermute | solution.py:199
  26.1 2.7 %collective-permute-start.8 = (bf16[16,4096]{1,0:T(8,128)(2,1)}, bf16[16,4096]{1,0:T(8,128)(2,1)S(1)}, u32[]{:S(2)}, u32[]{:S(2)}) collective-permute-start(bf16[16,4096]{1,0:T(8,128)(2,1)} %collective-permute-done.7), channel_id=1, source_target_pairs={{0,48},{1,49},{2,50},{3,51},{4,52},{5,53},{6,54},{7,55},{8,56},{9,... | collective-permute-start | bytes 393224 | tf_op jit(solution)/shard_map/ppermute | solution.py:28
  28.8 1.2 %slice_bitcast_fusion = (bf16[304,608]{1,0:T(8,128)(2,1)S(1)}, bf16[304,608]{1,0:T(8,128)(2,1)S(1)}) fusion(bf16[2,304,608]{2,1,0:T(8,128)(2,1)} %param.10), kind=kLoop, calls=%fused_computation | loop fusion | bytes 1478656 | tf_op jit(solution)/shard_map/squeeze | solution.py:270
  33.0 7.1 %far.2 = (bf16[608,4096]{1,0:T(8,128)(2,1)S(1)}, bf16[16,4096]{1,0:T(8,128)(2,1)S(1)}, bf16[16,4096]{1,0:T(8,128)(2,1)S(1)}, bf16[16,4096]{1,0:T(8,128)(2,1)}, b...) custom-call(bf16[208,2048]{1,0:T(8,128)(2,1)S(1)} %get-tuple-element.44.refs_0_.low, ...), custom_call_target="tpu_custom_call" | custom-call | flops 1 | bytes 1 | tf_op jit(solution)/shard_map/far/pallas_call | solution.py:281
  40.1 1.6 %collective-permute-start.11 = (bf16[16,4096]{1,0:T(8,128)(2,1)S(1)}, bf16[16,4096]{1,0:T(8,128)(2,1)S(1)}, u32[]{:S(2)}, u32[]{:S(2)}) collective-permute-start(bf16[16,4096]{1,0:T(8,128)(2,1)S(1)} %get-tuple-element.69), channel_id=1, source_target_pairs={{0,1},{1,2},{2,3},{3,4},{4,5},{5,6},{6,7},{7,8},{8,9},{9,10},{10,1... | collective-permute-start | bytes 393224 | tf_op jit(solution)/shard_map/ppermute | solution.py:28
  41.8 2.9 %collective-permute-start.13 = (bf16[16,4096]{1,0:T(8,128)(2,1)S(1)}, bf16[16,4096]{1,0:T(8,128)(2,1)}, u32[]{:S(2)}, u32[]{:S(2)}) collective-permute-start(bf16[16,4096]{1,0:T(8,128)(2,1)S(1)} %get-tuple-element.71), channel_id=1, source_target_pairs={{0,12},{1,13},{2,14},{3,15},{4,0},{5,1},{6,2},{7,3},{8,20},{9,21},... | collective-permute-start | bytes 393224 | tf_op jit(solution)/shard_map/ppermute | solution.py:199
  44.7 3.2 %collective-permute-start.16 = (bf16[16,4096]{1,0:T(8,128)(2,1)S(1)}, bf16[16,4096]{1,0:T(8,128)(2,1)}, u32[]{:S(2)}, u32[]{:S(2)}) collective-permute-start(bf16[16,4096]{1,0:T(8,128)(2,1)S(1)} %get-tuple-element.74), channel_id=1, source_target_pairs={{0,48},{1,49},{2,50},{3,51},{4,52},{5,53},{6,54},{7,55},{8,56},{9,... | collective-permute-start | bytes 393224 | tf_op jit(solution)/shard_map/ppermute | solution.py:28
  47.9 1.0 %collective-permute-done.9.refs_7_ = bf16[16,4096]{1,0:T(8,128)(2,1)S(1)} collective-permute-done((bf16[16,4096]{1,0:T(8,128)(2,1)S(1)}, bf16[16,4096]{1,0:T(8,128)(2,1)S(1)}, u32[]{:S(2)}, u32[]{:S(2)}) %collective-permute-start.9) | collective-permute-done | bytes 131104 | tf_op jit(solution)/shard_map/ppermute | solution.py:28
  48.9 2.3 %out.1 = (bf16[208,4096]{1,0:T(8,128)(2,1)S(1)}, bf16[16,4096]{1,0:T(8,128)(2,1)}) custom-call(bf16[208,2048]{1,0:T(8,128)(2,1)S(1)} %get-tuple-element.44.refs_0_.low, bf16[208,2048]{1,0:T(8,128)(2,1)S(1)} %get-tuple-element.46.refs_3_.high, bf16[608,4096]{1,0:T(8,128)(2,1)S(1)} %get-tuple-element.58.active, ...), custom_call_target="tpu_custom_call" | custom-call | flops 1 | bytes 1 | tf_op jit(solution)/shard_map/out/pallas_call | solution.py:288
  51.1 3.9 %collective-permute-start.10 = (bf16[16,4096]{1,0:T(8,128)(2,1)}, bf16[16,4096]{1,0:T(8,128)(2,1)}, u32[]{:S(2)}, u32[]{:S(2)}) collective-permute-start(bf16[16,4096]{1,0:T(8,128)(2,1)} %get-tuple-element.61), channel_id=1, source_target_pairs={{0,1},{1,2},{2,3},{3,4},{4,5},{5,6},{6,7},{7,8},{8,9},{9,10},{10,1... | collective-permute-start | bytes 393224 | tf_op jit(solution)/shard_map/ppermute | solution.py:28
  55.1 2.4 %collective-permute-start.14 = (bf16[16,4096]{1,0:T(8,128)(2,1)}, bf16[16,4096]{1,0:T(8,128)(2,1)}, u32[]{:S(2)}, u32[]{:S(2)}) collective-permute-start(bf16[16,4096]{1,0:T(8,128)(2,1)} %collective-permute-done.13), channel_id=1, source_target_pairs={{12,8},{13,9},{14,10},{15,11},{0,12},{1,13},{2,14},{3,15},{20,16},... | collective-permute-start | bytes 393224 | tf_op jit(solution)/shard_map/ppermute | solution.py:199
  57.4 2.1 %collective-permute-start.17 = (bf16[16,4096]{1,0:T(8,128)(2,1)}, bf16[16,4096]{1,0:T(8,128)(2,1)}, u32[]{:S(2)}, u32[]{:S(2)}) collective-permute-start(bf16[16,4096]{1,0:T(8,128)(2,1)} %collective-permute-done.16), channel_id=1, source_target_pairs={{0,48},{1,49},{2,50},{3,51},{4,52},{5,53},{6,54},{7,55},{8,56},{9,... | collective-permute-start | bytes 393224 | tf_op jit(solution)/shard_map/ppermute | solution.py:28
  59.6 1.2 %copy.23 = bf16[1,608,304]{2,1,0:T(8,128)(2,1)S(1)} copy(bf16[1,608,304]{1,2,0:T(8,128)(2,1)} %get-tuple-element.77) | data formatting | bytes 739328
  62.3 1.9 %low.3 = (bf16[208,2048]{1,0:T(8,128)(2,1)S(1)}, f32[8,2048]{1,0:T(8,128)S(1)}, bf16[608,2048]{1,0:T(8,128)(2,1)S(1)}) custom-call(bf16[208,4096]{1,0:T(8,128)(2,1)S(1)} %get-tuple-element.65.refs_0_, f32[304,1]{1,0:T(8,128)S(1)} %copy.17.refs_1_.refs_12_, bf16[608,304]{1,0:T(8,128)(2,1)S(1)} %bitcast.22, bf16[16,4096]{1,0:T(8,128)(2,1)} %collective-permute-done.10.refs_3_), custom_call_target="tpu_custom_call" | custom-call | flops 1 | bytes 1 | tf_op jit(solution)/shard_map/low/pallas_call | solution.py:275
  64.2 8.4 %far.3 = bf16[304,4096]{1,0:T(8,128)(2,1)} custom-call(bf16[208,2048]{1,0:T(8,128)(2,1)S(1)} %get-tuple-element.62.refs_0_, f32[8,2048]{1,0:T(8,128)S(1)} %get-tuple-element.63.refs_1_, bf16[608,2048]{1,0:T(8,128)(2,1)S(1)} %get-tuple-element.64.refs_2_, bf16[208,2048]{1,0:T(8,128)(2,1)S(1)} %get-tuple-element.66.refs_3_, ...), custom_call_target="tpu_custom_call" | custom-call | flops 1 | bytes 1 | tf_op jit(solution)/shard_map/far/pallas_call | solution.py:281
  (41 shorter events, 5.1 us)
Async XLA Ops:
  2.2 18.8 %collective-permute-start = (bf16[16,4096]{1,0:T(8,128)(2,1)}, bf16[16,4096]{1,0:T(8,128)(2,1)S(1)}, u32[]{:S(2)}, u32[]{:S(2)}) collective-permute-start(bf16[16,4096]{1,0:T(8,128)(2,1)} %get-tuple-element.42), channel_id=1, source_target_pairs={{0,2},{1,3},{2,4},{3,5},{4,6},{5,7},{6,8},{7,9},{8,10},{9,11},{10,... | collective-permute-start | bytes 393224 | tf_op jit(solution)/shard_map/ppermute | solution.py:28
  4.2 18.7 %collective-permute-start.2 = (bf16[16,4096]{1,0:T(8,128)(2,1)}, bf16[16,4096]{1,0:T(8,128)(2,1)S(1)}, u32[]{:S(2)}, u32[]{:S(2)}) collective-permute-start(bf16[16,4096]{1,0:T(8,128)(2,1)} %get-tuple-element.40), channel_id=1, source_target_pairs={{0,1},{1,2},{2,3},{3,4},{4,5},{5,6},{6,7},{7,8},{8,9},{9,10},{10,1... | collective-permute-start | bytes 393224 | tf_op jit(solution)/shard_map/ppermute | solution.py:28
  6.3 16.6 %collective-permute-start.4 = (bf16[16,4096]{1,0:T(8,128)(2,1)}, bf16[16,4096]{1,0:T(8,128)(2,1)}, u32[]{:S(2)}, u32[]{:S(2)}) collective-permute-start(bf16[16,4096]{1,0:T(8,128)(2,1)} %get-tuple-element.52), channel_id=1, source_target_pairs={{0,12},{1,13},{2,14},{3,15},{4,0},{5,1},{6,2},{7,3},{8,20},{9,21},... | collective-permute-start | bytes 393224 | tf_op jit(solution)/shard_map/ppermute | solution.py:199
  11.7 14.4 %collective-permute-start.7 = (bf16[16,4096]{1,0:T(8,128)(2,1)}, bf16[16,4096]{1,0:T(8,128)(2,1)}, u32[]{:S(2)}, u32[]{:S(2)}) collective-permute-start(bf16[16,4096]{1,0:T(8,128)(2,1)} %get-tuple-element.55), channel_id=1, source_target_pairs={{0,48},{1,49},{2,50},{3,51},{4,52},{5,53},{6,54},{7,55},{8,56},{9,... | collective-permute-start | bytes 393224 | tf_op jit(solution)/shard_map/ppermute | solution.py:28
  14.7 18.3 %collective-permute-start.3 = (bf16[16,4096]{1,0:T(8,128)(2,1)}, bf16[16,4096]{1,0:T(8,128)(2,1)}, u32[]{:S(2)}, u32[]{:S(2)}) collective-permute-start(bf16[16,4096]{1,0:T(8,128)(2,1)} %get-tuple-element.51), channel_id=1, source_target_pairs={{0,4},{1,5},{2,6},{3,7},{4,8},{5,9},{6,10},{7,11},{8,12},{9,13},{1... | collective-permute-start | bytes 393224 | tf_op jit(solution)/shard_map/ppermute | solution.py:28
  16.3 4.1 %copy-start.1 = (f32[2,304]{1,0:T(2,128)S(1)}, f32[2,304]{1,0:T(2,128)}, u32[]{:S(2)}) copy-start(f32[2,304]{1,0:T(2,128)} %param.7) | copy-start | bytes 7300
  16.3 4.3 %copy-start.2 = (f32[2,304]{1,0:T(2,128)S(1)}, f32[2,304]{1,0:T(2,128)}, u32[]{:S(2)}) copy-start(f32[2,304]{1,0:T(2,128)} %param.11) | copy-start | bytes 7300
  16.3 4.4 %copy-start = (f32[2,608]{1,0:T(2,128)S(1)}, f32[2,608]{1,0:T(2,128)}, u32[]{:S(2)}) copy-start(f32[2,608]{1,0:T(2,128)} %param.9) | copy-start | bytes 14596
  20.9 11.0 %collective-permute-start.1 = (bf16[16,4096]{1,0:T(8,128)(2,1)}, bf16[16,4096]{1,0:T(8,128)(2,1)S(1)}, u32[]{:S(2)}, u32[]{:S(2)}) collective-permute-start(bf16[16,4096]{1,0:T(8,128)(2,1)} %halo.1), channel_id=1, source_target_pairs={{0,1},{1,2},{2,3},{3,4},{4,5},{5,6},{6,7},{7,8},{8,9},{9,10},{10,1... | collective-permute-start | bytes 393224 | tf_op jit(solution)/shard_map/ppermute | solution.py:28
  22.9 10.1 %collective-permute-start.6 = (bf16[16,4096]{1,0:T(8,128)(2,1)}, bf16[16,4096]{1,0:T(8,128)(2,1)S(1)}, u32[]{:S(2)}, u32[]{:S(2)}) collective-permute-start(bf16[16,4096]{1,0:T(8,128)(2,1)} %get-tuple-element.54), channel_id=1, source_target_pairs={{0,16},{1,17},{2,18},{3,19},{4,20},{5,21},{6,22},{7,23},{8,24},{9,... | collective-permute-start | bytes 393224 | tf_op jit(solution)/shard_map/ppermute | solution.py:28
  22.9 10.1 %collective-permute-start.5 = (bf16[16,4096]{1,0:T(8,128)(2,1)}, bf16[16,4096]{1,0:T(8,128)(2,1)S(1)}, u32[]{:S(2)}, u32[]{:S(2)}) collective-permute-start(bf16[16,4096]{1,0:T(8,128)(2,1)} %collective-permute-done.4), channel_id=1, source_target_pairs={{12,8},{13,9},{14,10},{15,11},{0,12},{1,13},{2,14},{3,15},{20,16},... | collective-permute-start | bytes 393224 | tf_op jit(solution)/shard_map/ppermute | solution.py:199
  26.1 6.9 %collective-permute-start.8 = (bf16[16,4096]{1,0:T(8,128)(2,1)}, bf16[16,4096]{1,0:T(8,128)(2,1)S(1)}, u32[]{:S(2)}, u32[]{:S(2)}) collective-permute-start(bf16[16,4096]{1,0:T(8,128)(2,1)} %collective-permute-done.7), channel_id=1, source_target_pairs={{0,48},{1,49},{2,50},{3,51},{4,52},{5,53},{6,54},{7,55},{8,56},{9,... | collective-permute-start | bytes 393224 | tf_op jit(solution)/shard_map/ppermute | solution.py:28
  40.1 8.7 %collective-permute-start.9 = (bf16[16,4096]{1,0:T(8,128)(2,1)S(1)}, bf16[16,4096]{1,0:T(8,128)(2,1)S(1)}, u32[]{:S(2)}, u32[]{:S(2)}) collective-permute-start(bf16[16,4096]{1,0:T(8,128)(2,1)S(1)} %get-tuple-element.57), channel_id=1, source_target_pairs={{0,2},{1,3},{2,4},{3,5},{4,6},{5,7},{6,8},{7,9},{8,10},{9,11},{10,... | collective-permute-start | bytes 393224 | tf_op jit(solution)/shard_map/ppermute | solution.py:28
  40.1 11.0 %collective-permute-start.11 = (bf16[16,4096]{1,0:T(8,128)(2,1)S(1)}, bf16[16,4096]{1,0:T(8,128)(2,1)S(1)}, u32[]{:S(2)}, u32[]{:S(2)}) collective-permute-start(bf16[16,4096]{1,0:T(8,128)(2,1)S(1)} %get-tuple-element.69), channel_id=1, source_target_pairs={{0,1},{1,2},{2,3},{3,4},{4,5},{5,6},{6,7},{7,8},{8,9},{9,10},{10,1... | collective-permute-start | bytes 393224 | tf_op jit(solution)/shard_map/ppermute | solution.py:28
  41.8 13.3 %collective-permute-start.13 = (bf16[16,4096]{1,0:T(8,128)(2,1)S(1)}, bf16[16,4096]{1,0:T(8,128)(2,1)}, u32[]{:S(2)}, u32[]{:S(2)}) collective-permute-start(bf16[16,4096]{1,0:T(8,128)(2,1)S(1)} %get-tuple-element.71), channel_id=1, source_target_pairs={{0,12},{1,13},{2,14},{3,15},{4,0},{5,1},{6,2},{7,3},{8,20},{9,21},... | collective-permute-start | bytes 393224 | tf_op jit(solution)/shard_map/ppermute | solution.py:199
  44.7 12.7 %collective-permute-start.16 = (bf16[16,4096]{1,0:T(8,128)(2,1)S(1)}, bf16[16,4096]{1,0:T(8,128)(2,1)}, u32[]{:S(2)}, u32[]{:S(2)}) collective-permute-start(bf16[16,4096]{1,0:T(8,128)(2,1)S(1)} %get-tuple-element.74), channel_id=1, source_target_pairs={{0,48},{1,49},{2,50},{3,51},{4,52},{5,53},{6,54},{7,55},{8,56},{9,... | collective-permute-start | bytes 393224 | tf_op jit(solution)/shard_map/ppermute | solution.py:28
  47.9 16.3 %collective-permute-start.12 = (bf16[16,4096]{1,0:T(8,128)(2,1)}, bf16[16,4096]{1,0:T(8,128)(2,1)}, u32[]{:S(2)}, u32[]{:S(2)}) collective-permute-start(bf16[16,4096]{1,0:T(8,128)(2,1)} %get-tuple-element.70), channel_id=1, source_target_pairs={{0,4},{1,5},{2,6},{3,7},{4,8},{5,9},{6,10},{7,11},{8,12},{9,13},{1... | collective-permute-start | bytes 393224 | tf_op jit(solution)/shard_map/ppermute | solution.py:28
  51.1 11.1 %collective-permute-start.10 = (bf16[16,4096]{1,0:T(8,128)(2,1)}, bf16[16,4096]{1,0:T(8,128)(2,1)}, u32[]{:S(2)}, u32[]{:S(2)}) collective-permute-start(bf16[16,4096]{1,0:T(8,128)(2,1)} %get-tuple-element.61), channel_id=1, source_target_pairs={{0,1},{1,2},{2,3},{3,4},{4,5},{5,6},{6,7},{7,8},{8,9},{9,10},{10,1... | collective-permute-start | bytes 393224 | tf_op jit(solution)/shard_map/ppermute | solution.py:28
  55.0 9.1 %collective-permute-start.15 = (bf16[16,4096]{1,0:T(8,128)(2,1)}, bf16[16,4096]{1,0:T(8,128)(2,1)}, u32[]{:S(2)}, u32[]{:S(2)}) collective-permute-start(bf16[16,4096]{1,0:T(8,128)(2,1)} %get-tuple-element.73), channel_id=1, source_target_pairs={{0,16},{1,17},{2,18},{3,19},{4,20},{5,21},{6,22},{7,23},{8,24},{9,... | collective-permute-start | bytes 393224 | tf_op jit(solution)/shard_map/ppermute | solution.py:28
  55.1 9.1 %collective-permute-start.14 = (bf16[16,4096]{1,0:T(8,128)(2,1)}, bf16[16,4096]{1,0:T(8,128)(2,1)}, u32[]{:S(2)}, u32[]{:S(2)}) collective-permute-start(bf16[16,4096]{1,0:T(8,128)(2,1)} %collective-permute-done.13), channel_id=1, source_target_pairs={{12,8},{13,9},{14,10},{15,11},{0,12},{1,13},{2,14},{3,15},{20,16},... | collective-permute-start | bytes 393224 | tf_op jit(solution)/shard_map/ppermute | solution.py:199
  57.4 6.8 %collective-permute-start.17 = (bf16[16,4096]{1,0:T(8,128)(2,1)}, bf16[16,4096]{1,0:T(8,128)(2,1)}, u32[]{:S(2)}, u32[]{:S(2)}) collective-permute-start(bf16[16,4096]{1,0:T(8,128)(2,1)} %collective-permute-done.16), channel_id=1, source_target_pairs={{0,48},{1,49},{2,50},{3,51},{4,52},{5,53},{6,54},{7,55},{8,56},{9,... | collective-permute-start | bytes 393224 | tf_op jit(solution)/shard_map/ppermute | solution.py:28

commit v3 on v2

v3 whole, which is shorter than its diff:
```python
import functools

import jax
import jax.numpy as jnp
from jax import lax
from jax.experimental import pallas as pl
from jax.experimental.pallas import tpu as pltpu
from jax.sharding import PartitionSpec as P

TRACK_CH = 16
TRACKS = 19
BLOCKS = 2
LANES = 128
NEAR_TILE = 1024
TILE = 2048
COST = 1
GELU_A = 0.7978845608028654
ALPHA = (GELU_A * 0.044715) ** (1.0 / 3.0)
GELU_C = GELU_A / ALPHA
F32, BF16 = jnp.float32, jnp.bfloat16
VMEM = pl.BlockSpec(memory_space=pltpu.VMEM)


def shifted(value, axis, steps):
    count = lax.axis_size(axis)
    pairs = [(source, (source + steps) % count) for source in range(count)]
    return lax.ppermute(value, axis, pairs)


def after(value, *others):
    return lax.optimization_barrier((value, *others))[0]


def short_tracks(local_rows):
    count = 0
    while count + 1 < TRACKS and 2**count < local_rows:
        count = count + 1
    return count


def pack_halo(track, store, local_rows, short_count):
    lane = lax.broadcasted_iota(jnp.int32, (TRACK_CH, LANES), 1)
    packed = jnp.zeros((TRACK_CH, LANES), F32)
    for slot in range(short_count):
        offset = 2**slot
        if offset < LANES:
            last = track(1 + slot, local_rows - LANES, local_rows).astype(F32)
            moved = pltpu.roll(last, (2 * offset - 1) % LANES, 1)
            inside = (lane >= offset - 1) & (lane < 2 * offset - 1)
            packed = jnp.where(inside, moved, packed)
        else:
            store(offset, 2 * offset, track(1 + slot, local_rows - offset, local_rows))
    store(0, LANES, packed.astype(BF16))


def rotated_piece(track, halo, slot, begin, end):
    offset = 2**slot
    if offset < LANES:
        if begin == 0:
            packed = halo(0, LANES).astype(F32)
            before = pltpu.roll(packed, (LANES + 1 - 2 * offset) % LANES, 1)
            window = jnp.concatenate([before, track(1 + slot, 0, end).astype(F32)], 1)
        else:
            window = track(1 + slot, begin - LANES, end).astype(F32)
        return pltpu.roll(window, offset, 1)[:, LANES:].astype(BF16)
    parts = []
    if begin < offset:
        parts.append(halo(offset + begin, offset + min(end, offset)))
    if end > offset:
        parts.append(track(1 + slot, max(begin, offset) - offset, end - offset))
    return parts[0] if len(parts) == 1 else jnp.concatenate(parts, 1)


def split_kernel(first_row, tokens, *refs):
    count = len(refs) // 2
    copies = []
    for at in range(count):
        top = first_row + at * TRACK_CH
        copies.append(
            pltpu.make_async_copy(tokens.at[top : top + TRACK_CH, :], refs[at], refs[count + at])
        )
    for copy in copies:
        copy.start()
    for copy in copies:
        copy.wait()


def pair_kernel(short_count, tokens, out, tail, sem, own_sem):
    near_rows, half_rows = tail.shape
    local_rows = out.shape[1]
    base = local_rows - half_rows
    copy = pltpu.make_async_copy(tokens.at[:near_rows, base:], tail, sem)
    own = pltpu.make_async_copy(
        tokens.at[near_rows : near_rows + TRACK_CH, :], out.at[TRACK_CH:, :], own_sem
    )
    copy.start()
    own.start()
    copy.wait()

    def track(t, begin, end):
        return tail[t * TRACK_CH : (t + 1) * TRACK_CH, begin - base : end - base]

    def store(begin, end, value):
        out[:TRACK_CH, begin:end] = value

    pack_halo(track, store, local_rows, short_count)
    own.wait()


def weight_kernel(transposed, bias, *outs):
    depth, hidden = transposed.shape[1:]
    row = lax.broadcasted_iota(jnp.int32, (TRACK_CH, hidden), 0)
    for block_no, out in enumerate(outs):
        left = bias[block_no : block_no + 1, :] * ALPHA
        rows = jnp.zeros((TRACK_CH, hidden), F32)
        for at in range(3):
            term = left.astype(BF16).astype(F32)
            rows = jnp.where(row == at, jnp.broadcast_to(term, rows.shape), rows)
            left = left - term
        joined = jnp.concatenate([transposed[block_no], rows.astype(BF16)], 0)
        out[...] = jnp.transpose(joined)


def near_kernel(short_count, near, halo_in, rotated, squares):
    local_rows = halo_in.shape[1]

    def track(t, begin, end):
        return near[t * TRACK_CH : (t + 1) * TRACK_CH, begin:end]

    def halo(begin, end):
        return halo_in[:TRACK_CH, begin:end]

    for begin in range(0, local_rows, NEAR_TILE):
        end = begin + NEAR_TILE
        total = jnp.zeros((8, NEAR_TILE), F32)
        for t in range(1 + short_count):
            piece = track(0, begin, end) if t == 0 else rotated_piece(track, halo, t - 1, begin, end)
            rotated[t * TRACK_CH : (t + 1) * TRACK_CH, begin:end] = piece
            piece = piece.astype(F32)
            total = total + (piece[:8] * piece[:8] + piece[8:] * piece[8:])
        squares[:, begin:end] = total


def main_kernel(short_count, block_no, last, near, squares, pair, *refs):
    far, (gain, w_in, w_out, b_out), outs = refs[:5], refs[5:9], refs[9:]
    near_rows, local_rows = near.shape
    width = near_rows + (1 + len(far)) * TRACK_CH
    ones = jnp.ones((TRACK_CH, TILE), BF16)
    for begin in range(0, local_rows, TILE):
        end = begin + TILE
        parts = [pair[TRACK_CH:, begin:end].astype(F32)]
        parts += [ref[:, begin:end].astype(F32) for ref in far]
        total = squares[:, begin:end]
        for part in parts:
            total = total + (part[:8] * part[:8] + part[8:] * part[8:])
        scale = ALPHA * lax.rsqrt(jnp.sum(total, axis=0, keepdims=True) * (1.0 / width) + 1e-06)
        rotated = jnp.concatenate([near[:, begin:end].astype(F32)] + parts, 0)
        normed = (rotated * gain[...] * scale).astype(BF16)
        pre = jnp.dot(w_in[...], jnp.concatenate([normed, ones], 0), preferred_element_type=F32)
        inner = pre * (GELU_C + pre * pre)
        active = (pre * (1.0 + jnp.tanh(inner))).astype(BF16)
        out = jnp.dot(w_out[block_no], active, preferred_element_type=F32)
        mixed = (rotated + out * (0.5 / ALPHA) + b_out[...]).astype(BF16)
        if last:
            outs[0][:, begin:end] = mixed
        else:
            outs[0][:, begin:end] = mixed[:near_rows]
            outs[1][TRACK_CH:, begin:end] = mixed[near_rows : near_rows + TRACK_CH]
            for at in range(len(far)):
                top = near_rows + (1 + at) * TRACK_CH
                outs[2 + at][:, begin:end] = mixed[top : top + TRACK_CH]
    if not last:

        def track(t, begin, end):
            return outs[0][t * TRACK_CH : (t + 1) * TRACK_CH, begin:end]

        def store(begin, end, value):
            outs[1][:TRACK_CH, begin:end] = value

        pack_halo(track, store, local_rows, short_count)


def call(kernel, out_shape, in_specs, name, limit):
    return pl.pallas_call(
        kernel,
        out_shape=out_shape,
        in_specs=in_specs,
        out_specs=[VMEM] * len(out_shape),
        compiler_params=pltpu.CompilerParams(vmem_limit_bytes=limit << 20),
        cost_estimate=pl.CostEstimate(flops=COST, transcendentals=0, bytes_accessed=COST),
        name=name,
    )


def permuted(value, moves):
    return lax.ppermute(value, "seq", moves)


def routes():
    first, second = [], []
    for y in range(4):
        for z in range(8):
            for x in range(2):
                source = (y * 8 + z) * 2 + x
                middle = (((y + z // 4) % 4) * 8 + (z - 2) % 8) * 2 + x
                first.append((source, middle))
                second.append((middle, (source + 8) % 64))
    return first, second


def exchange(pair, far):
    two, four, eight, sixteen, thirty_two = far
    to_middle, from_middle = routes()
    eight = permuted(eight, to_middle)
    pair = shifted(pair, "seq", 1)
    back = shifted(thirty_two, "seq", -16)
    four = shifted(four, "seq", 4)
    two = shifted(two, "seq", 2)
    eight = permuted(eight, from_middle)
    back = shifted(back, "seq", -16)
    sixteen = shifted(after(sixteen, two), "seq", 16)
    return pair, [two, four, eight, sixteen, back]


def shards(tokens, norm_gain, in_weight, in_bias, out_weight, out_bias):
    width, local_rows = tokens.shape
    hidden = in_weight.shape[1]
    short_count = short_tracks(local_rows)
    far_count = TRACKS - 2 - short_count
    near_rows = (1 + short_count) * TRACK_CH
    one = jax.ShapeDtypeStruct((TRACK_CH, local_rows), BF16)
    two = jax.ShapeDtypeStruct((2 * TRACK_CH, local_rows), BF16)
    near_shape = jax.ShapeDtypeStruct((near_rows, local_rows), BF16)
    squares_shape = jax.ShapeDtypeStruct((8, local_rows), F32)
    whole = pl.BlockSpec(memory_space=pl.ANY)
    far = pl.pallas_call(
        functools.partial(split_kernel, near_rows + TRACK_CH),
        out_shape=[one] * far_count,
        in_specs=[whole],
        out_specs=[whole] * far_count,
        scratch_shapes=[pltpu.SemaphoreType.DMA] * far_count,
        name="split",
    )(tokens)
    pair = pl.pallas_call(
        functools.partial(pair_kernel, short_count),
        out_shape=two,
        in_specs=[whole],
        out_specs=VMEM,
        scratch_shapes=[
            pltpu.VMEM((near_rows, local_rows // 2), BF16),
            pltpu.SemaphoreType.DMA,
            pltpu.SemaphoreType.DMA,
        ],
        name="pair",
    )(tokens)
    w_ins = call(
        weight_kernel, [jax.ShapeDtypeStruct((hidden, width + TRACK_CH), BF16)] * BLOCKS, [VMEM] * 2, "weights", 8
    )(jnp.swapaxes(in_weight, 1, 2), in_bias)
    near = tokens
    for block_no in range(BLOCKS):
        last = block_no == BLOCKS - 1
        pair, moved = exchange(pair, far)
        rotated, squares = call(
            functools.partial(near_kernel, short_count), [near_shape, squares_shape], [VMEM] * 2, "near", 8
        )(near, pair)
        out_shape = [jax.ShapeDtypeStruct((width, local_rows), BF16)]
        if not last:
            out_shape = [near_shape, two] + [one] * far_count
        outs = call(
            functools.partial(main_kernel, short_count, block_no, last),
            out_shape,
            [VMEM] * (7 + far_count),
            "main",
            24,
        )(rotated, squares, pair, *moved, norm_gain[block_no][:, None], w_ins[block_no], out_weight, out_bias[block_no][:, None])
        if last:
            return outs[0]
        near, pair, far = outs[0], outs[1], outs[2:]


def solution(mesh):
    return jax.shard_map(
        shards,
        mesh=mesh,
        in_specs=(P("batch", "seq"), P(), P(), P(), P(), P()),
        out_specs=P("batch", "seq"),
        check_vma=False,
    )
```

time: 73.3 us -> 89.5 us (1.22)
  the two profiles are of different devices: /device:TPU:2 before, /device:TPU:30 now
where the time goes in v3:
time: 89.5 us; the launch traced here: 89.3 us
  Pallas kernels  40.2 us (45%)
  starting transfers between devices  33.9 us (38%)
  waiting for transfers between devices  10.5 us (12%)
  local copies, waits for them, and re-layouts  4.51 us (5%)
    pallas_call x1, Pallas kernels, shards(): pl.pallas_call(functools.partial(split_kernel, near_rows + TRACK_CH), out...  21 us
    ppermute x4, starting transfers between devices, permuted(): return lax.ppermute(value, 'seq', moves)  19.6 us
    pallas_call x2, Pallas kernels, shards(): call(functools.partial(main_kernel, short_count, block_no, last), out_sha...  15.5 us
    ppermute x12, starting transfers between devices, shifted(): return lax.ppermute(value, axis, pairs)  14.3 us
    ppermute x4, waiting for transfers between devices, permuted(): return lax.ppermute(value, 'seq', moves)  7.71 us
    ppermute x12, waiting for transfers between devices, shifted(): return lax.ppermute(value, axis, pairs)  2.75 us
    unnamed x24, local copies, waits for them, and re-layouts  2.6 us
    pallas_call x1, Pallas kernels, shards(): pl.pallas_call(functools.partial(pair_kernel, short_count), out_shape=two...  2.12 us
  transfers between devices with their start and end apart: 16, of which 5 were waited for; matrix products, arithmetic and copies ran while one was open for 2% of the time, Pallas kernels for 4%

profile of v3, /device:TPU:30, one launch (start us, length us, event | category | flops | bytes accessed | tf_op | source)
XLA Modules:
  0.0 89.3 jit_solution(14086579099919053596)
XLA Ops:
  0.0 21.0 %split.1 = (bf16[16,4096]{1,0:T(8,128)(2,1)}, bf16[16,4096]{1,0:T(8,128)(2,1)}, bf16[16,4096]{1,0:T(8,128)(2,1)}, bf16[16,4096]{1,0:T(8,128)(2,1)}, bf16[16,4096]{1,0:T(8,128)(2,1)}) custom-call(bf16[304,4096]{1,0:T(8,128)(2,1)} %tokens.3), custom_call_target="tpu_custom_call" | custom-call | tf_op jit(solution)/shard_map/split/pallas_call | solution.py:236
  21.0 2.0 %collective-permute-start.1 = (bf16[16,4096]{1,0:T(8,128)(2,1)}, bf16[16,4096]{1,0:T(8,128)(2,1)}, u32[]{:S(2)}, u32[]{:S(2)}) collective-permute-start(bf16[16,4096]{1,0:T(8,128)(2,1)} %get-tuple-element.27), channel_id=1, source_target_pairs={{0,2},{1,3},{2,4},{3,5},{4,6},{5,7},{6,8},{7,9},{8,10},{9,11},{10,... | collective-permute-start | bytes 393224 | tf_op jit(solution)/shard_map/ppermute | solution.py:27
  23.0 5.4 %collective-permute-start.3 = (bf16[16,4096]{1,0:T(8,128)(2,1)}, bf16[16,4096]{1,0:T(8,128)(2,1)}, u32[]{:S(2)}, u32[]{:S(2)}) collective-permute-start(bf16[16,4096]{1,0:T(8,128)(2,1)} %get-tuple-element.29), channel_id=1, source_target_pairs={{0,12},{1,13},{2,14},{3,15},{4,0},{5,1},{6,2},{7,3},{8,20},{9,21},... | collective-permute-start | bytes 393224 | tf_op jit(solution)/shard_map/ppermute | solution.py:196
  29.2 2.1 %pair.1 = bf16[32,4096]{1,0:T(8,128)(2,1)} custom-call(bf16[304,4096]{1,0:T(8,128)(2,1)} %tokens.3), custom_call_target="tpu_custom_call" | custom-call | tf_op jit(solution)/shard_map/pair/pallas_call | solution.py:244
  31.3 1.8 %collective-permute-start = (bf16[32,4096]{1,0:T(8,128)(2,1)}, bf16[32,4096]{1,0:T(8,128)(2,1)S(1)}, u32[]{:S(2)}, u32[]{:S(2)}) collective-permute-start(bf16[32,4096]{1,0:T(8,128)(2,1)} %pair.1), channel_id=1, source_target_pairs={{0,1},{1,2},{2,3},{3,4},{4,5},{5,6},{6,7},{7,8},{8,9},{9,10},{10,1... | collective-permute-start | bytes 786440 | tf_op jit(solution)/shard_map/ppermute | solution.py:27
  33.4 0.8 copy-done.5
  34.2 0.8 copy-done.7
  35.0 0.8 copy.7.refs_5_
  35.8 2.5 %collective-permute-start.5 = (bf16[16,4096]{1,0:T(8,128)(2,1)}, bf16[16,4096]{1,0:T(8,128)(2,1)}, u32[]{:S(2)}, u32[]{:S(2)}) collective-permute-start(bf16[16,4096]{1,0:T(8,128)(2,1)} %get-tuple-element.31), channel_id=1, source_target_pairs={{0,16},{1,17},{2,18},{3,19},{4,20},{5,21},{6,22},{7,23},{8,24},{9,... | collective-permute-start | bytes 393224 | tf_op jit(solution)/shard_map/ppermute | solution.py:27
  38.3 2.7 %collective-permute-start.4 = (bf16[16,4096]{1,0:T(8,128)(2,1)}, bf16[16,4096]{1,0:T(8,128)(2,1)}, u32[]{:S(2)}, u32[]{:S(2)}) collective-permute-start(bf16[16,4096]{1,0:T(8,128)(2,1)} %collective-permute-done.3), channel_id=1, source_target_pairs={{12,8},{13,9},{14,10},{15,11},{0,12},{1,13},{2,14},{3,15},{20,16},... | collective-permute-start | bytes 393224 | tf_op jit(solution)/shard_map/ppermute | solution.py:196
  41.0 1.9 %collective-permute-start.7 = (bf16[16,4096]{1,0:T(8,128)(2,1)}, bf16[16,4096]{1,0:T(8,128)(2,1)}, u32[]{:S(2)}, u32[]{:S(2)}) collective-permute-start(bf16[16,4096]{1,0:T(8,128)(2,1)} %collective-permute-done.6), channel_id=1, source_target_pairs={{0,48},{1,49},{2,50},{3,51},{4,52},{5,53},{6,54},{7,55},{8,56},{9,... | collective-permute-start | bytes 393224 | tf_op jit(solution)/shard_map/ppermute | solution.py:27
  43.0 0.8 copy.8.refs_8_
  44.5 2.1 %collective-permute-done.4.refs_2_ = bf16[16,4096]{1,0:T(8,128)(2,1)} collective-permute-done((bf16[16,4096]{1,0:T(8,128)(2,1)}, bf16[16,4096]{1,0:T(8,128)(2,1)}, u32[]{:S(2)}, u32[]{:S(2)}) %collective-permute-start.4) | collective-permute-done | bytes 131104 | tf_op jit(solution)/shard_map/ppermute | solution.py:196
  46.6 0.9 collective-permute-done.7.refs_4_
  47.5 7.6 %main.2 = (bf16[208,4096]{1,0:T(8,128)(2,1)S(1)}, bf16[32,4096]{1,0:T(8,128)(2,1)}, bf16[16,4096]{1,0:T(8,128)(2,1)S(1)}, bf16[16,4096]{1,0:T(8,128)(2,1)}, bf16...) custom-call(bf16[208,4096]{1,0:T(8,128)(2,1)S(1)} %get-tuple-element.25.near, ...), custom_call_target="tpu_custom_call" | custom-call | flops 1 | bytes 1 | tf_op jit(solution)/shard_map/main/pallas_call | solution.py:269
  55.7 1.5 %collective-permute-start.8 = (bf16[32,4096]{1,0:T(8,128)(2,1)}, bf16[32,4096]{1,0:T(8,128)(2,1)S(1)}, u32[]{:S(2)}, u32[]{:S(2)}) collective-permute-start(bf16[32,4096]{1,0:T(8,128)(2,1)} %get-tuple-element.35), channel_id=1, source_target_pairs={{0,1},{1,2},{2,3},{3,4},{4,5},{5,6},{6,7},{7,8},{8,9},{9,10},{10,1... | collective-permute-start | bytes 786440 | tf_op jit(solution)/shard_map/ppermute | solution.py:27
  57.2 6.6 %collective-permute-start.11 = (bf16[16,4096]{1,0:T(8,128)(2,1)S(1)}, bf16[16,4096]{1,0:T(8,128)(2,1)}, u32[]{:S(2)}, u32[]{:S(2)}) collective-permute-start(bf16[16,4096]{1,0:T(8,128)(2,1)S(1)} %get-tuple-element.40), channel_id=1, source_target_pairs={{0,12},{1,13},{2,14},{3,15},{4,0},{5,1},{6,2},{7,3},{8,20},{9,21},... | collective-permute-start | bytes 393224 | tf_op jit(solution)/shard_map/ppermute | solution.py:196
  63.9 3.2 %collective-permute-start.13 = (bf16[16,4096]{1,0:T(8,128)(2,1)}, bf16[16,4096]{1,0:T(8,128)(2,1)S(1)}, u32[]{:S(2)}, u32[]{:S(2)}) collective-permute-start(bf16[16,4096]{1,0:T(8,128)(2,1)} %get-tuple-element.42), channel_id=1, source_target_pairs={{0,16},{1,17},{2,18},{3,19},{4,20},{5,21},{6,22},{7,23},{8,24},{9,... | collective-permute-start | bytes 393224 | tf_op jit(solution)/shard_map/ppermute | solution.py:27
  67.1 1.9 %collective-permute-done.11 = bf16[16,4096]{1,0:T(8,128)(2,1)} collective-permute-done((bf16[16,4096]{1,0:T(8,128)(2,1)S(1)}, bf16[16,4096]{1,0:T(8,128)(2,1)}, u32[]{:S(2)}, u32[]{:S(2)}) %collective-permute-start.11) | collective-permute-done | bytes 131104 | tf_op jit(solution)/shard_map/ppermute | solution.py:196
  69.1 4.8 %collective-permute-start.12 = (bf16[16,4096]{1,0:T(8,128)(2,1)}, bf16[16,4096]{1,0:T(8,128)(2,1)}, u32[]{:S(2)}, u32[]{:S(2)}) collective-permute-start(bf16[16,4096]{1,0:T(8,128)(2,1)} %collective-permute-done.11), channel_id=1, source_target_pairs={{12,8},{13,9},{14,10},{15,11},{0,12},{1,13},{2,14},{3,15},{20,16},... | collective-permute-start | bytes 393224 | tf_op jit(solution)/shard_map/ppermute | solution.py:196
  74.8 3.7 %collective-permute-done.12.refs_2_ = bf16[16,4096]{1,0:T(8,128)(2,1)} collective-permute-done((bf16[16,4096]{1,0:T(8,128)(2,1)}, bf16[16,4096]{1,0:T(8,128)(2,1)}, u32[]{:S(2)}, u32[]{:S(2)}) %collective-permute-start.12) | collective-permute-done | bytes 131104 | tf_op jit(solution)/shard_map/ppermute | solution.py:196
  78.5 1.8 %collective-permute-done.15.refs_4_ = bf16[16,4096]{1,0:T(8,128)(2,1)} collective-permute-done((bf16[16,4096]{1,0:T(8,128)(2,1)}, bf16[16,4096]{1,0:T(8,128)(2,1)}, u32[]{:S(2)}, u32[]{:S(2)}) %collective-permute-start.15) | collective-permute-done | bytes 131104 | tf_op jit(solution)/shard_map/ppermute | solution.py:27
  80.4 1.0 %copy-done.6 = bf16[608,320]{1,0:T(8,128)(2,1)S(1)} copy-done((bf16[608,320]{1,0:T(8,128)(2,1)S(1)}, bf16[608,320]{1,0:T(8,128)(2,1)}, u32[]{:S(2)}) %copy-start.6) | copy-done | bytes 389144
  81.4 7.9 %main.3 = bf16[304,4096]{1,0:T(8,128)(2,1)} custom-call(bf16[208,4096]{1,0:T(8,128)(2,1)S(1)} %get-tuple-element.36.near, f32[8,4096]{1,0:T(8,128)S(1)} %get-tuple-element.37.squares, bf16[32,4096]{1,0:T(8,128)(2,1)S(1)} %collective-permute-done.8.halo_in.pair, bf16[16,4096]{1,0:T(8,128)(2,1)S(1)} %collective-permute-done.9.refs_0_, ...), custom_call_target="tpu_custom_call" | custom-call | flops 1 | bytes 1 | tf_op jit(solution)/shard_map/main/pallas_call | solution.py:269
  (45 shorter events, 3.4 us)
Async XLA Ops:
  21.0 12.1 %copy-start.10 = (f32[2,304]{1,0:T(2,128)S(1)}, f32[2,304]{1,0:T(2,128)}, u32[]{:S(2)}) copy-start(f32[2,304]{1,0:T(2,128)} %param.7) | copy-start | bytes 7300
  21.0 12.1 %copy-start.2 = (bf16[2,608,304]{1,2,0:T(8,128)(2,1)S(1)}, bf16[2,608,304]{1,2,0:T(8,128)(2,1)}, u32[]{:S(2)}) copy-start(bf16[2,608,304]{1,2,0:T(8,128)(2,1)} %param.8) | copy-start | bytes 2217988
  21.0 12.1 %copy-start.9 = (f32[2,608]{1,0:T(2,128)S(1)}, f32[2,608]{1,0:T(2,128)}, u32[]{:S(2)}) copy-start(f32[2,608]{1,0:T(2,128)} %bias.1) | copy-start | bytes 14596
  21.0 14.7 %collective-permute-start.1 = (bf16[16,4096]{1,0:T(8,128)(2,1)}, bf16[16,4096]{1,0:T(8,128)(2,1)}, u32[]{:S(2)}, u32[]{:S(2)}) collective-permute-start(bf16[16,4096]{1,0:T(8,128)(2,1)} %get-tuple-element.27), channel_id=1, source_target_pairs={{0,2},{1,3},{2,4},{3,5},{4,6},{5,7},{6,8},{7,9},{8,10},{9,11},{10,... | collective-permute-start | bytes 393224 | tf_op jit(solution)/shard_map/ppermute | solution.py:27
  23.0 15.2 %collective-permute-start.3 = (bf16[16,4096]{1,0:T(8,128)(2,1)}, bf16[16,4096]{1,0:T(8,128)(2,1)}, u32[]{:S(2)}, u32[]{:S(2)}) collective-permute-start(bf16[16,4096]{1,0:T(8,128)(2,1)} %get-tuple-element.29), channel_id=1, source_target_pairs={{0,12},{1,13},{2,14},{3,15},{4,0},{5,1},{6,2},{7,3},{8,20},{9,21},... | collective-permute-start | bytes 393224 | tf_op jit(solution)/shard_map/ppermute | solution.py:196
  28.4 12.6 %collective-permute-start.6 = (bf16[16,4096]{1,0:T(8,128)(2,1)}, bf16[16,4096]{1,0:T(8,128)(2,1)}, u32[]{:S(2)}, u32[]{:S(2)}) collective-permute-start(bf16[16,4096]{1,0:T(8,128)(2,1)} %get-tuple-element.32), channel_id=1, source_target_pairs={{0,48},{1,49},{2,50},{3,51},{4,52},{5,53},{6,54},{7,55},{8,56},{9,... | collective-permute-start | bytes 393224 | tf_op jit(solution)/shard_map/ppermute | solution.py:27
  29.2 13.8 %copy-start.11 = (f32[2,304]{1,0:T(2,128)S(1)}, f32[2,304]{1,0:T(2,128)}, u32[]{:S(2)}) copy-start(f32[2,304]{1,0:T(2,128)} %param.11) | copy-start | bytes 7300
  29.2 14.6 %copy-start = (bf16[304,4096]{1,0:T(8,128)(2,1)S(1)}, bf16[304,4096]{1,0:T(8,128)(2,1)}, u32[]{:S(2)}) copy-start(bf16[304,4096]{1,0:T(8,128)(2,1)} %tokens.3) | copy-start | bytes 7471108
  29.2 15.3 %collective-permute-start.2 = (bf16[16,4096]{1,0:T(8,128)(2,1)}, bf16[16,4096]{1,0:T(8,128)(2,1)}, u32[]{:S(2)}, u32[]{:S(2)}) collective-permute-start(bf16[16,4096]{1,0:T(8,128)(2,1)} %get-tuple-element.28), channel_id=1, source_target_pairs={{0,4},{1,5},{2,6},{3,7},{4,8},{5,9},{6,10},{7,11},{8,12},{9,13},{1... | collective-permute-start | bytes 393224 | tf_op jit(solution)/shard_map/ppermute | solution.py:27
  31.3 12.5 %collective-permute-start = (bf16[32,4096]{1,0:T(8,128)(2,1)}, bf16[32,4096]{1,0:T(8,128)(2,1)S(1)}, u32[]{:S(2)}, u32[]{:S(2)}) collective-permute-start(bf16[32,4096]{1,0:T(8,128)(2,1)} %pair.1), channel_id=1, source_target_pairs={{0,1},{1,2},{2,3},{3,4},{4,5},{5,6},{6,7},{7,8},{8,9},{9,10},{10,1... | collective-permute-start | bytes 786440 | tf_op jit(solution)/shard_map/ppermute | solution.py:27
  35.0 12.6 %copy-start.1 = (bf16[2,304,608]{2,1,0:T(8,128)(2,1)S(1)}, bf16[2,304,608]{2,1,0:T(8,128)(2,1)}, u32[]{:S(2)}) copy-start(bf16[2,304,608]{2,1,0:T(8,128)(2,1)} %refs_7_.3) | copy-start | bytes 2217988
  35.8 8.7 %collective-permute-start.5 = (bf16[16,4096]{1,0:T(8,128)(2,1)}, bf16[16,4096]{1,0:T(8,128)(2,1)}, u32[]{:S(2)}, u32[]{:S(2)}) collective-permute-start(bf16[16,4096]{1,0:T(8,128)(2,1)} %get-tuple-element.31), channel_id=1, source_target_pairs={{0,16},{1,17},{2,18},{3,19},{4,20},{5,21},{6,22},{7,23},{8,24},{9,... | collective-permute-start | bytes 393224 | tf_op jit(solution)/shard_map/ppermute | solution.py:27
  38.3 8.4 %collective-permute-start.4 = (bf16[16,4096]{1,0:T(8,128)(2,1)}, bf16[16,4096]{1,0:T(8,128)(2,1)}, u32[]{:S(2)}, u32[]{:S(2)}) collective-permute-start(bf16[16,4096]{1,0:T(8,128)(2,1)} %collective-permute-done.3), channel_id=1, source_target_pairs={{12,8},{13,9},{14,10},{15,11},{0,12},{1,13},{2,14},{3,15},{20,16},... | collective-permute-start | bytes 393224 | tf_op jit(solution)/shard_map/ppermute | solution.py:196
  41.0 6.5 %collective-permute-start.7 = (bf16[16,4096]{1,0:T(8,128)(2,1)}, bf16[16,4096]{1,0:T(8,128)(2,1)}, u32[]{:S(2)}, u32[]{:S(2)}) collective-permute-start(bf16[16,4096]{1,0:T(8,128)(2,1)} %collective-permute-done.6), channel_id=1, source_target_pairs={{0,48},{1,49},{2,50},{3,51},{4,52},{5,53},{6,54},{7,55},{8,56},{9,... | collective-permute-start | bytes 393224 | tf_op jit(solution)/shard_map/ppermute | solution.py:27
  43.8 3.7 %copy-start.4 = (f32[304,1]{1,0:T(8,128)S(1)}, f32[304,1]{1,0:T(8,128)}, u32[]{:S(2)}) copy-start(f32[304,1]{1,0:T(8,128)} %copy.8.refs_8_) | copy-start | bytes 3652
  43.8 3.7 %copy-start.8 = (bf16[608,320]{1,0:T(8,128)(2,1)S(1)}, bf16[608,320]{1,0:T(8,128)(2,1)}, u32[]{:S(2)}) copy-start(bf16[608,320]{1,0:T(8,128)(2,1)} %copy-done.7) | copy-start | bytes 1167364
  55.1 8.8 %collective-permute-start.9 = (bf16[16,4096]{1,0:T(8,128)(2,1)S(1)}, bf16[16,4096]{1,0:T(8,128)(2,1)S(1)}, u32[]{:S(2)}, u32[]{:S(2)}) collective-permute-start(bf16[16,4096]{1,0:T(8,128)(2,1)S(1)} %get-tuple-element.38), channel_id=1, source_target_pairs={{0,2},{1,3},{2,4},{3,5},{4,6},{5,7},{6,8},{7,9},{8,10},{9,11},{10,... | collective-permute-start | bytes 393224 | tf_op jit(solution)/shard_map/ppermute | solution.py:27
  55.7 18.4 %collective-permute-start.8 = (bf16[32,4096]{1,0:T(8,128)(2,1)}, bf16[32,4096]{1,0:T(8,128)(2,1)S(1)}, u32[]{:S(2)}, u32[]{:S(2)}) collective-permute-start(bf16[32,4096]{1,0:T(8,128)(2,1)} %get-tuple-element.35), channel_id=1, source_target_pairs={{0,1},{1,2},{2,3},{3,4},{4,5},{5,6},{6,7},{7,8},{8,9},{9,10},{10,1... | collective-permute-start | bytes 786440 | tf_op jit(solution)/shard_map/ppermute | solution.py:27
  57.2 11.8 %collective-permute-start.11 = (bf16[16,4096]{1,0:T(8,128)(2,1)S(1)}, bf16[16,4096]{1,0:T(8,128)(2,1)}, u32[]{:S(2)}, u32[]{:S(2)}) collective-permute-start(bf16[16,4096]{1,0:T(8,128)(2,1)S(1)} %get-tuple-element.40), channel_id=1, source_target_pairs={{0,12},{1,13},{2,14},{3,15},{4,0},{5,1},{6,2},{7,3},{8,20},{9,21},... | collective-permute-start | bytes 393224 | tf_op jit(solution)/shard_map/ppermute | solution.py:196
  63.9 10.0 %collective-permute-start.14 = (bf16[16,4096]{1,0:T(8,128)(2,1)S(1)}, bf16[16,4096]{1,0:T(8,128)(2,1)}, u32[]{:S(2)}, u32[]{:S(2)}) collective-permute-start(bf16[16,4096]{1,0:T(8,128)(2,1)S(1)} %get-tuple-element.43), channel_id=1, source_target_pairs={{0,48},{1,49},{2,50},{3,51},{4,52},{5,53},{6,54},{7,55},{8,56},{9,... | collective-permute-start | bytes 393224 | tf_op jit(solution)/shard_map/ppermute | solution.py:27
  63.9 10.9 %collective-permute-start.10 = (bf16[16,4096]{1,0:T(8,128)(2,1)}, bf16[16,4096]{1,0:T(8,128)(2,1)S(1)}, u32[]{:S(2)}, u32[]{:S(2)}) collective-permute-start(bf16[16,4096]{1,0:T(8,128)(2,1)} %get-tuple-element.39), channel_id=1, source_target_pairs={{0,4},{1,5},{2,6},{3,7},{4,8},{5,9},{6,10},{7,11},{8,12},{9,13},{1... | collective-permute-start | bytes 393224 | tf_op jit(solution)/shard_map/ppermute | solution.py:27
  63.9 10.9 %collective-permute-start.13 = (bf16[16,4096]{1,0:T(8,128)(2,1)}, bf16[16,4096]{1,0:T(8,128)(2,1)S(1)}, u32[]{:S(2)}, u32[]{:S(2)}) collective-permute-start(bf16[16,4096]{1,0:T(8,128)(2,1)} %get-tuple-element.42), channel_id=1, source_target_pairs={{0,16},{1,17},{2,18},{3,19},{4,20},{5,21},{6,22},{7,23},{8,24},{9,... | collective-permute-start | bytes 393224 | tf_op jit(solution)/shard_map/ppermute | solution.py:27
  69.1 9.5 %collective-permute-start.12 = (bf16[16,4096]{1,0:T(8,128)(2,1)}, bf16[16,4096]{1,0:T(8,128)(2,1)}, u32[]{:S(2)}, u32[]{:S(2)}) collective-permute-start(bf16[16,4096]{1,0:T(8,128)(2,1)} %collective-permute-done.11), channel_id=1, source_target_pairs={{12,8},{13,9},{14,10},{15,11},{0,12},{1,13},{2,14},{3,15},{20,16},... | collective-permute-start | bytes 393224 | tf_op jit(solution)/shard_map/ppermute | solution.py:196
  73.9 6.5 %collective-permute-start.15 = (bf16[16,4096]{1,0:T(8,128)(2,1)}, bf16[16,4096]{1,0:T(8,128)(2,1)}, u32[]{:S(2)}, u32[]{:S(2)}) collective-permute-start(bf16[16,4096]{1,0:T(8,128)(2,1)} %collective-permute-done.14), channel_id=1, source_target_pairs={{0,48},{1,49},{2,50},{3,51},{4,52},{5,53},{6,54},{7,55},{8,56},{9,... | collective-permute-start | bytes 393224 | tf_op jit(solution)/shard_map/ppermute | solution.py:27
  (4 other events, 6.3 us)

commit v4 on v3

--- a/solution.py
+++ b/solution.py
@@ -71,46 +71,39 @@
     return parts[0] if len(parts) == 1 else jnp.concatenate(parts, 1)
 
 
-def split_kernel(first_row, tokens, *refs):
-    count = len(refs) // 2
-    copies = []
-    for at in range(count):
-        top = first_row + at * TRACK_CH
+def first_kernel(short_count, tokens, *refs):
+    pair, far = refs[0], refs[1:6]
+    tail, sems = refs[6], refs[7:]
+    near_rows, half_rows = tail.shape
+    local_rows = pair.shape[1]
+    base = local_rows - half_rows
+    copies = [pltpu.make_async_copy(tokens.at[:near_rows, base:], tail, sems[0])]
+    for at, target in enumerate([pair.at[TRACK_CH:, :], *far]):
+        top = near_rows + at * TRACK_CH
         copies.append(
-            pltpu.make_async_copy(tokens.at[top : top + TRACK_CH, :], refs[at], refs[count + at])
+            pltpu.make_async_copy(tokens.at[top : top + TRACK_CH, :], target, sems[1 + at])
         )
     for copy in copies:
         copy.start()
-    for copy in copies:
-        copy.wait()
-
-
-def pair_kernel(short_count, tokens, out, tail, sem, own_sem):
-    near_rows, half_rows = tail.shape
-    local_rows = out.shape[1]
-    base = local_rows - half_rows
-    copy = pltpu.make_async_copy(tokens.at[:near_rows, base:], tail, sem)
-    own = pltpu.make_async_copy(
-        tokens.at[near_rows : near_rows + TRACK_CH, :], out.at[TRACK_CH:, :], own_sem
-    )
-    copy.start()
-    own.start()
-    copy.wait()
+    copies[0].wait()
 
     def track(t, begin, end):
         return tail[t * TRACK_CH : (t + 1) * TRACK_CH, begin - base : end - base]
 
     def store(begin, end, value):
-        out[:TRACK_CH, begin:end] = value
+        pair[:TRACK_CH, begin:end] = value
 
     pack_halo(track, store, local_rows, short_count)
-    own.wait()
-
-
-def weight_kernel(transposed, bias, *outs):
+    for copy in copies[1:]:
+        copy.wait()
+
+
+def weight_kernel(transposed, bias, gain, last_bias, *refs):
+    outs, made, sems = refs[:3], refs[3:6], refs[6:]
     depth, hidden = transposed.shape[1:]
     row = lax.broadcasted_iota(jnp.int32, (TRACK_CH, hidden), 0)
-    for block_no, out in enumerate(outs):
+    copies = []
+    for block_no in range(BLOCKS):
         left = bias[block_no : block_no + 1, :] * ALPHA
         rows = jnp.zeros((TRACK_CH, hidden), F32)
         for at in range(3):
@@ -118,7 +111,15 @@
             rows = jnp.where(row == at, jnp.broadcast_to(term, rows.shape), rows)
             left = left - term
         joined = jnp.concatenate([transposed[block_no], rows.astype(BF16)], 0)
-        out[...] = jnp.transpose(joined)
+        made[block_no][...] = jnp.transpose(joined)
+        copies.append(pltpu.make_async_copy(made[block_no], outs[block_no], sems[block_no]))
+        copies[-1].start()
+    columns = [gain[...], last_bias[...], jnp.zeros((8 - 2 * BLOCKS, depth), F32)]
+    made[2][...] = jnp.transpose(jnp.concatenate(columns, 0))
+    copies.append(pltpu.make_async_copy(made[2], outs[2], sems[2]))
+    copies[-1].start()
+    for copy in copies:
+        copy.wait()
 
 
 def near_kernel(short_count, near, halo_in, rotated, squares):
@@ -142,10 +143,12 @@
 
 
 def main_kernel(short_count, block_no, last, near, squares, pair, *refs):
-    far, (gain, w_in, w_out, b_out), outs = refs[:5], refs[5:9], refs[9:]
+    far, (columns, w_in, w_out), outs = refs[:5], refs[5:8], refs[8:]
     near_rows, local_rows = near.shape
     width = near_rows + (1 + len(far)) * TRACK_CH
     ones = jnp.ones((TRACK_CH, TILE), BF16)
+    gain = columns[:, block_no : block_no + 1]
+    b_out = columns[:, BLOCKS + block_no : BLOCKS + block_no + 1]
     for begin in range(0, local_rows, TILE):
         end = begin + TILE
         parts = [pair[TRACK_CH:, begin:end].astype(F32)]
@@ -155,12 +158,12 @@
             total = total + (part[:8] * part[:8] + part[8:] * part[8:])
         scale = ALPHA * lax.rsqrt(jnp.sum(total, axis=0, keepdims=True) * (1.0 / width) + 1e-06)
         rotated = jnp.concatenate([near[:, begin:end].astype(F32)] + parts, 0)
-        normed = (rotated * gain[...] * scale).astype(BF16)
+        normed = (rotated * gain * scale).astype(BF16)
         pre = jnp.dot(w_in[...], jnp.concatenate([normed, ones], 0), preferred_element_type=F32)
         inner = pre * (GELU_C + pre * pre)
         active = (pre * (1.0 + jnp.tanh(inner))).astype(BF16)
         out = jnp.dot(w_out[block_no], active, preferred_element_type=F32)
-        mixed = (rotated + out * (0.5 / ALPHA) + b_out[...]).astype(BF16)
+        mixed = (rotated + out * (0.5 / ALPHA) + b_out).astype(BF16)
         if last:
             outs[0][:, begin:end] = mixed
         else:
@@ -233,29 +236,24 @@
     near_shape = jax.ShapeDtypeStruct((near_rows, local_rows), BF16)
     squares_shape = jax.ShapeDtypeStruct((8, local_rows), F32)
     whole = pl.BlockSpec(memory_space=pl.ANY)
-    far = pl.pallas_call(
-        functools.partial(split_kernel, near_rows + TRACK_CH),
-        out_shape=[one] * far_count,
-        in_specs=[whole],
-        out_specs=[whole] * far_count,
-        scratch_shapes=[pltpu.SemaphoreType.DMA] * far_count,
-        name="split",
+    pair, *far = pl.pallas_call(
+        functools.partial(first_kernel, short_count),
+        out_shape=[two] + [one] * far_count,
+        in_specs=[pl.BlockSpec(memory_space=pl.ANY)],
+        out_specs=[VMEM] * (1 + far_count),
+        scratch_shapes=[pltpu.VMEM((near_rows, local_rows // 2), BF16)]
+        + [pltpu.SemaphoreType.DMA] * (2 + far_count),
+        name="first",
     )(tokens)
-    pair = pl.pallas_call(
-        functools.partial(pair_kernel, short_count),
-        out_shape=two,
-        in_specs=[whole],
-        out_specs=VMEM,
-        scratch_shapes=[
-            pltpu.VMEM((near_rows, local_rows // 2), BF16),
-            pltpu.SemaphoreType.DMA,
-            pltpu.SemaphoreType.DMA,
-        ],
-        name="pair",
-    )(tokens)
-    w_ins = call(
-        weight_kernel, [jax.ShapeDtypeStruct((hidden, width + TRACK_CH), BF16)] * BLOCKS, [VMEM] * 2, "weights", 8
-    )(jnp.swapaxes(in_weight, 1, 2), in_bias)
+    made = [((hidden, width + TRACK_CH), BF16)] * BLOCKS + [((width, 8), F32)]
+    *w_ins, columns = pl.pallas_call(
+        weight_kernel,
+        out_shape=[jax.ShapeDtypeStruct(*entry) for entry in made],
+        in_specs=[VMEM] * 4,
+        out_specs=[pl.BlockSpec(memory_space=pltpu.HBM)] * 3,
+        scratch_shapes=[pltpu.VMEM(*entry) for entry in made] + [pltpu.SemaphoreType.DMA] * 3,
+        name="weights",
+    )(jnp.swapaxes(in_weight, 1, 2), in_bias, norm_gain, out_bias)
     near = tokens
     for block_no in range(BLOCKS):
         last = block_no == BLOCKS - 1
@@ -269,10 +267,10 @@
         outs = call(
             functools.partial(main_kernel, short_count, block_no, last),
             out_shape,
-            [VMEM] * (7 + far_count),
+            [VMEM] * (6 + far_count),
             "main",
             24,
-        )(rotated, squares, pair, *moved, norm_gain[block_no][:, None], w_ins[block_no], out_weight, out_bias[block_no][:, None])
+        )(rotated, squares, pair, *moved, columns, w_ins[block_no], out_weight)
         if last:
             return outs[0]
         near, pair, far = outs[0], outs[1], outs[2:]

time: 89.5 us -> 64.1 us (0.72)
  the two profiles are of different devices: /device:TPU:30 before, /device:TPU:34 now
where the time goes in v4:
time: 64.1 us; the launch traced here: 64 us
  starting transfers between devices  31.7 us (49%)
  Pallas kernels  19.7 us (31%)
  waiting for transfers between devices  11.7 us (18%)
  local copies, waits for them, and re-layouts  0.66 us (1%)
    ppermute x12, starting transfers between devices, shifted(): return lax.ppermute(value, axis, pairs)  22.8 us
    pallas_call x2, Pallas kernels, shards(): call(functools.partial(main_kernel, short_count, block_no, last), out_sha...  13.5 us
    ppermute x4, waiting for transfers between devices, permuted(): return lax.ppermute(value, 'seq', moves)  10.4 us
    ppermute x4, starting transfers between devices, permuted(): return lax.ppermute(value, 'seq', moves)  8.93 us
    pallas_call x1, Pallas kernels, shards(): pl.pallas_call(functools.partial(first_kernel, short_count), out_shape=[t...  2.48 us
    pallas_call x1, Pallas kernels, shards(): pl.pallas_call(weight_kernel, out_shape=[jax.ShapeDtypeStruct(*entry) for...  2.4 us
    ppermute x12, waiting for transfers between devices, shifted(): return lax.ppermute(value, axis, pairs)  1.36 us
    pallas_call x2, Pallas kernels, shards(): call(functools.partial(near_kernel, short_count), [near_shape, squares_sh...  1.33 us
  transfers between devices with their start and end apart: 16, of which 4 were waited for; matrix products, arithmetic and copies ran while one was open for 0% of the time, Pallas kernels for 6%

profile of v4, /device:TPU:34, one launch (start us, length us, event | category | flops | bytes accessed | tf_op | source)
XLA Modules:
  0.0 64.0 jit_solution(2495186426108410583)
XLA Ops:
  0.0 2.5 %first.1 = (bf16[32,4096]{1,0:T(8,128)(2,1)}, bf16[16,4096]{1,0:T(8,128)(2,1)}, bf16[16,4096]{1,0:T(8,128)(2,1)}, bf16[16,4096]{1,0:T(8,128)(2,1)}, bf16[16,4096]{1,0:T(8,128)(2,1)}, /*index=5*/bf16[16,4096]{1,0:T(8,128)(2,1)}) custom-call(bf16[304,4096]{1,0:T(8,128)(2,1)} %near.4), custom_call_target="tpu_custom_call" | custom-call | tf_op jit(solution)/shard_map/first/pallas_call | solution.py:239
  2.5 2.0 %collective-permute-start.1 = (bf16[16,4096]{1,0:T(8,128)(2,1)}, bf16[16,4096]{1,0:T(8,128)(2,1)S(1)}, u32[]{:S(2)}, u32[]{:S(2)}) collective-permute-start(bf16[16,4096]{1,0:T(8,128)(2,1)} %get-tuple-element.30), channel_id=1, source_target_pairs={{0,2},{1,3},{2,4},{3,5},{4,6},{5,7},{6,8},{7,9},{8,10},{9,11},{10,... | collective-permute-start | bytes 393224 | tf_op jit(solution)/shard_map/ppermute | solution.py:27
  4.5 2.1 %collective-permute-start = (bf16[32,4096]{1,0:T(8,128)(2,1)}, bf16[32,4096]{1,0:T(8,128)(2,1)S(1)}, u32[]{:S(2)}, u32[]{:S(2)}) collective-permute-start(bf16[32,4096]{1,0:T(8,128)(2,1)} %get-tuple-element.27), channel_id=1, source_target_pairs={{0,1},{1,2},{2,3},{3,4},{4,5},{5,6},{6,7},{7,8},{8,9},{9,10},{10,1... | collective-permute-start | bytes 786440 | tf_op jit(solution)/shard_map/ppermute | solution.py:27
  6.6 3.6 %collective-permute-start.3 = (bf16[16,4096]{1,0:T(8,128)(2,1)}, bf16[16,4096]{1,0:T(8,128)(2,1)}, u32[]{:S(2)}, u32[]{:S(2)}) collective-permute-start(bf16[16,4096]{1,0:T(8,128)(2,1)} %get-tuple-element.32), channel_id=1, source_target_pairs={{0,12},{1,13},{2,14},{3,15},{4,0},{5,1},{6,2},{7,3},{8,20},{9,21},... | collective-permute-start | bytes 393224 | tf_op jit(solution)/shard_map/ppermute | solution.py:199
  10.2 3.0 %collective-permute-start.6 = (bf16[16,4096]{1,0:T(8,128)(2,1)}, bf16[16,4096]{1,0:T(8,128)(2,1)}, u32[]{:S(2)}, u32[]{:S(2)}) collective-permute-start(bf16[16,4096]{1,0:T(8,128)(2,1)} %get-tuple-element.35), channel_id=1, source_target_pairs={{0,48},{1,49},{2,50},{3,51},{4,52},{5,53},{6,54},{7,55},{8,56},{9,... | collective-permute-start | bytes 393224 | tf_op jit(solution)/shard_map/ppermute | solution.py:27
  13.2 0.9 %collective-permute-start.2 = (bf16[16,4096]{1,0:T(8,128)(2,1)}, bf16[16,4096]{1,0:T(8,128)(2,1)}, u32[]{:S(2)}, u32[]{:S(2)}) collective-permute-start(bf16[16,4096]{1,0:T(8,128)(2,1)} %get-tuple-element.31), channel_id=1, source_target_pairs={{0,4},{1,5},{2,6},{3,7},{4,8},{5,9},{6,10},{7,11},{8,12},{9,13},{1... | collective-permute-start | bytes 393224 | tf_op jit(solution)/shard_map/ppermute | solution.py:27
  14.1 0.6 copy-done.5
  14.8 2.2 %collective-permute-done.3 = bf16[16,4096]{1,0:T(8,128)(2,1)} collective-permute-done((bf16[16,4096]{1,0:T(8,128)(2,1)}, bf16[16,4096]{1,0:T(8,128)(2,1)}, u32[]{:S(2)}, u32[]{:S(2)}) %collective-permute-start.3) | collective-permute-done | bytes 131104 | tf_op jit(solution)/shard_map/ppermute | solution.py:199
  16.9 1.3 %collective-permute-start.4 = (bf16[16,4096]{1,0:T(8,128)(2,1)}, bf16[16,4096]{1,0:T(8,128)(2,1)}, u32[]{:S(2)}, u32[]{:S(2)}) collective-permute-start(bf16[16,4096]{1,0:T(8,128)(2,1)} %collective-permute-done.3), channel_id=1, source_target_pairs={{12,8},{13,9},{14,10},{15,11},{0,12},{1,13},{2,14},{3,15},{20,16},... | collective-permute-start | bytes 393224 | tf_op jit(solution)/shard_map/ppermute | solution.py:199
  18.2 3.0 %collective-permute-start.7 = (bf16[16,4096]{1,0:T(8,128)(2,1)}, bf16[16,4096]{1,0:T(8,128)(2,1)}, u32[]{:S(2)}, u32[]{:S(2)}) collective-permute-start(bf16[16,4096]{1,0:T(8,128)(2,1)} %collective-permute-done.6), channel_id=1, source_target_pairs={{0,48},{1,49},{2,50},{3,51},{4,52},{5,53},{6,54},{7,55},{8,56},{9,... | collective-permute-start | bytes 393224 | tf_op jit(solution)/shard_map/ppermute | solution.py:27
  21.2 2.4 %weights.1 = (bf16[608,320]{1,0:T(8,128)(2,1)}, bf16[608,320]{1,0:T(8,128)(2,1)}, f32[304,8]{1,0:T(8,128)}) custom-call(bf16[2,304,608]{2,1,0:T(8,128)(2,1)} %bitcast.1, f32[2,608]{1,0:T(2,128)} %bias.1, f32[2,304]{1,0:T(2,128)} %gain.1, f32[2,304]{1,0:T(2,128)} %last_bias.1), custom_call_target="tpu_custom_call" | custom-call | tf_op jit(solution)/shard_map/weights/pallas_call | solution.py:249
  23.7 0.7 %near.3 = (bf16[208,4096]{1,0:T(8,128)(2,1)S(1)}, f32[8,4096]{1,0:T(8,128)S(1)}) custom-call(bf16[304,4096]{1,0:T(8,128)(2,1)S(1)} %copy-done, bf16[32,4096]{1,0:T(8,128)(2,1)S(1)} %collective-permute-done.halo_in.pair), custom_call_target="tpu_custom_call" | custom-call | flops 1 | bytes 1 | tf_op jit(solution)/shard_map/near/pallas_call | solution.py:261
  24.4 4.0 %collective-permute-done.4.refs_2_ = bf16[16,4096]{1,0:T(8,128)(2,1)} collective-permute-done((bf16[16,4096]{1,0:T(8,128)(2,1)}, bf16[16,4096]{1,0:T(8,128)(2,1)}, u32[]{:S(2)}, u32[]{:S(2)}) %collective-permute-start.4) | collective-permute-done | bytes 131104 | tf_op jit(solution)/shard_map/ppermute | solution.py:199
  28.4 6.6 %main.2 = (bf16[208,4096]{1,0:T(8,128)(2,1)S(1)}, bf16[32,4096]{1,0:T(8,128)(2,1)S(1)}, bf16[16,4096]{1,0:T(8,128)(2,1)S(1)}, bf16[16,4096]{1,0:T(8,128)(2,1)S(1...) custom-call(bf16[208,4096]{1,0:T(8,128)(2,1)S(1)} %get-tuple-element.28.near, ...), custom_call_target="tpu_custom_call" | custom-call | flops 1 | bytes 1 | tf_op jit(solution)/shard_map/main/pallas_call | solution.py:267
  35.0 3.6 %collective-permute-start.8 = (bf16[32,4096]{1,0:T(8,128)(2,1)S(1)}, bf16[32,4096]{1,0:T(8,128)(2,1)S(1)}, u32[]{:S(2)}, u32[]{:S(2)}) collective-permute-start(bf16[32,4096]{1,0:T(8,128)(2,1)S(1)} %get-tuple-element.39), channel_id=1, source_target_pairs={{0,1},{1,2},{2,3},{3,4},{4,5},{5,6},{6,7},{7,8},{8,9},{9,10},{10,1... | collective-permute-start | bytes 786440 | tf_op jit(solution)/shard_map/ppermute | solution.py:27
  38.6 1.1 %collective-permute-start.11 = (bf16[16,4096]{1,0:T(8,128)(2,1)S(1)}, bf16[16,4096]{1,0:T(8,128)(2,1)S(1)}, u32[]{:S(2)}, u32[]{:S(2)}) collective-permute-start(bf16[16,4096]{1,0:T(8,128)(2,1)S(1)} %get-tuple-element.44), channel_id=1, source_target_pairs={{0,12},{1,13},{2,14},{3,15},{4,0},{5,1},{6,2},{7,3},{8,20},{9,21},... | collective-permute-start | bytes 393224 | tf_op jit(solution)/shard_map/ppermute | solution.py:199
  39.7 3.0 %collective-permute-start.14 = (bf16[16,4096]{1,0:T(8,128)(2,1)S(1)}, bf16[16,4096]{1,0:T(8,128)(2,1)S(1)}, u32[]{:S(2)}, u32[]{:S(2)}) collective-permute-start(bf16[16,4096]{1,0:T(8,128)(2,1)S(1)} %get-tuple-element.47), channel_id=1, source_target_pairs={{0,48},{1,49},{2,50},{3,51},{4,52},{5,53},{6,54},{7,55},{8,56},{9,... | collective-permute-start | bytes 393224 | tf_op jit(solution)/shard_map/ppermute | solution.py:27
  42.8 2.2 %collective-permute-start.10 = (bf16[16,4096]{1,0:T(8,128)(2,1)S(1)}, bf16[16,4096]{1,0:T(8,128)(2,1)S(1)}, u32[]{:S(2)}, u32[]{:S(2)}) collective-permute-start(bf16[16,4096]{1,0:T(8,128)(2,1)S(1)} %get-tuple-element.43), channel_id=1, source_target_pairs={{0,4},{1,5},{2,6},{3,7},{4,8},{5,9},{6,10},{7,11},{8,12},{9,13},{1... | collective-permute-start | bytes 393224 | tf_op jit(solution)/shard_map/ppermute | solution.py:27
  45.0 3.0 %collective-permute-start.12 = (bf16[16,4096]{1,0:T(8,128)(2,1)S(1)}, bf16[16,4096]{1,0:T(8,128)(2,1)S(1)}, u32[]{:S(2)}, u32[]{:S(2)}) collective-permute-start(bf16[16,4096]{1,0:T(8,128)(2,1)S(1)} %collective-permute-done.11), channel_id=1, source_target_pairs={{12,8},{13,9},{14,10},{15,11},{0,12},{1,13},{2,14},{3,15},{20,16},... | collective-permute-start | bytes 393224 | tf_op jit(solution)/shard_map/ppermute | solution.py:199
  48.0 2.8 %collective-permute-start.15 = (bf16[16,4096]{1,0:T(8,128)(2,1)S(1)}, bf16[16,4096]{1,0:T(8,128)(2,1)S(1)}, u32[]{:S(2)}, u32[]{:S(2)}) collective-permute-start(bf16[16,4096]{1,0:T(8,128)(2,1)S(1)} %collective-permute-done.14), channel_id=1, source_target_pairs={{0,48},{1,49},{2,50},{3,51},{4,52},{5,53},{6,54},{7,55},{8,56},{9,... | collective-permute-start | bytes 393224 | tf_op jit(solution)/shard_map/ppermute | solution.py:27
  50.8 0.7 %near.5 = (bf16[208,4096]{1,0:T(8,128)(2,1)S(1)}, f32[8,4096]{1,0:T(8,128)S(1)}) custom-call(bf16[208,4096]{1,0:T(8,128)(2,1)S(1)} %get-tuple-element.38.near, bf16[32,4096]{1,0:T(8,128)(2,1)S(1)} %collective-permute-done.8.halo_in.pair), custom_call_target="tpu_custom_call" | custom-call | flops 1 | bytes 1 | tf_op jit(solution)/shard_map/near/pallas_call | solution.py:261
  51.5 1.3 %collective-permute-done.10.refs_1_ = bf16[16,4096]{1,0:T(8,128)(2,1)S(1)} collective-permute-done((bf16[16,4096]{1,0:T(8,128)(2,1)S(1)}, bf16[16,4096]{1,0:T(8,128)(2,1)S(1)}, u32[]{:S(2)}, u32[]{:S(2)}) %collective-permute-start.10) | collective-permute-done | bytes 131104 | tf_op jit(solution)/shard_map/ppermute | solution.py:27
  52.8 4.2 %collective-permute-done.12.refs_2_ = bf16[16,4096]{1,0:T(8,128)(2,1)S(1)} collective-permute-done((bf16[16,4096]{1,0:T(8,128)(2,1)S(1)}, bf16[16,4096]{1,0:T(8,128)(2,1)S(1)}, u32[]{:S(2)}, u32[]{:S(2)}) %collective-permute-start.12) | collective-permute-done | bytes 131104 | tf_op jit(solution)/shard_map/ppermute | solution.py:199
  57.1 6.9 %main.3 = bf16[304,4096]{1,0:T(8,128)(2,1)} custom-call(bf16[208,4096]{1,0:T(8,128)(2,1)S(1)} %get-tuple-element.40.near, f32[8,4096]{1,0:T(8,128)S(1)} %get-tuple-element.41.squares, bf16[32,4096]{1,0:T(8,128)(2,1)S(1)} %collective-permute-done.8.halo_in.pair, bf16[16,4096]{1,0:T(8,128)(2,1)S(1)} %collective-permute-done.9.refs_0_, ...), custom_call_target="tpu_custom_call" | custom-call | flops 1 | bytes 1 | tf_op jit(solution)/shard_map/main/pallas_call | solution.py:267
  (28 shorter events, 0.1 us)
Async XLA Ops:
  0.0 23.7 %copy-start = (bf16[304,4096]{1,0:T(8,128)(2,1)S(1)}, bf16[304,4096]{1,0:T(8,128)(2,1)}, u32[]{:S(2)}) copy-start(bf16[304,4096]{1,0:T(8,128)(2,1)} %near.4) | copy-start | bytes 7471108
  2.5 11.6 %collective-permute-start.1 = (bf16[16,4096]{1,0:T(8,128)(2,1)}, bf16[16,4096]{1,0:T(8,128)(2,1)S(1)}, u32[]{:S(2)}, u32[]{:S(2)}) collective-permute-start(bf16[16,4096]{1,0:T(8,128)(2,1)} %get-tuple-element.30), channel_id=1, source_target_pairs={{0,2},{1,3},{2,4},{3,5},{4,6},{5,7},{6,8},{7,9},{8,10},{9,11},{10,... | collective-permute-start | bytes 393224 | tf_op jit(solution)/shard_map/ppermute | solution.py:27
  4.5 19.2 %collective-permute-start = (bf16[32,4096]{1,0:T(8,128)(2,1)}, bf16[32,4096]{1,0:T(8,128)(2,1)S(1)}, u32[]{:S(2)}, u32[]{:S(2)}) collective-permute-start(bf16[32,4096]{1,0:T(8,128)(2,1)} %get-tuple-element.27), channel_id=1, source_target_pairs={{0,1},{1,2},{2,3},{3,4},{4,5},{5,6},{6,7},{7,8},{8,9},{9,10},{10,1... | collective-permute-start | bytes 786440 | tf_op jit(solution)/shard_map/ppermute | solution.py:27
  6.6 10.3 %collective-permute-start.3 = (bf16[16,4096]{1,0:T(8,128)(2,1)}, bf16[16,4096]{1,0:T(8,128)(2,1)}, u32[]{:S(2)}, u32[]{:S(2)}) collective-permute-start(bf16[16,4096]{1,0:T(8,128)(2,1)} %get-tuple-element.32), channel_id=1, source_target_pairs={{0,12},{1,13},{2,14},{3,15},{4,0},{5,1},{6,2},{7,3},{8,20},{9,21},... | collective-permute-start | bytes 393224 | tf_op jit(solution)/shard_map/ppermute | solution.py:199
  10.2 8.0 %collective-permute-start.6 = (bf16[16,4096]{1,0:T(8,128)(2,1)}, bf16[16,4096]{1,0:T(8,128)(2,1)}, u32[]{:S(2)}, u32[]{:S(2)}) collective-permute-start(bf16[16,4096]{1,0:T(8,128)(2,1)} %get-tuple-element.35), channel_id=1, source_target_pairs={{0,48},{1,49},{2,50},{3,51},{4,52},{5,53},{6,54},{7,55},{8,56},{9,... | collective-permute-start | bytes 393224 | tf_op jit(solution)/shard_map/ppermute | solution.py:27
  13.2 11.1 %collective-permute-start.2 = (bf16[16,4096]{1,0:T(8,128)(2,1)}, bf16[16,4096]{1,0:T(8,128)(2,1)}, u32[]{:S(2)}, u32[]{:S(2)}) collective-permute-start(bf16[16,4096]{1,0:T(8,128)(2,1)} %get-tuple-element.31), channel_id=1, source_target_pairs={{0,4},{1,5},{2,6},{3,7},{4,8},{5,9},{6,10},{7,11},{8,12},{9,13},{1... | collective-permute-start | bytes 393224 | tf_op jit(solution)/shard_map/ppermute | solution.py:27
  14.1 0.6 copy-start.5
  14.8 9.6 %collective-permute-start.5 = (bf16[16,4096]{1,0:T(8,128)(2,1)}, bf16[16,4096]{1,0:T(8,128)(2,1)}, u32[]{:S(2)}, u32[]{:S(2)}) collective-permute-start(bf16[16,4096]{1,0:T(8,128)(2,1)} %get-tuple-element.34), channel_id=1, source_target_pairs={{0,16},{1,17},{2,18},{3,19},{4,20},{5,21},{6,22},{7,23},{8,24},{9,... | collective-permute-start | bytes 393224 | tf_op jit(solution)/shard_map/ppermute | solution.py:27
  16.9 11.4 %collective-permute-start.4 = (bf16[16,4096]{1,0:T(8,128)(2,1)}, bf16[16,4096]{1,0:T(8,128)(2,1)}, u32[]{:S(2)}, u32[]{:S(2)}) collective-permute-start(bf16[16,4096]{1,0:T(8,128)(2,1)} %collective-permute-done.3), channel_id=1, source_target_pairs={{12,8},{13,9},{14,10},{15,11},{0,12},{1,13},{2,14},{3,15},{20,16},... | collective-permute-start | bytes 393224 | tf_op jit(solution)/shard_map/ppermute | solution.py:199
  18.2 10.1 %collective-permute-start.7 = (bf16[16,4096]{1,0:T(8,128)(2,1)}, bf16[16,4096]{1,0:T(8,128)(2,1)}, u32[]{:S(2)}, u32[]{:S(2)}) collective-permute-start(bf16[16,4096]{1,0:T(8,128)(2,1)} %collective-permute-done.6), channel_id=1, source_target_pairs={{0,48},{1,49},{2,50},{3,51},{4,52},{5,53},{6,54},{7,55},{8,56},{9,... | collective-permute-start | bytes 393224 | tf_op jit(solution)/shard_map/ppermute | solution.py:27
  21.2 7.2 %copy-start.1 = (bf16[2,304,608]{2,1,0:T(8,128)(2,1)S(1)}, bf16[2,304,608]{2,1,0:T(8,128)(2,1)}, u32[]{:S(2)}) copy-start(bf16[2,304,608]{2,1,0:T(8,128)(2,1)} %refs_7_.3) | copy-start | bytes 2217988
  23.6 4.7 %copy-start.2 = (f32[304,8]{1,0:T(8,128)S(1)}, f32[304,8]{1,0:T(8,128)}, u32[]{:S(2)}) copy-start(f32[304,8]{1,0:T(8,128)} %get-tuple-element.36.refs_5_) | copy-start | bytes 29188
  23.6 4.7 %copy-start.4 = (bf16[608,320]{1,0:T(8,128)(2,1)S(1)}, bf16[608,320]{1,0:T(8,128)(2,1)}, u32[]{:S(2)}) copy-start(bf16[608,320]{1,0:T(8,128)(2,1)} %get-tuple-element.37.refs_6_) | copy-start | bytes 1167364
  23.6 4.7 %copy-start.6 = (bf16[16,4096]{1,0:T(8,128)(2,1)S(1)}, bf16[16,4096]{1,0:T(8,128)(2,1)}, u32[]{:S(2)}) copy-start(bf16[16,4096]{1,0:T(8,128)(2,1)} %copy-done.5) | copy-start | bytes 393220
  35.0 22.1 %copy-start.3 = (bf16[608,320]{1,0:T(8,128)(2,1)S(1)}, bf16[608,320]{1,0:T(8,128)(2,1)}, u32[]{:S(2)}) copy-start(bf16[608,320]{1,0:T(8,128)(2,1)} %get-tuple-element.48.refs_6_) | copy-start | bytes 1167364
  35.0 10.0 %collective-permute-start.9 = (bf16[16,4096]{1,0:T(8,128)(2,1)S(1)}, bf16[16,4096]{1,0:T(8,128)(2,1)S(1)}, u32[]{:S(2)}, u32[]{:S(2)}) collective-permute-start(bf16[16,4096]{1,0:T(8,128)(2,1)S(1)} %get-tuple-element.42), channel_id=1, source_target_pairs={{0,2},{1,3},{2,4},{3,5},{4,6},{5,7},{6,8},{7,9},{8,10},{9,11},{10,... | collective-permute-start | bytes 393224 | tf_op jit(solution)/shard_map/ppermute | solution.py:27
  35.0 15.8 %collective-permute-start.8 = (bf16[32,4096]{1,0:T(8,128)(2,1)S(1)}, bf16[32,4096]{1,0:T(8,128)(2,1)S(1)}, u32[]{:S(2)}, u32[]{:S(2)}) collective-permute-start(bf16[32,4096]{1,0:T(8,128)(2,1)S(1)} %get-tuple-element.39), channel_id=1, source_target_pairs={{0,1},{1,2},{2,3},{3,4},{4,5},{5,6},{6,7},{7,8},{8,9},{9,10},{10,1... | collective-permute-start | bytes 786440 | tf_op jit(solution)/shard_map/ppermute | solution.py:27
  38.6 6.4 %collective-permute-start.11 = (bf16[16,4096]{1,0:T(8,128)(2,1)S(1)}, bf16[16,4096]{1,0:T(8,128)(2,1)S(1)}, u32[]{:S(2)}, u32[]{:S(2)}) collective-permute-start(bf16[16,4096]{1,0:T(8,128)(2,1)S(1)} %get-tuple-element.44), channel_id=1, source_target_pairs={{0,12},{1,13},{2,14},{3,15},{4,0},{5,1},{6,2},{7,3},{8,20},{9,21},... | collective-permute-start | bytes 393224 | tf_op jit(solution)/shard_map/ppermute | solution.py:199
  39.7 8.3 %collective-permute-start.14 = (bf16[16,4096]{1,0:T(8,128)(2,1)S(1)}, bf16[16,4096]{1,0:T(8,128)(2,1)S(1)}, u32[]{:S(2)}, u32[]{:S(2)}) collective-permute-start(bf16[16,4096]{1,0:T(8,128)(2,1)S(1)} %get-tuple-element.47), channel_id=1, source_target_pairs={{0,48},{1,49},{2,50},{3,51},{4,52},{5,53},{6,54},{7,55},{8,56},{9,... | collective-permute-start | bytes 393224 | tf_op jit(solution)/shard_map/ppermute | solution.py:27
  42.8 10.1 %collective-permute-start.10 = (bf16[16,4096]{1,0:T(8,128)(2,1)S(1)}, bf16[16,4096]{1,0:T(8,128)(2,1)S(1)}, u32[]{:S(2)}, u32[]{:S(2)}) collective-permute-start(bf16[16,4096]{1,0:T(8,128)(2,1)S(1)} %get-tuple-element.43), channel_id=1, source_target_pairs={{0,4},{1,5},{2,6},{3,7},{4,8},{5,9},{6,10},{7,11},{8,12},{9,13},{1... | collective-permute-start | bytes 393224 | tf_op jit(solution)/shard_map/ppermute | solution.py:27
  45.0 7.8 %collective-permute-start.13 = (bf16[16,4096]{1,0:T(8,128)(2,1)S(1)}, bf16[16,4096]{1,0:T(8,128)(2,1)S(1)}, u32[]{:S(2)}, u32[]{:S(2)}) collective-permute-start(bf16[16,4096]{1,0:T(8,128)(2,1)S(1)} %get-tuple-element.46), channel_id=1, source_target_pairs={{0,16},{1,17},{2,18},{3,19},{4,20},{5,21},{6,22},{7,23},{8,24},{9,... | collective-permute-start | bytes 393224 | tf_op jit(solution)/shard_map/ppermute | solution.py:27
  45.0 12.0 %collective-permute-start.12 = (bf16[16,4096]{1,0:T(8,128)(2,1)S(1)}, bf16[16,4096]{1,0:T(8,128)(2,1)S(1)}, u32[]{:S(2)}, u32[]{:S(2)}) collective-permute-start(bf16[16,4096]{1,0:T(8,128)(2,1)S(1)} %collective-permute-done.11), channel_id=1, source_target_pairs={{12,8},{13,9},{14,10},{15,11},{0,12},{1,13},{2,14},{3,15},{20,16},... | collective-permute-start | bytes 393224 | tf_op jit(solution)/shard_map/ppermute | solution.py:199
  48.0 9.0 %collective-permute-start.15 = (bf16[16,4096]{1,0:T(8,128)(2,1)S(1)}, bf16[16,4096]{1,0:T(8,128)(2,1)S(1)}, u32[]{:S(2)}, u32[]{:S(2)}) collective-permute-start(bf16[16,4096]{1,0:T(8,128)(2,1)S(1)} %collective-permute-done.14), channel_id=1, source_target_pairs={{0,48},{1,49},{2,50},{3,51},{4,52},{5,53},{6,54},{7,55},{8,56},{9,... | collective-permute-start | bytes 393224 | tf_op jit(solution)/shard_map/ppermute | solution.py:27

commit v5 on v4

--- a/solution.py
+++ b/solution.py
@@ -72,13 +72,13 @@
 
 
 def first_kernel(short_count, tokens, *refs):
-    pair, far = refs[0], refs[1:6]
-    tail, sems = refs[6], refs[7:]
+    pair, duo, far = refs[0], refs[1], refs[2:5]
+    tail, sems = refs[5], refs[6:]
     near_rows, half_rows = tail.shape
     local_rows = pair.shape[1]
     base = local_rows - half_rows
     copies = [pltpu.make_async_copy(tokens.at[:near_rows, base:], tail, sems[0])]
-    for at, target in enumerate([pair.at[TRACK_CH:, :], *far]):
+    for at, target in enumerate([pair.at[TRACK_CH:, :], duo.at[:TRACK_CH, :], duo.at[TRACK_CH:, :], *far]):
         top = near_rows + at * TRACK_CH
         copies.append(
             pltpu.make_async_copy(tokens.at[top : top + TRACK_CH, :], target, sems[1 + at])
@@ -152,7 +152,7 @@
     for begin in range(0, local_rows, TILE):
         end = begin + TILE
         parts = [pair[TRACK_CH:, begin:end].astype(F32)]
-        parts += [ref[:, begin:end].astype(F32) for ref in far]
+        parts += [ref[:TRACK_CH, begin:end].astype(F32) for ref in far]
         total = squares[:, begin:end]
         for part in parts:
             total = total + (part[:8] * part[:8] + part[8:] * part[8:])
@@ -169,9 +169,10 @@
         else:
             outs[0][:, begin:end] = mixed[:near_rows]
             outs[1][TRACK_CH:, begin:end] = mixed[near_rows : near_rows + TRACK_CH]
-            for at in range(len(far)):
-                top = near_rows + (1 + at) * TRACK_CH
-                outs[2 + at][:, begin:end] = mixed[top : top + TRACK_CH]
+            outs[2][:, begin:end] = mixed[near_rows + TRACK_CH : near_rows + 3 * TRACK_CH]
+            for at in range(3):
+                top = near_rows + (3 + at) * TRACK_CH
+                outs[3 + at][:, begin:end] = mixed[top : top + TRACK_CH]
     if not last:
 
         def track(t, begin, end):
@@ -211,18 +212,18 @@
     return first, second
 
 
-def exchange(pair, far):
-    two, four, eight, sixteen, thirty_two = far
+def exchange(pair, duo, far):
+    eight, sixteen, thirty_two = far
     to_middle, from_middle = routes()
     eight = permuted(eight, to_middle)
+    duo = shifted(duo, "seq", 2)
     pair = shifted(pair, "seq", 1)
     back = shifted(thirty_two, "seq", -16)
-    four = shifted(four, "seq", 4)
-    two = shifted(two, "seq", 2)
+    sixteen = shifted(sixteen, "seq", 16)
+    four = shifted(after(duo[TRACK_CH:], eight), "seq", 2)
+    back = shifted(after(back, duo), "seq", -16)
     eight = permuted(eight, from_middle)
-    back = shifted(back, "seq", -16)
-    sixteen = shifted(after(sixteen, two), "seq", 16)
-    return pair, [two, four, eight, sixteen, back]
+    return pair, [duo, four, eight, sixteen, back]
 
 
 def shards(tokens, norm_gain, in_weight, in_bias, out_weight, out_bias):
@@ -236,11 +237,11 @@
     near_shape = jax.ShapeDtypeStruct((near_rows, local_rows), BF16)
     squares_shape = jax.ShapeDtypeStruct((8, local_rows), F32)
     whole = pl.BlockSpec(memory_space=pl.ANY)
-    pair, *far = pl.pallas_call(
+    pair, duo, *far = pl.pallas_call(
         functools.partial(first_kernel, short_count),
-        out_shape=[two] + [one] * far_count,
+        out_shape=[two] * 2 + [one] * (far_count - 2),
         in_specs=[pl.BlockSpec(memory_space=pl.ANY)],
-        out_specs=[VMEM] * (1 + far_count),
+        out_specs=[VMEM] * far_count,
         scratch_shapes=[pltpu.VMEM((near_rows, local_rows // 2), BF16)]
         + [pltpu.SemaphoreType.DMA] * (2 + far_count),
         name="first",
@@ -257,13 +258,13 @@
     near = tokens
     for block_no in range(BLOCKS):
         last = block_no == BLOCKS - 1
-        pair, moved = exchange(pair, far)
+        pair, moved = exchange(pair, duo, far)
         rotated, squares = call(
             functools.partial(near_kernel, short_count), [near_shape, squares_shape], [VMEM] * 2, "near", 8
         )(near, pair)
         out_shape = [jax.ShapeDtypeStruct((width, local_rows), BF16)]
         if not last:
-            out_shape = [near_shape, two] + [one] * far_count
+            out_shape = [near_shape, two, two] + [one] * (far_count - 2)
         outs = call(
             functools.partial(main_kernel, short_count, block_no, last),
             out_shape,
@@ -273,7 +274,7 @@
         )(rotated, squares, pair, *moved, columns, w_ins[block_no], out_weight)
         if last:
             return outs[0]
-        near, pair, far = outs[0], outs[1], outs[2:]
+        near, pair, duo, far = outs[0], outs[1], outs[2], outs[3:]
 
 
 def solution(mesh):

time: 64.1 us -> 64.8 us (1.011)
  the two profiles are of different devices: /device:TPU:34 before, /device:TPU:2 now
where the time goes in v5:
time: 64.8 us; the launch traced here: 64.7 us
  starting transfers between devices  35.6 us (55%)
  Pallas kernels  19.9 us (31%)
  waiting for transfers between devices  8.34 us (13%)
  local copies, waits for them, and re-layouts  0.74 us (1%)
    ppermute x12, starting transfers between devices, shifted(): return lax.ppermute(value, axis, pairs)  21.4 us
    ppermute x4, starting transfers between devices, permuted(): return lax.ppermute(value, 'seq', moves)  14.1 us
    pallas_call x2, Pallas kernels, shards(): call(functools.partial(main_kernel, short_count, block_no, last), out_sha...  13.6 us
    ppermute x12, waiting for transfers between devices, shifted(): return lax.ppermute(value, axis, pairs)  7.19 us
    pallas_call x1, Pallas kernels, shards(): pl.pallas_call(functools.partial(first_kernel, short_count), out_shape=[t...  2.5 us
    pallas_call x1, Pallas kernels, shards(): pl.pallas_call(weight_kernel, out_shape=[jax.ShapeDtypeStruct(*entry) for...  2.41 us
    pallas_call x2, Pallas kernels, shards(): call(functools.partial(near_kernel, short_count), [near_shape, squares_sh...  1.33 us
  transfers between devices with their start and end apart: 16, of which 5 were waited for; matrix products, arithmetic and copies ran while one was open for 1% of the time, Pallas kernels for 6%

profile of v5, /device:TPU:2, one launch (start us, length us, event | category | flops | bytes accessed | tf_op | source)
XLA Modules:
  0.0 64.7 jit_solution(15136982383071783458)
XLA Ops:
  0.0 2.5 %first.1 = (bf16[32,4096]{1,0:T(8,128)(2,1)}, bf16[32,4096]{1,0:T(8,128)(2,1)}, bf16[16,4096]{1,0:T(8,128)(2,1)}, bf16[16,4096]{1,0:T(8,128)(2,1)}, bf16[16,4096]{1,0:T(8,128)(2,1)}) custom-call(bf16[304,4096]{1,0:T(8,128)(2,1)} %near.4), custom_call_target="tpu_custom_call" | custom-call | tf_op jit(solution)/shard_map/first/pallas_call | solution.py:240
  2.5 2.0 %collective-permute-start.1 = (bf16[32,4096]{1,0:T(8,128)(2,1)}, bf16[32,4096]{1,0:T(8,128)(2,1)S(1)}, u32[]{:S(2)}, u32[]{:S(2)}) collective-permute-start(bf16[32,4096]{1,0:T(8,128)(2,1)} %get-tuple-element.30), channel_id=1, source_target_pairs={{0,2},{1,3},{2,4},{3,5},{4,6},{5,7},{6,8},{7,9},{8,10},{9,11},{10,... | collective-permute-start | bytes 786440 | tf_op jit(solution)/shard_map/ppermute | solution.py:27
  4.5 5.4 %collective-permute-start.2 = (bf16[16,4096]{1,0:T(8,128)(2,1)}, bf16[16,4096]{1,0:T(8,128)(2,1)}, u32[]{:S(2)}, u32[]{:S(2)}) collective-permute-start(bf16[16,4096]{1,0:T(8,128)(2,1)} %get-tuple-element.31), channel_id=1, source_target_pairs={{0,12},{1,13},{2,14},{3,15},{4,0},{5,1},{6,2},{7,3},{8,20},{9,21},... | collective-permute-start | bytes 393224 | tf_op jit(solution)/shard_map/ppermute | solution.py:200
  9.9 3.0 %collective-permute-start.6 = (bf16[16,4096]{1,0:T(8,128)(2,1)}, bf16[16,4096]{1,0:T(8,128)(2,1)}, u32[]{:S(2)}, u32[]{:S(2)}) collective-permute-start(bf16[16,4096]{1,0:T(8,128)(2,1)} %get-tuple-element.34), channel_id=1, source_target_pairs={{0,48},{1,49},{2,50},{3,51},{4,52},{5,53},{6,54},{7,55},{8,56},{9,... | collective-permute-start | bytes 393224 | tf_op jit(solution)/shard_map/ppermute | solution.py:27
  12.9 2.1 %collective-permute-start = (bf16[32,4096]{1,0:T(8,128)(2,1)}, bf16[32,4096]{1,0:T(8,128)(2,1)S(1)}, u32[]{:S(2)}, u32[]{:S(2)}) collective-permute-start(bf16[32,4096]{1,0:T(8,128)(2,1)} %get-tuple-element.27), channel_id=1, source_target_pairs={{0,1},{1,2},{2,3},{3,4},{4,5},{5,6},{6,7},{7,8},{8,9},{9,10},{10,1... | collective-permute-start | bytes 786440 | tf_op jit(solution)/shard_map/ppermute | solution.py:27
  15.1 0.4 collective-permute-done.2
  15.5 4.6 %collective-permute-start.4 = (bf16[16,4096]{1,0:T(8,128)(2,1)}, bf16[16,4096]{1,0:T(8,128)(2,1)}, u32[]{:S(2)}, u32[]{:S(2)}) collective-permute-start(bf16[16,4096]{1,0:T(8,128)(2,1)} %collective-permute-done.2), channel_id=1, source_target_pairs={{12,8},{13,9},{14,10},{15,11},{0,12},{1,13},{2,14},{3,15},{20,16},... | collective-permute-start | bytes 393224 | tf_op jit(solution)/shard_map/ppermute | solution.py:200
  20.1 0.7 %slice.8 = bf16[16,4096]{1,0:T(8,128)(2,1)} slice(bf16[32,4096]{1,0:T(8,128)(2,1)S(1)} %collective-permute-done.1.refs_0_), slice={[16:32], [0:4096]} | slice | bytes 262144 | tf_op jit(solution)/shard_map/slice | solution.py:223
  20.8 3.1 %collective-permute-start.7 = (bf16[16,4096]{1,0:T(8,128)(2,1)}, bf16[16,4096]{1,0:T(8,128)(2,1)}, u32[]{:S(2)}, u32[]{:S(2)}) collective-permute-start(bf16[16,4096]{1,0:T(8,128)(2,1)} %collective-permute-done.6), channel_id=1, source_target_pairs={{0,48},{1,49},{2,50},{3,51},{4,52},{5,53},{6,54},{7,55},{8,56},{9,... | collective-permute-start | bytes 393224 | tf_op jit(solution)/shard_map/ppermute | solution.py:27
  23.9 2.4 %weights.1 = (bf16[608,320]{1,0:T(8,128)(2,1)}, bf16[608,320]{1,0:T(8,128)(2,1)}, f32[304,8]{1,0:T(8,128)}) custom-call(bf16[2,304,608]{2,1,0:T(8,128)(2,1)} %bitcast.1, f32[2,608]{1,0:T(2,128)} %bias.1, f32[2,304]{1,0:T(2,128)} %gain.1, f32[2,304]{1,0:T(2,128)} %last_bias.1), custom_call_target="tpu_custom_call" | custom-call | tf_op jit(solution)/shard_map/weights/pallas_call | solution.py:250
  26.3 0.7 %near.3 = (bf16[208,4096]{1,0:T(8,128)(2,1)S(1)}, f32[8,4096]{1,0:T(8,128)S(1)}) custom-call(bf16[304,4096]{1,0:T(8,128)(2,1)S(1)} %copy-done, bf16[32,4096]{1,0:T(8,128)(2,1)S(1)} %collective-permute-done.halo_in.pair), custom_call_target="tpu_custom_call" | custom-call | flops 1 | bytes 1 | tf_op jit(solution)/shard_map/near/pallas_call | solution.py:262
  27.0 3.0 %collective-permute-done.5.refs_3_ = bf16[16,4096]{1,0:T(8,128)(2,1)} collective-permute-done((bf16[16,4096]{1,0:T(8,128)(2,1)}, bf16[16,4096]{1,0:T(8,128)(2,1)}, u32[]{:S(2)}, u32[]{:S(2)}) %collective-permute-start.5) | collective-permute-done | bytes 131104 | tf_op jit(solution)/shard_map/ppermute | solution.py:27
  30.0 6.7 %main.2 = (bf16[208,4096]{1,0:T(8,128)(2,1)S(1)}, bf16[32,4096]{1,0:T(8,128)(2,1)S(1)}, bf16[32,4096]{1,0:T(8,128)(2,1)S(1)}, bf16[16,4096]{1,0:T(8,128)(2,1)S(1...) custom-call(bf16[208,4096]{1,0:T(8,128)(2,1)S(1)} %get-tuple-element.28.near, ...), custom_call_target="tpu_custom_call" | custom-call | flops 1 | bytes 1 | tf_op jit(solution)/shard_map/main/pallas_call | solution.py:268
  36.8 1.8 %collective-permute-start.10 = (bf16[16,4096]{1,0:T(8,128)(2,1)S(1)}, bf16[16,4096]{1,0:T(8,128)(2,1)S(1)}, u32[]{:S(2)}, u32[]{:S(2)}) collective-permute-start(bf16[16,4096]{1,0:T(8,128)(2,1)S(1)} %get-tuple-element.43), channel_id=1, source_target_pairs={{0,12},{1,13},{2,14},{3,15},{4,0},{5,1},{6,2},{7,3},{8,20},{9,21},... | collective-permute-start | bytes 393224 | tf_op jit(solution)/shard_map/ppermute | solution.py:200
  38.6 2.8 %collective-permute-start.14 = (bf16[16,4096]{1,0:T(8,128)(2,1)S(1)}, bf16[16,4096]{1,0:T(8,128)(2,1)S(1)}, u32[]{:S(2)}, u32[]{:S(2)}) collective-permute-start(bf16[16,4096]{1,0:T(8,128)(2,1)S(1)} %get-tuple-element.46), channel_id=1, source_target_pairs={{0,48},{1,49},{2,50},{3,51},{4,52},{5,53},{6,54},{7,55},{8,56},{9,... | collective-permute-start | bytes 393224 | tf_op jit(solution)/shard_map/ppermute | solution.py:27
  41.4 2.1 %collective-permute-start.8 = (bf16[32,4096]{1,0:T(8,128)(2,1)S(1)}, bf16[32,4096]{1,0:T(8,128)(2,1)S(1)}, u32[]{:S(2)}, u32[]{:S(2)}) collective-permute-start(bf16[32,4096]{1,0:T(8,128)(2,1)S(1)} %get-tuple-element.39), channel_id=1, source_target_pairs={{0,1},{1,2},{2,3},{3,4},{4,5},{5,6},{6,7},{7,8},{8,9},{9,10},{10,1... | collective-permute-start | bytes 786440 | tf_op jit(solution)/shard_map/ppermute | solution.py:27
  43.6 0.7 %collective-permute-done.10 = bf16[16,4096]{1,0:T(8,128)(2,1)S(1)} collective-permute-done((bf16[16,4096]{1,0:T(8,128)(2,1)S(1)}, bf16[16,4096]{1,0:T(8,128)(2,1)S(1)}, u32[]{:S(2)}, u32[]{:S(2)}) %collective-permute-start.10) | collective-permute-done | bytes 131104 | tf_op jit(solution)/shard_map/ppermute | solution.py:200
  44.3 2.3 %collective-permute-start.12 = (bf16[16,4096]{1,0:T(8,128)(2,1)S(1)}, bf16[16,4096]{1,0:T(8,128)(2,1)S(1)}, u32[]{:S(2)}, u32[]{:S(2)}) collective-permute-start(bf16[16,4096]{1,0:T(8,128)(2,1)S(1)} %collective-permute-done.10), channel_id=1, source_target_pairs={{12,8},{13,9},{14,10},{15,11},{0,12},{1,13},{2,14},{3,15},{20,16},... | collective-permute-start | bytes 393224 | tf_op jit(solution)/shard_map/ppermute | solution.py:200
  46.6 4.9 %collective-permute-start.11 = (bf16[16,4096]{1,0:T(8,128)(2,1)S(1)}, bf16[16,4096]{1,0:T(8,128)(2,1)S(1)}, u32[]{:S(2)}, u32[]{:S(2)}) collective-permute-start(bf16[16,4096]{1,0:T(8,128)(2,1)S(1)} %slice.9), channel_id=1, source_target_pairs={{0,2},{1,3},{2,4},{3,5},{4,6},{5,7},{6,8},{7,9},{8,10},{9,11},{10,... | collective-permute-start | bytes 393224 | tf_op jit(solution)/shard_map/ppermute | solution.py:27
  51.5 1.3 %collective-permute-start.15 = (bf16[16,4096]{1,0:T(8,128)(2,1)S(1)}, bf16[16,4096]{1,0:T(8,128)(2,1)S(1)}, u32[]{:S(2)}, u32[]{:S(2)}) collective-permute-start(bf16[16,4096]{1,0:T(8,128)(2,1)S(1)} %collective-permute-done.14), channel_id=1, source_target_pairs={{0,48},{1,49},{2,50},{3,51},{4,52},{5,53},{6,54},{7,55},{8,56},{9,... | collective-permute-start | bytes 393224 | tf_op jit(solution)/shard_map/ppermute | solution.py:27
  52.8 3.1 %collective-permute-done.8.halo_in.pair = bf16[32,4096]{1,0:T(8,128)(2,1)S(1)} collective-permute-done((bf16[32,4096]{1,0:T(8,128)(2,1)S(1)}, bf16[32,4096]{1,0:T(8,128)(2,1)S(1)}, u32[]{:S(2)}, u32[]{:S(2)}) %collective-permute-start.8) | collective-permute-done | bytes 262176 | tf_op jit(solution)/shard_map/ppermute | solution.py:27
  56.0 0.7 %near.5 = (bf16[208,4096]{1,0:T(8,128)(2,1)S(1)}, f32[8,4096]{1,0:T(8,128)S(1)}) custom-call(bf16[208,4096]{1,0:T(8,128)(2,1)S(1)} %get-tuple-element.38.near, bf16[32,4096]{1,0:T(8,128)(2,1)S(1)} %collective-permute-done.8.halo_in.pair), custom_call_target="tpu_custom_call" | custom-call | flops 1 | bytes 1 | tf_op jit(solution)/shard_map/near/pallas_call | solution.py:262
  56.7 1.1 %collective-permute-done.13.refs_3_ = bf16[16,4096]{1,0:T(8,128)(2,1)S(1)} collective-permute-done((bf16[16,4096]{1,0:T(8,128)(2,1)S(1)}, bf16[16,4096]{1,0:T(8,128)(2,1)S(1)}, u32[]{:S(2)}, u32[]{:S(2)}) %collective-permute-start.13) | collective-permute-done | bytes 131104 | tf_op jit(solution)/shard_map/ppermute | solution.py:27
  57.7 7.0 %main.3 = bf16[304,4096]{1,0:T(8,128)(2,1)} custom-call(bf16[208,4096]{1,0:T(8,128)(2,1)S(1)} %get-tuple-element.40.near, f32[8,4096]{1,0:T(8,128)S(1)} %get-tuple-element.41.squares, bf16[32,4096]{1,0:T(8,128)(2,1)S(1)} %collective-permute-done.8.halo_in.pair, bf16[32,4096]{1,0:T(8,128)(2,1)S(1)} %collective-permute-done.9.refs_0_, ...), custom_call_target="tpu_custom_call" | custom-call | flops 1 | bytes 1 | tf_op jit(solution)/shard_map/main/pallas_call | solution.py:268
  (30 shorter events, 0.2 us)
Async XLA Ops:
  0.0 26.3 %copy-start = (bf16[304,4096]{1,0:T(8,128)(2,1)S(1)}, bf16[304,4096]{1,0:T(8,128)(2,1)}, u32[]{:S(2)}) copy-start(bf16[304,4096]{1,0:T(8,128)(2,1)} %near.4) | copy-start | bytes 7471108
  2.5 17.6 %collective-permute-start.1 = (bf16[32,4096]{1,0:T(8,128)(2,1)}, bf16[32,4096]{1,0:T(8,128)(2,1)S(1)}, u32[]{:S(2)}, u32[]{:S(2)}) collective-permute-start(bf16[32,4096]{1,0:T(8,128)(2,1)} %get-tuple-element.30), channel_id=1, source_target_pairs={{0,2},{1,3},{2,4},{3,5},{4,6},{5,7},{6,8},{7,9},{8,10},{9,11},{10,... | collective-permute-start | bytes 786440 | tf_op jit(solution)/shard_map/ppermute | solution.py:27
  4.5 11.0 %collective-permute-start.2 = (bf16[16,4096]{1,0:T(8,128)(2,1)}, bf16[16,4096]{1,0:T(8,128)(2,1)}, u32[]{:S(2)}, u32[]{:S(2)}) collective-permute-start(bf16[16,4096]{1,0:T(8,128)(2,1)} %get-tuple-element.31), channel_id=1, source_target_pairs={{0,12},{1,13},{2,14},{3,15},{4,0},{5,1},{6,2},{7,3},{8,20},{9,21},... | collective-permute-start | bytes 393224 | tf_op jit(solution)/shard_map/ppermute | solution.py:200
  9.9 10.2 %collective-permute-start.6 = (bf16[16,4096]{1,0:T(8,128)(2,1)}, bf16[16,4096]{1,0:T(8,128)(2,1)}, u32[]{:S(2)}, u32[]{:S(2)}) collective-permute-start(bf16[16,4096]{1,0:T(8,128)(2,1)} %get-tuple-element.34), channel_id=1, source_target_pairs={{0,48},{1,49},{2,50},{3,51},{4,52},{5,53},{6,54},{7,55},{8,56},{9,... | collective-permute-start | bytes 393224 | tf_op jit(solution)/shard_map/ppermute | solution.py:27
  12.9 13.4 %collective-permute-start = (bf16[32,4096]{1,0:T(8,128)(2,1)}, bf16[32,4096]{1,0:T(8,128)(2,1)S(1)}, u32[]{:S(2)}, u32[]{:S(2)}) collective-permute-start(bf16[32,4096]{1,0:T(8,128)(2,1)} %get-tuple-element.27), channel_id=1, source_target_pairs={{0,1},{1,2},{2,3},{3,4},{4,5},{5,6},{6,7},{7,8},{8,9},{9,10},{10,1... | collective-permute-start | bytes 786440 | tf_op jit(solution)/shard_map/ppermute | solution.py:27
  15.0 14.9 %collective-permute-start.5 = (bf16[16,4096]{1,0:T(8,128)(2,1)}, bf16[16,4096]{1,0:T(8,128)(2,1)}, u32[]{:S(2)}, u32[]{:S(2)}) collective-permute-start(bf16[16,4096]{1,0:T(8,128)(2,1)} %get-tuple-element.33), channel_id=1, source_target_pairs={{0,16},{1,17},{2,18},{3,19},{4,20},{5,21},{6,22},{7,23},{8,24},{9,... | collective-permute-start | bytes 393224 | tf_op jit(solution)/shard_map/ppermute | solution.py:27
  15.5 14.5 %collective-permute-start.4 = (bf16[16,4096]{1,0:T(8,128)(2,1)}, bf16[16,4096]{1,0:T(8,128)(2,1)}, u32[]{:S(2)}, u32[]{:S(2)}) collective-permute-start(bf16[16,4096]{1,0:T(8,128)(2,1)} %collective-permute-done.2), channel_id=1, source_target_pairs={{12,8},{13,9},{14,10},{15,11},{0,12},{1,13},{2,14},{3,15},{20,16},... | collective-permute-start | bytes 393224 | tf_op jit(solution)/shard_map/ppermute | solution.py:200
  20.1 3.8 %copy-start.3 = (bf16[32,4096]{1,0:T(8,128)(2,1)}, bf16[32,4096]{1,0:T(8,128)(2,1)S(1)}, u32[]{:S(2)}) copy-start(bf16[32,4096]{1,0:T(8,128)(2,1)S(1)} %collective-permute-done.1.refs_0_) | copy-start | bytes 786436
  20.8 9.2 %collective-permute-start.3 = (bf16[16,4096]{1,0:T(8,128)(2,1)}, bf16[16,4096]{1,0:T(8,128)(2,1)}, u32[]{:S(2)}, u32[]{:S(2)}) collective-permute-start(bf16[16,4096]{1,0:T(8,128)(2,1)} %slice.8), channel_id=1, source_target_pairs={{0,2},{1,3},{2,4},{3,5},{4,6},{5,7},{6,8},{7,9},{8,10},{9,11},{10,... | collective-permute-start | bytes 393224 | tf_op jit(solution)/shard_map/ppermute | solution.py:27
  20.8 9.2 %collective-permute-start.7 = (bf16[16,4096]{1,0:T(8,128)(2,1)}, bf16[16,4096]{1,0:T(8,128)(2,1)}, u32[]{:S(2)}, u32[]{:S(2)}) collective-permute-start(bf16[16,4096]{1,0:T(8,128)(2,1)} %collective-permute-done.6), channel_id=1, source_target_pairs={{0,48},{1,49},{2,50},{3,51},{4,52},{5,53},{6,54},{7,55},{8,56},{9,... | collective-permute-start | bytes 393224 | tf_op jit(solution)/shard_map/ppermute | solution.py:27
  23.9 6.1 %copy-start.1 = (bf16[2,304,608]{2,1,0:T(8,128)(2,1)S(1)}, bf16[2,304,608]{2,1,0:T(8,128)(2,1)}, u32[]{:S(2)}) copy-start(bf16[2,304,608]{2,1,0:T(8,128)(2,1)} %refs_7_.3) | copy-start | bytes 2217988
  26.3 3.7 %copy-start.2 = (f32[304,8]{1,0:T(8,128)S(1)}, f32[304,8]{1,0:T(8,128)}, u32[]{:S(2)}) copy-start(f32[304,8]{1,0:T(8,128)} %get-tuple-element.36.refs_5_) | copy-start | bytes 29188
  26.3 3.7 %copy-start.4 = (bf16[32,4096]{1,0:T(8,128)(2,1)S(1)}, bf16[32,4096]{1,0:T(8,128)(2,1)}, u32[]{:S(2)}) copy-start(bf16[32,4096]{1,0:T(8,128)(2,1)} %copy-done.3) | copy-start | bytes 786436
  26.3 3.7 %copy-start.6 = (bf16[608,320]{1,0:T(8,128)(2,1)S(1)}, bf16[608,320]{1,0:T(8,128)(2,1)}, u32[]{:S(2)}) copy-start(bf16[608,320]{1,0:T(8,128)(2,1)} %get-tuple-element.37.refs_6_) | copy-start | bytes 1167364
  36.7 21.0 %copy-start.5 = (bf16[608,320]{1,0:T(8,128)(2,1)S(1)}, bf16[608,320]{1,0:T(8,128)(2,1)}, u32[]{:S(2)}) copy-start(bf16[608,320]{1,0:T(8,128)(2,1)} %get-tuple-element.48.refs_6_) | copy-start | bytes 1167364
  36.7 9.9 %collective-permute-start.9 = (bf16[32,4096]{1,0:T(8,128)(2,1)S(1)}, bf16[32,4096]{1,0:T(8,128)(2,1)S(1)}, u32[]{:S(2)}, u32[]{:S(2)}) collective-permute-start(bf16[32,4096]{1,0:T(8,128)(2,1)S(1)} %get-tuple-element.42), channel_id=1, source_target_pairs={{0,2},{1,3},{2,4},{3,5},{4,6},{5,7},{6,8},{7,9},{8,10},{9,11},{10,... | collective-permute-start | bytes 786440 | tf_op jit(solution)/shard_map/ppermute | solution.py:27
  36.8 7.5 %collective-permute-start.10 = (bf16[16,4096]{1,0:T(8,128)(2,1)S(1)}, bf16[16,4096]{1,0:T(8,128)(2,1)S(1)}, u32[]{:S(2)}, u32[]{:S(2)}) collective-permute-start(bf16[16,4096]{1,0:T(8,128)(2,1)S(1)} %get-tuple-element.43), channel_id=1, source_target_pairs={{0,12},{1,13},{2,14},{3,15},{4,0},{5,1},{6,2},{7,3},{8,20},{9,21},... | collective-permute-start | bytes 393224 | tf_op jit(solution)/shard_map/ppermute | solution.py:200
  38.6 8.0 %collective-permute-start.14 = (bf16[16,4096]{1,0:T(8,128)(2,1)S(1)}, bf16[16,4096]{1,0:T(8,128)(2,1)S(1)}, u32[]{:S(2)}, u32[]{:S(2)}) collective-permute-start(bf16[16,4096]{1,0:T(8,128)(2,1)S(1)} %get-tuple-element.46), channel_id=1, source_target_pairs={{0,48},{1,49},{2,50},{3,51},{4,52},{5,53},{6,54},{7,55},{8,56},{9,... | collective-permute-start | bytes 393224 | tf_op jit(solution)/shard_map/ppermute | solution.py:27
  41.4 14.5 %collective-permute-start.8 = (bf16[32,4096]{1,0:T(8,128)(2,1)S(1)}, bf16[32,4096]{1,0:T(8,128)(2,1)S(1)}, u32[]{:S(2)}, u32[]{:S(2)}) collective-permute-start(bf16[32,4096]{1,0:T(8,128)(2,1)S(1)} %get-tuple-element.39), channel_id=1, source_target_pairs={{0,1},{1,2},{2,3},{3,4},{4,5},{5,6},{6,7},{7,8},{8,9},{9,10},{10,1... | collective-permute-start | bytes 786440 | tf_op jit(solution)/shard_map/ppermute | solution.py:27
  43.6 14.1 %collective-permute-start.13 = (bf16[16,4096]{1,0:T(8,128)(2,1)S(1)}, bf16[16,4096]{1,0:T(8,128)(2,1)S(1)}, u32[]{:S(2)}, u32[]{:S(2)}) collective-permute-start(bf16[16,4096]{1,0:T(8,128)(2,1)S(1)} %get-tuple-element.45), channel_id=1, source_target_pairs={{0,16},{1,17},{2,18},{3,19},{4,20},{5,21},{6,22},{7,23},{8,24},{9,... | collective-permute-start | bytes 393224 | tf_op jit(solution)/shard_map/ppermute | solution.py:27
  44.3 13.4 %collective-permute-start.12 = (bf16[16,4096]{1,0:T(8,128)(2,1)S(1)}, bf16[16,4096]{1,0:T(8,128)(2,1)S(1)}, u32[]{:S(2)}, u32[]{:S(2)}) collective-permute-start(bf16[16,4096]{1,0:T(8,128)(2,1)S(1)} %collective-permute-done.10), channel_id=1, source_target_pairs={{12,8},{13,9},{14,10},{15,11},{0,12},{1,13},{2,14},{3,15},{20,16},... | collective-permute-start | bytes 393224 | tf_op jit(solution)/shard_map/ppermute | solution.py:200
  46.6 11.1 %collective-permute-start.11 = (bf16[16,4096]{1,0:T(8,128)(2,1)S(1)}, bf16[16,4096]{1,0:T(8,128)(2,1)S(1)}, u32[]{:S(2)}, u32[]{:S(2)}) collective-permute-start(bf16[16,4096]{1,0:T(8,128)(2,1)S(1)} %slice.9), channel_id=1, source_target_pairs={{0,2},{1,3},{2,4},{3,5},{4,6},{5,7},{6,8},{7,9},{8,10},{9,11},{10,... | collective-permute-start | bytes 393224 | tf_op jit(solution)/shard_map/ppermute | solution.py:27
  51.5 6.2 %collective-permute-start.15 = (bf16[16,4096]{1,0:T(8,128)(2,1)S(1)}, bf16[16,4096]{1,0:T(8,128)(2,1)S(1)}, u32[]{:S(2)}, u32[]{:S(2)}) collective-permute-start(bf16[16,4096]{1,0:T(8,128)(2,1)S(1)} %collective-permute-done.14), channel_id=1, source_target_pairs={{0,48},{1,49},{2,50},{3,51},{4,52},{5,53},{6,54},{7,55},{8,56},{9,... | collective-permute-start | bytes 393224 | tf_op jit(solution)/shard_map/ppermute | solution.py:27

commit v6 on v5

--- a/solution.py
+++ b/solution.py
@@ -99,31 +99,28 @@
 
 
 def weight_kernel(transposed, bias, gain, last_bias, *refs):
-    outs, made, sems = refs[:3], refs[3:6], refs[6:]
+    outs, made, sems = refs[:4], refs[4:8], refs[8:]
     depth, hidden = transposed.shape[1:]
-    row = lax.broadcasted_iota(jnp.int32, (TRACK_CH, hidden), 0)
     copies = []
     for block_no in range(BLOCKS):
-        left = bias[block_no : block_no + 1, :] * ALPHA
-        rows = jnp.zeros((TRACK_CH, hidden), F32)
-        for at in range(3):
-            term = left.astype(BF16).astype(F32)
-            rows = jnp.where(row == at, jnp.broadcast_to(term, rows.shape), rows)
-            left = left - term
-        joined = jnp.concatenate([transposed[block_no], rows.astype(BF16)], 0)
-        made[block_no][...] = jnp.transpose(joined)
+        made[block_no][...] = jnp.transpose(transposed[block_no])
         copies.append(pltpu.make_async_copy(made[block_no], outs[block_no], sems[block_no]))
         copies[-1].start()
     columns = [gain[...], last_bias[...], jnp.zeros((8 - 2 * BLOCKS, depth), F32)]
     made[2][...] = jnp.transpose(jnp.concatenate(columns, 0))
-    copies.append(pltpu.make_async_copy(made[2], outs[2], sems[2]))
-    copies[-1].start()
+    made[3][...] = jnp.transpose(jnp.concatenate([bias[...], jnp.zeros((8 - BLOCKS, hidden), F32)], 0))
+    for at in (2, 3):
+        copies.append(pltpu.make_async_copy(made[at], outs[at], sems[at]))
+        copies[-1].start()
     for copy in copies:
         copy.wait()
 
 
-def near_kernel(short_count, near, halo_in, rotated, squares):
-    local_rows = halo_in.shape[1]
+def near_kernel(short_count, block_no, first, near, columns, w_in, *refs):
+    halo_in = refs[0]
+    rotated, squares, partial = refs[-3:]
+    near_rows, width = rotated.shape
+    gain = columns[:near_rows, block_no : block_no + 1]
 
     def track(t, begin, end):
         return near[t * TRACK_CH : (t + 1) * TRACK_CH, begin:end]
@@ -131,48 +128,58 @@
     def halo(begin, end):
         return halo_in[:TRACK_CH, begin:end]
 
-    for begin in range(0, local_rows, NEAR_TILE):
-        end = begin + NEAR_TILE
+    for at in range(0, width, NEAR_TILE):
+        begin, end = first + at, first + at + NEAR_TILE
         total = jnp.zeros((8, NEAR_TILE), F32)
+        scaled = []
         for t in range(1 + short_count):
+            rows = slice(t * TRACK_CH, (t + 1) * TRACK_CH)
             piece = track(0, begin, end) if t == 0 else rotated_piece(track, halo, t - 1, begin, end)
-            rotated[t * TRACK_CH : (t + 1) * TRACK_CH, begin:end] = piece
+            rotated[rows, at : at + NEAR_TILE] = piece
             piece = piece.astype(F32)
             total = total + (piece[:8] * piece[:8] + piece[8:] * piece[8:])
-        squares[:, begin:end] = total
-
-
-def main_kernel(short_count, block_no, last, near, squares, pair, *refs):
-    far, (columns, w_in, w_out), outs = refs[:5], refs[5:8], refs[8:]
-    near_rows, local_rows = near.shape
+            scaled.append((piece * gain[rows]).astype(BF16))
+        squares[:, at : at + NEAR_TILE] = total
+        partial[:, at : at + NEAR_TILE] = jnp.dot(
+            w_in[:, :near_rows], jnp.concatenate(scaled, 0), preferred_element_type=F32
+        ).astype(BF16)
+
+
+def main_kernel(short_count, block_no, last, *refs):
+    nears, pair, far = refs[:6], refs[6], refs[7:12]
+    (columns, hidden_columns, w_in, w_out), outs = refs[12:16], refs[16:]
+    near_rows, half_rows = nears[0].shape
+    local_rows = pair.shape[1]
     width = near_rows + (1 + len(far)) * TRACK_CH
-    ones = jnp.ones((TRACK_CH, TILE), BF16)
-    gain = columns[:, block_no : block_no + 1]
+    gain = columns[near_rows:, block_no : block_no + 1]
     b_out = columns[:, BLOCKS + block_no : BLOCKS + block_no + 1]
+    b_in = hidden_columns[:, block_no : block_no + 1] * ALPHA
     for begin in range(0, local_rows, TILE):
         end = begin + TILE
+        rotated, squares, partial = nears[:3] if begin < half_rows else nears[3:]
+        here = slice(begin % half_rows, begin % half_rows + TILE)
         parts = [pair[TRACK_CH:, begin:end].astype(F32)]
         parts += [ref[:TRACK_CH, begin:end].astype(F32) for ref in far]
-        total = squares[:, begin:end]
+        total = squares[:, here]
         for part in parts:
             total = total + (part[:8] * part[:8] + part[8:] * part[8:])
         scale = ALPHA * lax.rsqrt(jnp.sum(total, axis=0, keepdims=True) * (1.0 / width) + 1e-06)
-        rotated = jnp.concatenate([near[:, begin:end].astype(F32)] + parts, 0)
-        normed = (rotated * gain * scale).astype(BF16)
-        pre = jnp.dot(w_in[...], jnp.concatenate([normed, ones], 0), preferred_element_type=F32)
+        far_part = jnp.concatenate(parts, 0)
+        pre = jnp.dot(w_in[:, near_rows:], (far_part * gain).astype(BF16), preferred_element_type=F32)
+        pre = (partial[:, here].astype(F32) + pre) * scale + b_in
         inner = pre * (GELU_C + pre * pre)
         active = (pre * (1.0 + jnp.tanh(inner))).astype(BF16)
-        out = jnp.dot(w_out[block_no], active, preferred_element_type=F32)
-        mixed = (rotated + out * (0.5 / ALPHA) + b_out).astype(BF16)
+        out = jnp.dot(w_out[block_no], active, preferred_element_type=F32) * (0.5 / ALPHA) + b_out
+        near_out = (rotated[:, here].astype(F32) + out[:near_rows]).astype(BF16)
+        far_out = (far_part + out[near_rows:]).astype(BF16)
+        outs[0][:near_rows, begin:end] = near_out
         if last:
-            outs[0][:, begin:end] = mixed
+            outs[0][near_rows:, begin:end] = far_out
         else:
-            outs[0][:, begin:end] = mixed[:near_rows]
-            outs[1][TRACK_CH:, begin:end] = mixed[near_rows : near_rows + TRACK_CH]
-            outs[2][:, begin:end] = mixed[near_rows + TRACK_CH : near_rows + 3 * TRACK_CH]
+            outs[1][TRACK_CH:, begin:end] = far_out[:TRACK_CH]
+            outs[2][:, begin:end] = far_out[TRACK_CH : 3 * TRACK_CH]
             for at in range(3):
-                top = near_rows + (3 + at) * TRACK_CH
-                outs[3 + at][:, begin:end] = mixed[top : top + TRACK_CH]
+                outs[3 + at][:, begin:end] = far_out[(3 + at) * TRACK_CH : (4 + at) * TRACK_CH]
     if not last:
 
         def track(t, begin, end):
@@ -212,7 +219,7 @@
     return first, second
 
 
-def exchange(pair, duo, far):
+def exchange(pair, duo, far, fill):
     eight, sixteen, thirty_two = far
     to_middle, from_middle = routes()
     eight = permuted(eight, to_middle)
@@ -222,12 +229,13 @@
     sixteen = shifted(sixteen, "seq", 16)
     four = shifted(after(duo[TRACK_CH:], eight), "seq", 2)
     back = shifted(after(back, duo), "seq", -16)
-    eight = permuted(eight, from_middle)
+    eight = permuted(after(eight, *fill), from_middle)
     return pair, [duo, four, eight, sixteen, back]
 
 
 def shards(tokens, norm_gain, in_weight, in_bias, out_weight, out_bias):
     width, local_rows = tokens.shape
+    half_rows = local_rows // 2
     hidden = in_weight.shape[1]
     short_count = short_tracks(local_rows)
     far_count = TRACKS - 2 - short_count
@@ -235,8 +243,11 @@
     one = jax.ShapeDtypeStruct((TRACK_CH, local_rows), BF16)
     two = jax.ShapeDtypeStruct((2 * TRACK_CH, local_rows), BF16)
     near_shape = jax.ShapeDtypeStruct((near_rows, local_rows), BF16)
-    squares_shape = jax.ShapeDtypeStruct((8, local_rows), F32)
-    whole = pl.BlockSpec(memory_space=pl.ANY)
+    half_shapes = [
+        jax.ShapeDtypeStruct((near_rows, half_rows), BF16),
+        jax.ShapeDtypeStruct((8, half_rows), F32),
+        jax.ShapeDtypeStruct((hidden, half_rows), BF16),
+    ]
     pair, duo, *far = pl.pallas_call(
         functools.partial(first_kernel, short_count),
         out_shape=[two] * 2 + [one] * (far_count - 2),
@@ -246,32 +257,31 @@
         + [pltpu.SemaphoreType.DMA] * (2 + far_count),
         name="first",
     )(tokens)
-    made = [((hidden, width + TRACK_CH), BF16)] * BLOCKS + [((width, 8), F32)]
-    *w_ins, columns = pl.pallas_call(
+    made = [((hidden, width), BF16)] * BLOCKS + [((width, 8), F32), ((hidden, 8), F32)]
+    *w_ins, columns, hidden_columns = pl.pallas_call(
         weight_kernel,
         out_shape=[jax.ShapeDtypeStruct(*entry) for entry in made],
         in_specs=[VMEM] * 4,
-        out_specs=[pl.BlockSpec(memory_space=pltpu.HBM)] * 3,
-        scratch_shapes=[pltpu.VMEM(*entry) for entry in made] + [pltpu.SemaphoreType.DMA] * 3,
+        out_specs=[pl.BlockSpec(memory_space=pltpu.HBM)] * 4,
+        scratch_shapes=[pltpu.VMEM(*entry) for entry in made] + [pltpu.SemaphoreType.DMA] * 4,
         name="weights",
     )(jnp.swapaxes(in_weight, 1, 2), in_bias, norm_gain, out_bias)
     near = tokens
     for block_no in range(BLOCKS):
         last = block_no == BLOCKS - 1
-        pair, moved = exchange(pair, duo, far)
-        rotated, squares = call(
-            functools.partial(near_kernel, short_count), [near_shape, squares_shape], [VMEM] * 2, "near", 8
-        )(near, pair)
+        high = call(
+            functools.partial(near_kernel, short_count, block_no, half_rows), half_shapes, [VMEM] * 3, "high", 8
+        )(near, columns, w_ins[block_no])
+        pair, moved = exchange(pair, duo, far, [columns] if block_no == 0 else high[1:2])
+        low = call(functools.partial(near_kernel, short_count, block_no, 0), half_shapes, [VMEM] * 4, "low", 8)(
+            near, columns, w_ins[block_no], pair
+        )
         out_shape = [jax.ShapeDtypeStruct((width, local_rows), BF16)]
         if not last:
             out_shape = [near_shape, two, two] + [one] * (far_count - 2)
         outs = call(
-            functools.partial(main_kernel, short_count, block_no, last),
-            out_shape,
-            [VMEM] * (6 + far_count),
-            "main",
-            24,
-        )(rotated, squares, pair, *moved, columns, w_ins[block_no], out_weight)
+            functools.partial(main_kernel, short_count, block_no, last), out_shape, [VMEM] * 16, "main", 24
+        )(*low, *high, pair, *moved, columns, hidden_columns, w_ins[block_no], out_weight)
         if last:
             return outs[0]
         near, pair, duo, far = outs[0], outs[1], outs[2], outs[3:]

time: 64.8 us -> 64.8 us (level); the launches traced: 64.7 us -> 63.7 us
  starting transfers between devices: 35.6 us -> 31.6 us
  Pallas kernels: 19.9 us -> 21.7 us
  local copies, waits for them, and re-layouts: 0.74 us -> 1.98 us
    pallas_call x2 -> x4, Pallas kernels: 1.33 us -> 3.94 us  [the longest x2 1.99 us: shards(): call(functools.partial(near_kernel, short_count, block_no, 0), half_shape...]
    ppermute x12, starting transfers between devices: 21.4 us -> 19.1 us  [shifted(): return lax.ppermute(value, axis, pairs)]
    unnamed x14 -> x16, local copies, waits for them, and re-layouts: 0.03 us -> 1.96 us
    ppermute x4, starting transfers between devices: 14.1 us -> 12.5 us  [permuted(): return lax.ppermute(value, 'seq', moves)]
    pallas_call x2, Pallas kernels: 13.6 us -> 12.8 us  [shards(): call(functools.partial(main_kernel, short_count, block_no, last), out_sha...]
    ppermute x4, waiting for transfers between devices: 1.15 us -> 0.32 us  [permuted(): return lax.ppermute(value, 'seq', moves)]
    ppermute x12, waiting for transfers between devices: 7.19 us -> 7.96 us  [shifted(): return lax.ppermute(value, axis, pairs)]
    slice x2, local copies, waits for them, and re-layouts: 0.71 us -> 0.02 us  [exchange(): four = shifted(after(duo[TRACK_CH:], eight), 'seq', 2)]
  transfers between devices with their start and end apart: 16 -> 16, of which waited for: 5 -> 5; matrix products, arithmetic and copies ran while one was open for 1% -> 0% of each run, Pallas kernels for 6% -> 10%
where the time goes in v6:
time: 64.8 us; the launch traced here: 63.7 us
  starting transfers between devices  31.6 us (49%)
  Pallas kernels  21.7 us (33%)
  waiting for transfers between devices  8.28 us (13%)
  local copies, waits for them, and re-layouts  1.98 us (3%)
    ppermute x12, starting transfers between devices, shifted(): return lax.ppermute(value, axis, pairs)  19.1 us
    pallas_call x2, Pallas kernels, shards(): call(functools.partial(main_kernel, short_count, block_no, last), out_sha...  12.8 us
    ppermute x4, starting transfers between devices, permuted(): return lax.ppermute(value, 'seq', moves)  12.5 us
    ppermute x12, waiting for transfers between devices, shifted(): return lax.ppermute(value, axis, pairs)  7.96 us
    pallas_call x1, Pallas kernels, shards(): pl.pallas_call(functools.partial(first_kernel, short_count), out_shape=[t...  2.56 us
    pallas_call x1, Pallas kernels, shards(): pl.pallas_call(weight_kernel, out_shape=[jax.ShapeDtypeStruct(*entry) for...  2.47 us
    pallas_call x2, Pallas kernels, shards(): call(functools.partial(near_kernel, short_count, block_no, 0), half_shape...  1.99 us
    unnamed x16, local copies, waits for them, and re-layouts  1.96 us
  transfers between devices with their start and end apart: 16, of which 5 were waited for; matrix products, arithmetic and copies ran while one was open for 0% of the time, Pallas kernels for 10%

profile of v6, /device:TPU:2, one launch (start us, length us, event | category | flops | bytes accessed | tf_op | source)
XLA Modules:
  0.0 63.7 jit_solution(325440644969343538)
XLA Ops:
  0.0 2.6 %first.1 = (bf16[32,4096]{1,0:T(8,128)(2,1)}, bf16[32,4096]{1,0:T(8,128)(2,1)}, bf16[16,4096]{1,0:T(8,128)(2,1)}, bf16[16,4096]{1,0:T(8,128)(2,1)}, bf16[16,4096]{1,0:T(8,128)(2,1)}) custom-call(bf16[304,4096]{1,0:T(8,128)(2,1)} %near.3), custom_call_target="tpu_custom_call" | custom-call | tf_op jit(solution)/shard_map/first/pallas_call | solution.py:251
  2.6 2.0 %collective-permute-start.1 = (bf16[32,4096]{1,0:T(8,128)(2,1)}, bf16[32,4096]{1,0:T(8,128)(2,1)S(1)}, u32[]{:S(2)}, u32[]{:S(2)}) collective-permute-start(bf16[32,4096]{1,0:T(8,128)(2,1)} %get-tuple-element.47), channel_id=1, source_target_pairs={{0,2},{1,3},{2,4},{3,5},{4,6},{5,7},{6,8},{7,9},{8,10},{9,11},{10,... | collective-permute-start | bytes 786440 | tf_op jit(solution)/shard_map/ppermute | solution.py:27
  4.6 5.4 %collective-permute-start.2 = (bf16[16,4096]{1,0:T(8,128)(2,1)}, bf16[16,4096]{1,0:T(8,128)(2,1)S(1)}, u32[]{:S(2)}, u32[]{:S(2)}) collective-permute-start(bf16[16,4096]{1,0:T(8,128)(2,1)} %get-tuple-element.48), channel_id=1, source_target_pairs={{0,12},{1,13},{2,14},{3,15},{4,0},{5,1},{6,2},{7,3},{8,20},{9,21},... | collective-permute-start | bytes 393224 | tf_op jit(solution)/shard_map/ppermute | solution.py:207
  10.0 3.0 %collective-permute-start.6 = (bf16[16,4096]{1,0:T(8,128)(2,1)}, bf16[16,4096]{1,0:T(8,128)(2,1)S(1)}, u32[]{:S(2)}, u32[]{:S(2)}) collective-permute-start(bf16[16,4096]{1,0:T(8,128)(2,1)} %get-tuple-element.52), channel_id=1, source_target_pairs={{0,48},{1,49},{2,50},{3,51},{4,52},{5,53},{6,54},{7,55},{8,56},{9,... | collective-permute-start | bytes 393224 | tf_op jit(solution)/shard_map/ppermute | solution.py:27
  13.0 2.1 %collective-permute-start = (bf16[32,4096]{1,0:T(8,128)(2,1)}, bf16[32,4096]{1,0:T(8,128)(2,1)S(1)}, u32[]{:S(2)}, u32[]{:S(2)}) collective-permute-start(bf16[32,4096]{1,0:T(8,128)(2,1)} %get-tuple-element.40), channel_id=1, source_target_pairs={{0,1},{1,2},{2,3},{3,4},{4,5},{5,6},{6,7},{7,8},{8,9},{9,10},{10,1... | collective-permute-start | bytes 786440 | tf_op jit(solution)/shard_map/ppermute | solution.py:27
  15.1 2.5 %weights.1 = (bf16[608,304]{1,0:T(8,128)(2,1)}, bf16[608,304]{1,0:T(8,128)(2,1)}, f32[304,8]{1,0:T(8,128)}, f32[608,8]{1,0:T(8,128)}) custom-call(bf16[2,304,608]{2,1,0:T(8,128)(2,1)} %bitcast.1, f32[2,608]{1,0:T(2,128)} %bias.1, f32[2,304]{1,0:T(2,128)} %gain.1, f32[2,304]{1,0:T(2,128)} %last_bias.1), custom_call_target="tpu_custom_call" | custom-call | tf_op jit(solution)/shard_map/weights/pallas_call | solution.py:261
  17.6 2.4 %collective-permute-start.4 = (bf16[16,4096]{1,0:T(8,128)(2,1)S(1)}, bf16[16,4096]{1,0:T(8,128)(2,1)S(1)}, u32[]{:S(2)}, u32[]{:S(2)}) collective-permute-start(bf16[16,4096]{1,0:T(8,128)(2,1)S(1)} %collective-permute-done.2), channel_id=1, source_target_pairs={{12,8},{13,9},{14,10},{15,11},{0,12},{1,13},{2,14},{3,15},{20,16},... | collective-permute-start | bytes 393224 | tf_op jit(solution)/shard_map/ppermute | solution.py:207
  20.3 3.2 %collective-permute-start.7 = (bf16[16,4096]{1,0:T(8,128)(2,1)S(1)}, bf16[16,4096]{1,0:T(8,128)(2,1)S(1)}, u32[]{:S(2)}, u32[]{:S(2)}) collective-permute-start(bf16[16,4096]{1,0:T(8,128)(2,1)S(1)} %collective-permute-done.6), channel_id=1, source_target_pairs={{0,48},{1,49},{2,50},{3,51},{4,52},{5,53},{6,54},{7,55},{8,56},{9,... | collective-permute-start | bytes 393224 | tf_op jit(solution)/shard_map/ppermute | solution.py:27
  24.3 1.0 %copy-done.4 = bf16[608,304]{1,0:T(8,128)(2,1)S(1)} copy-done((bf16[608,304]{1,0:T(8,128)(2,1)S(1)}, bf16[608,304]{1,0:T(8,128)(2,1)}, u32[]{:S(2)}) %copy-start.4) | copy-done | bytes 369688
  25.4 1.0 %high.2 = (bf16[208,2048]{1,0:T(8,128)(2,1)S(1)}, f32[8,2048]{1,0:T(8,128)S(1)}, bf16[608,2048]{1,0:T(8,128)(2,1)S(1)}) custom-call(bf16[304,4096]{1,0:T(8,128)(2,1)S(1)} %copy-done, f32[304,8]{1,0:T(8,128)S(1)} %copy-done.1, bf16[608,304]{1,0:T(8,128)(2,1)S(1)} %copy-done.4), custom_call_target="tpu_custom_call" | custom-call | flops 1 | bytes 1 | tf_op jit(solution)/shard_map/high/pallas_call | solution.py:272
  26.9 1.0 %low.2 = (bf16[208,2048]{1,0:T(8,128)(2,1)S(1)}, f32[8,2048]{1,0:T(8,128)S(1)}, bf16[608,2048]{1,0:T(8,128)(2,1)S(1)}) custom-call(bf16[304,4096]{1,0:T(8,128)(2,1)S(1)} %copy-done, f32[304,8]{1,0:T(8,128)S(1)} %copy-done.1, bf16[608,304]{1,0:T(8,128)(2,1)S(1)} %copy-done.4, bf16[32,4096]{1,0:T(8,128)(2,1)S(1)} %collective-permute-done.refs_0_.refs_6_), custom_call_target="tpu_custom_call" | custom-call | flops 1 | bytes 1 | tf_op jit(solution)/shard_map/low/pallas_call | solution.py:276
  27.9 2.0 %collective-permute-done.5.refs_10_ = bf16[16,4096]{1,0:T(8,128)(2,1)S(1)} collective-permute-done((bf16[16,4096]{1,0:T(8,128)(2,1)}, bf16[16,4096]{1,0:T(8,128)(2,1)S(1)}, u32[]{:S(2)}, u32[]{:S(2)}) %collective-permute-start.5) | collective-permute-done | bytes 131104 | tf_op jit(solution)/shard_map/ppermute | solution.py:27
  30.0 5.6 %main.2 = (bf16[208,4096]{1,0:T(8,128)(2,1)S(1)}, bf16[32,4096]{1,0:T(8,128)(2,1)S(1)}, bf16[32,4096]{1,0:T(8,128)(2,1)S(1)}, bf16[16,4096]{1,0:T(8,128)(2,1)S(1...) custom-call(bf16[208,2048]{1,0:T(8,128)(2,1)S(1)} %get-tuple-element.41.refs_0_, ...), custom_call_target="tpu_custom_call" | custom-call | flops 1 | bytes 1 | tf_op jit(solution)/shard_map/main/pallas_call | solution.py:282
  35.6 1.6 %collective-permute-start.10 = (bf16[16,4096]{1,0:T(8,128)(2,1)S(1)}, bf16[16,4096]{1,0:T(8,128)(2,1)S(1)}, u32[]{:S(2)}, u32[]{:S(2)}) collective-permute-start(bf16[16,4096]{1,0:T(8,128)(2,1)S(1)} %get-tuple-element.65), channel_id=1, source_target_pairs={{0,12},{1,13},{2,14},{3,15},{4,0},{5,1},{6,2},{7,3},{8,20},{9,21},... | collective-permute-start | bytes 393224 | tf_op jit(solution)/shard_map/ppermute | solution.py:207
  37.2 2.2 %collective-permute-start.14 = (bf16[16,4096]{1,0:T(8,128)(2,1)S(1)}, bf16[16,4096]{1,0:T(8,128)(2,1)S(1)}, u32[]{:S(2)}, u32[]{:S(2)}) collective-permute-start(bf16[16,4096]{1,0:T(8,128)(2,1)S(1)} %get-tuple-element.69), channel_id=1, source_target_pairs={{0,48},{1,49},{2,50},{3,51},{4,52},{5,53},{6,54},{7,55},{8,56},{9,... | collective-permute-start | bytes 393224 | tf_op jit(solution)/shard_map/ppermute | solution.py:27
  39.4 2.1 %collective-permute-start.8 = (bf16[32,4096]{1,0:T(8,128)(2,1)S(1)}, bf16[32,4096]{1,0:T(8,128)(2,1)S(1)}, u32[]{:S(2)}, u32[]{:S(2)}) collective-permute-start(bf16[32,4096]{1,0:T(8,128)(2,1)S(1)} %get-tuple-element.57), channel_id=1, source_target_pairs={{0,1},{1,2},{2,3},{3,4},{4,5},{5,6},{6,7},{7,8},{8,9},{9,10},{10,1... | collective-permute-start | bytes 786440 | tf_op jit(solution)/shard_map/ppermute | solution.py:27
  41.5 1.0 %high.3 = (bf16[208,2048]{1,0:T(8,128)(2,1)S(1)}, f32[8,2048]{1,0:T(8,128)S(1)}, bf16[608,2048]{1,0:T(8,128)(2,1)S(1)}) custom-call(bf16[208,4096]{1,0:T(8,128)(2,1)S(1)} %get-tuple-element.55.near, f32[304,8]{1,0:T(8,128)S(1)} %copy-done.2, bf16[608,304]{1,0:T(8,128)(2,1)S(1)} %copy-done.3), custom_call_target="tpu_custom_call" | custom-call | flops 1 | bytes 1 | tf_op jit(solution)/shard_map/high/pallas_call | solution.py:272
  42.8 3.1 %collective-permute-start.12 = (bf16[16,4096]{1,0:T(8,128)(2,1)S(1)}, bf16[16,4096]{1,0:T(8,128)(2,1)S(1)}, u32[]{:S(2)}, u32[]{:S(2)}) collective-permute-start(bf16[16,4096]{1,0:T(8,128)(2,1)S(1)} %collective-permute-done.10), channel_id=1, source_target_pairs={{12,8},{13,9},{14,10},{15,11},{0,12},{1,13},{2,14},{3,15},{20,16},... | collective-permute-start | bytes 393224 | tf_op jit(solution)/shard_map/ppermute | solution.py:207
  45.9 1.3 %collective-permute-start.11 = (bf16[16,4096]{1,0:T(8,128)(2,1)S(1)}, bf16[16,4096]{1,0:T(8,128)(2,1)S(1)}, u32[]{:S(2)}, u32[]{:S(2)}) collective-permute-start(bf16[16,4096]{1,0:T(8,128)(2,1)S(1)} %slice.9), channel_id=1, source_target_pairs={{0,2},{1,3},{2,4},{3,5},{4,6},{5,7},{6,8},{7,9},{8,10},{9,11},{10,... | collective-permute-start | bytes 393224 | tf_op jit(solution)/shard_map/ppermute | solution.py:27
  47.2 3.0 %collective-permute-start.15 = (bf16[16,4096]{1,0:T(8,128)(2,1)S(1)}, bf16[16,4096]{1,0:T(8,128)(2,1)S(1)}, u32[]{:S(2)}, u32[]{:S(2)}) collective-permute-start(bf16[16,4096]{1,0:T(8,128)(2,1)S(1)} %collective-permute-done.14), channel_id=1, source_target_pairs={{0,48},{1,49},{2,50},{3,51},{4,52},{5,53},{6,54},{7,55},{8,56},{9,... | collective-permute-start | bytes 393224 | tf_op jit(solution)/shard_map/ppermute | solution.py:27
  50.2 2.7 %collective-permute-done.8.refs_0_.refs_6_ = bf16[32,4096]{1,0:T(8,128)(2,1)S(1)} collective-permute-done((bf16[32,4096]{1,0:T(8,128)(2,1)S(1)}, bf16[32,4096]{1,0:T(8,128)(2,1)S(1)}, u32[]{:S(2)}, u32[]{:S(2)}) %collective-permute-start.8) | collective-permute-done | bytes 262176 | tf_op jit(solution)/shard_map/ppermute | solution.py:27
  52.9 1.0 %low.3 = (bf16[208,2048]{1,0:T(8,128)(2,1)S(1)}, f32[8,2048]{1,0:T(8,128)S(1)}, bf16[608,2048]{1,0:T(8,128)(2,1)S(1)}) custom-call(bf16[208,4096]{1,0:T(8,128)(2,1)S(1)} %get-tuple-element.55.near, f32[304,8]{1,0:T(8,128)S(1)} %copy-done.2, bf16[608,304]{1,0:T(8,128)(2,1)S(1)} %copy-done.3, bf16[32,4096]{1,0:T(8,128)(2,1)S(1)} %collective-permute-done.8.refs_0_.refs_6_), custom_call_target="tpu_custom_call" | custom-call | flops 1 | bytes 1 | tf_op jit(solution)/shard_map/low/pallas_call | solution.py:276
  53.9 2.6 %collective-permute-done.13.refs_10_ = bf16[16,4096]{1,0:T(8,128)(2,1)S(1)} collective-permute-done((bf16[16,4096]{1,0:T(8,128)(2,1)S(1)}, bf16[16,4096]{1,0:T(8,128)(2,1)S(1)}, u32[]{:S(2)}, u32[]{:S(2)}) %collective-permute-start.13) | collective-permute-done | bytes 131104 | tf_op jit(solution)/shard_map/ppermute | solution.py:27
  56.6 7.2 %main.3 = bf16[304,4096]{1,0:T(8,128)(2,1)} custom-call(bf16[208,2048]{1,0:T(8,128)(2,1)S(1)} %get-tuple-element.58.refs_0_, f32[8,2048]{1,0:T(8,128)S(1)} %get-tuple-element.59.refs_1_, bf16[608,2048]{1,0:T(8,128)(2,1)S(1)} %get-tuple-element.60.refs_2_, bf16[208,2048]{1,0:T(8,128)(2,1)S(1)} %get-tuple-element.61.refs_3_, ...), custom_call_target="tpu_custom_call" | custom-call | flops 1 | bytes 1 | tf_op jit(solution)/shard_map/main/pallas_call | solution.py:282
  (34 shorter events, 2.1 us)
Async XLA Ops:
  0.0 23.4 %copy-start = (bf16[304,4096]{1,0:T(8,128)(2,1)S(1)}, bf16[304,4096]{1,0:T(8,128)(2,1)}, u32[]{:S(2)}) copy-start(bf16[304,4096]{1,0:T(8,128)(2,1)} %near.3) | copy-start | bytes 7471108
  2.6 17.5 %collective-permute-start.1 = (bf16[32,4096]{1,0:T(8,128)(2,1)}, bf16[32,4096]{1,0:T(8,128)(2,1)S(1)}, u32[]{:S(2)}, u32[]{:S(2)}) collective-permute-start(bf16[32,4096]{1,0:T(8,128)(2,1)} %get-tuple-element.47), channel_id=1, source_target_pairs={{0,2},{1,3},{2,4},{3,5},{4,6},{5,7},{6,8},{7,9},{8,10},{9,11},{10,... | collective-permute-start | bytes 786440 | tf_op jit(solution)/shard_map/ppermute | solution.py:27
  4.6 13.0 %collective-permute-start.2 = (bf16[16,4096]{1,0:T(8,128)(2,1)}, bf16[16,4096]{1,0:T(8,128)(2,1)S(1)}, u32[]{:S(2)}, u32[]{:S(2)}) collective-permute-start(bf16[16,4096]{1,0:T(8,128)(2,1)} %get-tuple-element.48), channel_id=1, source_target_pairs={{0,12},{1,13},{2,14},{3,15},{4,0},{5,1},{6,2},{7,3},{8,20},{9,21},... | collective-permute-start | bytes 393224 | tf_op jit(solution)/shard_map/ppermute | solution.py:207
  10.0 10.1 %collective-permute-start.6 = (bf16[16,4096]{1,0:T(8,128)(2,1)}, bf16[16,4096]{1,0:T(8,128)(2,1)S(1)}, u32[]{:S(2)}, u32[]{:S(2)}) collective-permute-start(bf16[16,4096]{1,0:T(8,128)(2,1)} %get-tuple-element.52), channel_id=1, source_target_pairs={{0,48},{1,49},{2,50},{3,51},{4,52},{5,53},{6,54},{7,55},{8,56},{9,... | collective-permute-start | bytes 393224 | tf_op jit(solution)/shard_map/ppermute | solution.py:27
  13.0 13.9 %collective-permute-start = (bf16[32,4096]{1,0:T(8,128)(2,1)}, bf16[32,4096]{1,0:T(8,128)(2,1)S(1)}, u32[]{:S(2)}, u32[]{:S(2)}) collective-permute-start(bf16[32,4096]{1,0:T(8,128)(2,1)} %get-tuple-element.40), channel_id=1, source_target_pairs={{0,1},{1,2},{2,3},{3,4},{4,5},{5,6},{6,7},{7,8},{8,9},{9,10},{10,1... | collective-permute-start | bytes 786440 | tf_op jit(solution)/shard_map/ppermute | solution.py:27
  15.1 14.8 %collective-permute-start.5 = (bf16[16,4096]{1,0:T(8,128)(2,1)}, bf16[16,4096]{1,0:T(8,128)(2,1)S(1)}, u32[]{:S(2)}, u32[]{:S(2)}) collective-permute-start(bf16[16,4096]{1,0:T(8,128)(2,1)} %get-tuple-element.51), channel_id=1, source_target_pairs={{0,16},{1,17},{2,18},{3,19},{4,20},{5,21},{6,22},{7,23},{8,24},{9,... | collective-permute-start | bytes 393224 | tf_op jit(solution)/shard_map/ppermute | solution.py:27
  17.6 12.3 %collective-permute-start.4 = (bf16[16,4096]{1,0:T(8,128)(2,1)S(1)}, bf16[16,4096]{1,0:T(8,128)(2,1)S(1)}, u32[]{:S(2)}, u32[]{:S(2)}) collective-permute-start(bf16[16,4096]{1,0:T(8,128)(2,1)S(1)} %collective-permute-done.2), channel_id=1, source_target_pairs={{12,8},{13,9},{14,10},{15,11},{0,12},{1,13},{2,14},{3,15},{20,16},... | collective-permute-start | bytes 393224 | tf_op jit(solution)/shard_map/ppermute | solution.py:207
  20.1 9.9 %collective-permute-start.3 = (bf16[16,4096]{1,0:T(8,128)(2,1)S(1)}, bf16[16,4096]{1,0:T(8,128)(2,1)S(1)}, u32[]{:S(2)}, u32[]{:S(2)}) collective-permute-start(bf16[16,4096]{1,0:T(8,128)(2,1)S(1)} %slice.8), channel_id=1, source_target_pairs={{0,2},{1,3},{2,4},{3,5},{4,6},{5,7},{6,8},{7,9},{8,10},{9,11},{10,... | collective-permute-start | bytes 393224 | tf_op jit(solution)/shard_map/ppermute | solution.py:27
  20.3 9.7 %collective-permute-start.7 = (bf16[16,4096]{1,0:T(8,128)(2,1)S(1)}, bf16[16,4096]{1,0:T(8,128)(2,1)S(1)}, u32[]{:S(2)}, u32[]{:S(2)}) collective-permute-start(bf16[16,4096]{1,0:T(8,128)(2,1)S(1)} %collective-permute-done.6), channel_id=1, source_target_pairs={{0,48},{1,49},{2,50},{3,51},{4,52},{5,53},{6,54},{7,55},{8,56},{9,... | collective-permute-start | bytes 393224 | tf_op jit(solution)/shard_map/ppermute | solution.py:27
  23.4 0.9 %copy-start.1 = (f32[304,8]{1,0:T(8,128)S(1)}, f32[304,8]{1,0:T(8,128)}, u32[]{:S(2)}) copy-start(f32[304,8]{1,0:T(8,128)} %get-tuple-element.38.columns.refs_12_) | copy-start | bytes 29188
  24.3 1.0 %copy-start.4 = (bf16[608,304]{1,0:T(8,128)(2,1)S(1)}, bf16[608,304]{1,0:T(8,128)(2,1)}, u32[]{:S(2)}) copy-start(bf16[608,304]{1,0:T(8,128)(2,1)} %get-tuple-element.39.w_in.refs_14_) | copy-start | bytes 1108996
  25.4 4.6 %copy-start.2 = (f32[304,8]{1,0:T(8,128)S(1)}, f32[304,8]{1,0:T(8,128)}, u32[]{:S(2)}) copy-start(f32[304,8]{1,0:T(8,128)} %get-tuple-element.38.columns.refs_12_) | copy-start | bytes 29188
  25.4 4.6 %copy-start.5 = (bf16[608,304]{1,0:T(8,128)(2,1)S(1)}, bf16[608,304]{1,0:T(8,128)(2,1)}, u32[]{:S(2)}) copy-start(bf16[608,304]{1,0:T(8,128)(2,1)} %get-tuple-element.39.w_in.refs_14_) | copy-start | bytes 1108996
  25.4 4.6 %copy-start.6 = (bf16[2,304,608]{2,1,0:T(8,128)(2,1)S(1)}, bf16[2,304,608]{2,1,0:T(8,128)(2,1)}, u32[]{:S(2)}) copy-start(bf16[2,304,608]{2,1,0:T(8,128)(2,1)} %refs_15_.3) | copy-start | bytes 2217988
  25.4 4.6 %copy-start.7 = (f32[608,8]{1,0:T(8,128)S(1)}, f32[608,8]{1,0:T(8,128)}, u32[]{:S(2)}) copy-start(f32[608,8]{1,0:T(8,128)} %get-tuple-element.54.refs_13_) | copy-start | bytes 58372
  30.0 11.5 %copy-start.3 = (bf16[608,304]{1,0:T(8,128)(2,1)S(1)}, bf16[608,304]{1,0:T(8,128)(2,1)}, u32[]{:S(2)}) copy-start(bf16[608,304]{1,0:T(8,128)(2,1)} %get-tuple-element.56.w_in.refs_14_) | copy-start | bytes 1108996
  35.6 10.4 %collective-permute-start.9 = (bf16[32,4096]{1,0:T(8,128)(2,1)S(1)}, bf16[32,4096]{1,0:T(8,128)(2,1)S(1)}, u32[]{:S(2)}, u32[]{:S(2)}) collective-permute-start(bf16[32,4096]{1,0:T(8,128)(2,1)S(1)} %get-tuple-element.64), channel_id=1, source_target_pairs={{0,2},{1,3},{2,4},{3,5},{4,6},{5,7},{6,8},{7,9},{8,10},{9,11},{10,... | collective-permute-start | bytes 786440 | tf_op jit(solution)/shard_map/ppermute | solution.py:27
  35.6 7.1 %collective-permute-start.10 = (bf16[16,4096]{1,0:T(8,128)(2,1)S(1)}, bf16[16,4096]{1,0:T(8,128)(2,1)S(1)}, u32[]{:S(2)}, u32[]{:S(2)}) collective-permute-start(bf16[16,4096]{1,0:T(8,128)(2,1)S(1)} %get-tuple-element.65), channel_id=1, source_target_pairs={{0,12},{1,13},{2,14},{3,15},{4,0},{5,1},{6,2},{7,3},{8,20},{9,21},... | collective-permute-start | bytes 393224 | tf_op jit(solution)/shard_map/ppermute | solution.py:207
  37.2 8.7 %collective-permute-start.14 = (bf16[16,4096]{1,0:T(8,128)(2,1)S(1)}, bf16[16,4096]{1,0:T(8,128)(2,1)S(1)}, u32[]{:S(2)}, u32[]{:S(2)}) collective-permute-start(bf16[16,4096]{1,0:T(8,128)(2,1)S(1)} %get-tuple-element.69), channel_id=1, source_target_pairs={{0,48},{1,49},{2,50},{3,51},{4,52},{5,53},{6,54},{7,55},{8,56},{9,... | collective-permute-start | bytes 393224 | tf_op jit(solution)/shard_map/ppermute | solution.py:27
  39.4 13.6 %collective-permute-start.8 = (bf16[32,4096]{1,0:T(8,128)(2,1)S(1)}, bf16[32,4096]{1,0:T(8,128)(2,1)S(1)}, u32[]{:S(2)}, u32[]{:S(2)}) collective-permute-start(bf16[32,4096]{1,0:T(8,128)(2,1)S(1)} %get-tuple-element.57), channel_id=1, source_target_pairs={{0,1},{1,2},{2,3},{3,4},{4,5},{5,6},{6,7},{7,8},{8,9},{9,10},{10,1... | collective-permute-start | bytes 786440 | tf_op jit(solution)/shard_map/ppermute | solution.py:27
  41.5 15.1 %collective-permute-start.13 = (bf16[16,4096]{1,0:T(8,128)(2,1)S(1)}, bf16[16,4096]{1,0:T(8,128)(2,1)S(1)}, u32[]{:S(2)}, u32[]{:S(2)}) collective-permute-start(bf16[16,4096]{1,0:T(8,128)(2,1)S(1)} %get-tuple-element.68), channel_id=1, source_target_pairs={{0,16},{1,17},{2,18},{3,19},{4,20},{5,21},{6,22},{7,23},{8,24},{9,... | collective-permute-start | bytes 393224 | tf_op jit(solution)/shard_map/ppermute | solution.py:27
  42.8 13.8 %collective-permute-start.12 = (bf16[16,4096]{1,0:T(8,128)(2,1)S(1)}, bf16[16,4096]{1,0:T(8,128)(2,1)S(1)}, u32[]{:S(2)}, u32[]{:S(2)}) collective-permute-start(bf16[16,4096]{1,0:T(8,128)(2,1)S(1)} %collective-permute-done.10), channel_id=1, source_target_pairs={{12,8},{13,9},{14,10},{15,11},{0,12},{1,13},{2,14},{3,15},{20,16},... | collective-permute-start | bytes 393224 | tf_op jit(solution)/shard_map/ppermute | solution.py:207
  45.9 10.6 %collective-permute-start.11 = (bf16[16,4096]{1,0:T(8,128)(2,1)S(1)}, bf16[16,4096]{1,0:T(8,128)(2,1)S(1)}, u32[]{:S(2)}, u32[]{:S(2)}) collective-permute-start(bf16[16,4096]{1,0:T(8,128)(2,1)S(1)} %slice.9), channel_id=1, source_target_pairs={{0,2},{1,3},{2,4},{3,5},{4,6},{5,7},{6,8},{7,9},{8,10},{9,11},{10,... | collective-permute-start | bytes 393224 | tf_op jit(solution)/shard_map/ppermute | solution.py:27
  47.2 9.4 %collective-permute-start.15 = (bf16[16,4096]{1,0:T(8,128)(2,1)S(1)}, bf16[16,4096]{1,0:T(8,128)(2,1)S(1)}, u32[]{:S(2)}, u32[]{:S(2)}) collective-permute-start(bf16[16,4096]{1,0:T(8,128)(2,1)S(1)} %collective-permute-done.14), channel_id=1, source_target_pairs={{0,48},{1,49},{2,50},{3,51},{4,52},{5,53},{6,54},{7,55},{8,56},{9,... | collective-permute-start | bytes 393224 | tf_op jit(solution)/shard_map/ppermute | solution.py:27

commit v7 on v6

--- a/solution.py
+++ b/solution.py
@@ -98,8 +98,8 @@
         copy.wait()
 
 
-def weight_kernel(transposed, bias, gain, last_bias, *refs):
-    outs, made, sems = refs[:4], refs[4:8], refs[8:]
+def start_kernel(short_count, half_rows, transposed, bias, gain, last_bias, tokens, *refs):
+    outs, high, made, sems = refs[:4], refs[4:7], refs[7:11], refs[11:]
     depth, hidden = transposed.shape[1:]
     copies = []
     for block_no in range(BLOCKS):
@@ -112,6 +112,7 @@
     for at in (2, 3):
         copies.append(pltpu.make_async_copy(made[at], outs[at], sems[at]))
         copies[-1].start()
+    near_kernel(short_count, 0, half_rows, tokens, made[2], made[0], *high)
     for copy in copies:
         copy.wait()
 
@@ -148,6 +149,7 @@
 def main_kernel(short_count, block_no, last, *refs):
     nears, pair, far = refs[:6], refs[6], refs[7:12]
     (columns, hidden_columns, w_in, w_out), outs = refs[12:16], refs[16:]
+    copies = []
     near_rows, half_rows = nears[0].shape
     local_rows = pair.shape[1]
     width = near_rows + (1 + len(far)) * TRACK_CH
@@ -172,14 +174,23 @@
         out = jnp.dot(w_out[block_no], active, preferred_element_type=F32) * (0.5 / ALPHA) + b_out
         near_out = (rotated[:, here].astype(F32) + out[:near_rows]).astype(BF16)
         far_out = (far_part + out[near_rows:]).astype(BF16)
-        outs[0][:near_rows, begin:end] = near_out
         if last:
-            outs[0][near_rows:, begin:end] = far_out
+            made = outs[1]
+            made[:near_rows, begin:end] = near_out
+            made[near_rows:, begin:end] = far_out
+            copy = pltpu.make_async_copy(
+                made.at[:, begin:end], outs[0].at[:, begin:end], outs[2 + len(copies)]
+            )
+            copy.start()
+            copies.append(copy)
         else:
+            outs[0][:, begin:end] = near_out
             outs[1][TRACK_CH:, begin:end] = far_out[:TRACK_CH]
             outs[2][:, begin:end] = far_out[TRACK_CH : 3 * TRACK_CH]
             for at in range(3):
                 outs[3 + at][:, begin:end] = far_out[(3 + at) * TRACK_CH : (4 + at) * TRACK_CH]
+    for copy in copies:
+        copy.wait()
     if not last:
 
         def track(t, begin, end):
@@ -191,12 +202,13 @@
         pack_halo(track, store, local_rows, short_count)
 
 
-def call(kernel, out_shape, in_specs, name, limit):
+def call(kernel, out_shape, in_specs, name, limit, out_specs=None, scratch=()):
     return pl.pallas_call(
         kernel,
         out_shape=out_shape,
         in_specs=in_specs,
-        out_specs=[VMEM] * len(out_shape),
+        out_specs=out_specs or [VMEM] * len(out_shape),
+        scratch_shapes=scratch,
         compiler_params=pltpu.CompilerParams(vmem_limit_bytes=limit << 20),
         cost_estimate=pl.CostEstimate(flops=COST, transcendentals=0, bytes_accessed=COST),
         name=name,
@@ -258,29 +270,36 @@
         name="first",
     )(tokens)
     made = [((hidden, width), BF16)] * BLOCKS + [((width, 8), F32), ((hidden, 8), F32)]
-    *w_ins, columns, hidden_columns = pl.pallas_call(
-        weight_kernel,
-        out_shape=[jax.ShapeDtypeStruct(*entry) for entry in made],
-        in_specs=[VMEM] * 4,
-        out_specs=[pl.BlockSpec(memory_space=pltpu.HBM)] * 4,
+    *w_ins, columns, hidden_columns, rotated, squares, partial = pl.pallas_call(
+        functools.partial(start_kernel, short_count, half_rows),
+        out_shape=[jax.ShapeDtypeStruct(*entry) for entry in made] + half_shapes,
+        in_specs=[VMEM] * 5,
+        out_specs=[pl.BlockSpec(memory_space=pltpu.HBM)] * 4 + [VMEM] * 3,
         scratch_shapes=[pltpu.VMEM(*entry) for entry in made] + [pltpu.SemaphoreType.DMA] * 4,
-        name="weights",
-    )(jnp.swapaxes(in_weight, 1, 2), in_bias, norm_gain, out_bias)
+        compiler_params=pltpu.CompilerParams(vmem_limit_bytes=16 << 20),
+        name="start",
+    )(jnp.swapaxes(in_weight, 1, 2), in_bias, norm_gain, out_bias, tokens)
+    high = [rotated, squares, partial]
     near = tokens
     for block_no in range(BLOCKS):
         last = block_no == BLOCKS - 1
-        high = call(
-            functools.partial(near_kernel, short_count, block_no, half_rows), half_shapes, [VMEM] * 3, "high", 8
-        )(near, columns, w_ins[block_no])
-        pair, moved = exchange(pair, duo, far, [columns] if block_no == 0 else high[1:2])
+        if block_no:
+            high = call(
+                functools.partial(near_kernel, short_count, block_no, half_rows), half_shapes, [VMEM] * 3, "high", 8
+            )(near, columns, w_ins[block_no])
+        pair, moved = exchange(pair, duo, far, [high[1]])
         low = call(functools.partial(near_kernel, short_count, block_no, 0), half_shapes, [VMEM] * 4, "low", 8)(
             near, columns, w_ins[block_no], pair
         )
         out_shape = [jax.ShapeDtypeStruct((width, local_rows), BF16)]
         if not last:
             out_shape = [near_shape, two, two] + [one] * (far_count - 2)
+        out_specs, scratch = [VMEM] * len(out_shape), []
+        if last:
+            out_specs = [pl.BlockSpec(memory_space=pltpu.HBM)]
+            scratch = [pltpu.VMEM((width, local_rows), BF16)] + [pltpu.SemaphoreType.DMA] * (local_rows // TILE)
         outs = call(
-            functools.partial(main_kernel, short_count, block_no, last), out_shape, [VMEM] * 16, "main", 24
+            functools.partial(main_kernel, short_count, block_no, last), out_shape, [VMEM] * 16, "main", 24, out_specs, scratch
         )(*low, *high, pair, *moved, columns, hidden_columns, w_ins[block_no], out_weight)
         if last:
             return outs[0]

time: 64.8 us -> 64.5 us (level)
  waiting for transfers between devices: 8.28 us -> 10.3 us
  Pallas kernels: 21.7 us -> 20.2 us
  local copies, waits for them, and re-layouts: 1.98 us -> 1.17 us
    ppermute x12, waiting for transfers between devices: 7.96 us -> 10.3 us  [shifted(): return lax.ppermute(value, axis, pairs)]
    ppermute x4, starting transfers between devices: 12.5 us -> 10.2 us  [permuted(): return lax.ppermute(value, 'seq', moves)]
    ppermute x12, starting transfers between devices: 19.1 us -> 21.2 us  [shifted(): return lax.ppermute(value, axis, pairs)]
    pallas_call x2 -> x1, Pallas kernels: 1.95 us -> 0.98 us  [shards(): call(functools.partial(near_kernel, short_count, block_no, half_rows), ha...]
    unnamed x16 -> x12, local copies, waits for them, and re-layouts: 1.96 us -> 1.15 us
  transfers between devices with their start and end apart: 16 -> 16, of which waited for: 5 -> 5; matrix products, arithmetic and copies ran while one was open for 0% -> 0% of each run, Pallas kernels for 10% -> 9%
where the time goes in v7:
time: 64.5 us; the launch traced here: 63.4 us
  starting transfers between devices  31.4 us (49%)
  Pallas kernels  20.2 us (31%)
  waiting for transfers between devices  10.3 us (16%)
  local copies, waits for them, and re-layouts  1.17 us (2%)
    ppermute x12, starting transfers between devices, shifted(): return lax.ppermute(value, axis, pairs)  21.2 us
    pallas_call x2, Pallas kernels, shards(): call(functools.partial(main_kernel, short_count, block_no, last), out_sha...  12.3 us
    ppermute x12, waiting for transfers between devices, shifted(): return lax.ppermute(value, axis, pairs)  10.3 us
    ppermute x4, starting transfers between devices, permuted(): return lax.ppermute(value, 'seq', moves)  10.2 us
    pallas_call x1, Pallas kernels, shards(): pl.pallas_call(functools.partial(first_kernel, short_count), out_shape=[t...  2.5 us
    pallas_call x1, Pallas kernels, shards(): pl.pallas_call(functools.partial(start_kernel, short_count, half_rows), o...  2.41 us
    pallas_call x2, Pallas kernels, shards(): call(functools.partial(near_kernel, short_count, block_no, 0), half_shape...  2 us
  transfers between devices with their start and end apart: 16, of which 5 were waited for; matrix products, arithmetic and copies ran while one was open for 0% of the time, Pallas kernels for 9%

profile of v7, /device:TPU:2, one launch (start us, length us, event | category | flops | bytes accessed | tf_op | source)
XLA Modules:
  0.0 63.4 jit_solution(16351361523621800821)
XLA Ops:
  0.0 2.5 %first.1 = (bf16[32,4096]{1,0:T(8,128)(2,1)}, bf16[32,4096]{1,0:T(8,128)(2,1)}, bf16[16,4096]{1,0:T(8,128)(2,1)}, bf16[16,4096]{1,0:T(8,128)(2,1)}, bf16[16,4096]{1,0:T(8,128)(2,1)}) custom-call(bf16[304,4096]{1,0:T(8,128)(2,1)} %near.1), custom_call_target="tpu_custom_call" | custom-call | tf_op jit(solution)/shard_map/first/pallas_call | solution.py:263
  2.5 2.0 %collective-permute-start.1 = (bf16[32,4096]{1,0:T(8,128)(2,1)}, bf16[32,4096]{1,0:T(8,128)(2,1)S(1)}, u32[]{:S(2)}, u32[]{:S(2)}) collective-permute-start(bf16[32,4096]{1,0:T(8,128)(2,1)} %get-tuple-element.47), channel_id=1, source_target_pairs={{0,2},{1,3},{2,4},{3,5},{4,6},{5,7},{6,8},{7,9},{8,10},{9,11},{10,... | collective-permute-start | bytes 786440 | tf_op jit(solution)/shard_map/ppermute | solution.py:27
  4.5 5.4 %collective-permute-start.2 = (bf16[16,4096]{1,0:T(8,128)(2,1)}, bf16[16,4096]{1,0:T(8,128)(2,1)S(1)}, u32[]{:S(2)}, u32[]{:S(2)}) collective-permute-start(bf16[16,4096]{1,0:T(8,128)(2,1)} %get-tuple-element.48), channel_id=1, source_target_pairs={{0,12},{1,13},{2,14},{3,15},{4,0},{5,1},{6,2},{7,3},{8,20},{9,21},... | collective-permute-start | bytes 393224 | tf_op jit(solution)/shard_map/ppermute | solution.py:219
  9.9 3.0 %collective-permute-start.6 = (bf16[16,4096]{1,0:T(8,128)(2,1)}, bf16[16,4096]{1,0:T(8,128)(2,1)S(1)}, u32[]{:S(2)}, u32[]{:S(2)}) collective-permute-start(bf16[16,4096]{1,0:T(8,128)(2,1)} %get-tuple-element.52), channel_id=1, source_target_pairs={{0,48},{1,49},{2,50},{3,51},{4,52},{5,53},{6,54},{7,55},{8,56},{9,... | collective-permute-start | bytes 393224 | tf_op jit(solution)/shard_map/ppermute | solution.py:27
  12.9 2.1 %collective-permute-start = (bf16[32,4096]{1,0:T(8,128)(2,1)}, bf16[32,4096]{1,0:T(8,128)(2,1)S(1)}, u32[]{:S(2)}, u32[]{:S(2)}) collective-permute-start(bf16[32,4096]{1,0:T(8,128)(2,1)} %get-tuple-element.40), channel_id=1, source_target_pairs={{0,1},{1,2},{2,3},{3,4},{4,5},{5,6},{6,7},{7,8},{8,9},{9,10},{10,1... | collective-permute-start | bytes 786440 | tf_op jit(solution)/shard_map/ppermute | solution.py:27
  15.1 1.1 %copy-done.2 = bf16[2,608,304]{1,2,0:T(8,128)(2,1)S(1)} copy-done((bf16[2,608,304]{1,2,0:T(8,128)(2,1)S(1)}, bf16[2,608,304]{1,2,0:T(8,128)(2,1)}, u32[]{:S(2)}) %copy-start.2) | copy-done | bytes 739352
  16.2 2.4 %start.1 = (bf16[608,304]{1,0:T(8,128)(2,1)S(1)}, bf16[608,304]{1,0:T(8,128)(2,1)S(1)}, f32[304,8]{1,0:T(8,128)S(1)}, f32[608,8]{1,0:T(8,128)S(1)}, bf16[208,204...) custom-call(bf16[2,304,608]{2,1,0:T(8,128)(2,1)S(1)} %bitcast.1, f32[2,608]{1,0:T(2,128)S(1)} %copy-done.3, ...), custom_call_target="tpu_custom_call" | custom-call | tf_op jit(solution)/shard_map/start/pallas_call | solution.py:273
  18.7 1.5 %collective-permute-start.4 = (bf16[16,4096]{1,0:T(8,128)(2,1)S(1)}, bf16[16,4096]{1,0:T(8,128)(2,1)S(1)}, u32[]{:S(2)}, u32[]{:S(2)}) collective-permute-start(bf16[16,4096]{1,0:T(8,128)(2,1)S(1)} %collective-permute-done.2), channel_id=1, source_target_pairs={{12,8},{13,9},{14,10},{15,11},{0,12},{1,13},{2,14},{3,15},{20,16},... | collective-permute-start | bytes 393224 | tf_op jit(solution)/shard_map/ppermute | solution.py:219
  20.2 1.1 %collective-permute-start.3 = (bf16[16,4096]{1,0:T(8,128)(2,1)S(1)}, bf16[16,4096]{1,0:T(8,128)(2,1)S(1)}, u32[]{:S(2)}, u32[]{:S(2)}) collective-permute-start(bf16[16,4096]{1,0:T(8,128)(2,1)S(1)} %slice.8), channel_id=1, source_target_pairs={{0,2},{1,3},{2,4},{3,5},{4,6},{5,7},{6,8},{7,9},{8,10},{9,11},{10,... | collective-permute-start | bytes 393224 | tf_op jit(solution)/shard_map/ppermute | solution.py:27
  21.3 2.9 %collective-permute-start.7 = (bf16[16,4096]{1,0:T(8,128)(2,1)S(1)}, bf16[16,4096]{1,0:T(8,128)(2,1)S(1)}, u32[]{:S(2)}, u32[]{:S(2)}) collective-permute-start(bf16[16,4096]{1,0:T(8,128)(2,1)S(1)} %collective-permute-done.6), channel_id=1, source_target_pairs={{0,48},{1,49},{2,50},{3,51},{4,52},{5,53},{6,54},{7,55},{8,56},{9,... | collective-permute-start | bytes 393224 | tf_op jit(solution)/shard_map/ppermute | solution.py:27
  24.2 2.7 %collective-permute-done.refs_0_.refs_6_ = bf16[32,4096]{1,0:T(8,128)(2,1)S(1)} collective-permute-done((bf16[32,4096]{1,0:T(8,128)(2,1)}, bf16[32,4096]{1,0:T(8,128)(2,1)S(1)}, u32[]{:S(2)}, u32[]{:S(2)}) %collective-permute-start) | collective-permute-done | bytes 262176 | tf_op jit(solution)/shard_map/ppermute | solution.py:27
  26.9 1.0 %low.2 = (bf16[208,2048]{1,0:T(8,128)(2,1)S(1)}, f32[8,2048]{1,0:T(8,128)S(1)}, bf16[608,2048]{1,0:T(8,128)(2,1)S(1)}) custom-call(bf16[304,4096]{1,0:T(8,128)(2,1)S(1)} %copy-done, f32[304,8]{1,0:T(8,128)S(1)} %get-tuple-element.38.columns.refs_12_, bf16[608,304]{1,0:T(8,128)(2,1)S(1)} %get-tuple-element.39.w_in.refs_14_, ...), custom_call_target="tpu_custom_call" | custom-call | flops 1 | bytes 1 | tf_op jit(solution)/shard_map/low/pallas_call | solution.py:291
  27.9 2.0 %collective-permute-done.5.refs_10_ = bf16[16,4096]{1,0:T(8,128)(2,1)S(1)} collective-permute-done((bf16[16,4096]{1,0:T(8,128)(2,1)}, bf16[16,4096]{1,0:T(8,128)(2,1)S(1)}, u32[]{:S(2)}, u32[]{:S(2)}) %collective-permute-start.5) | collective-permute-done | bytes 131104 | tf_op jit(solution)/shard_map/ppermute | solution.py:27
  29.9 5.6 %main.2 = (bf16[208,4096]{1,0:T(8,128)(2,1)S(1)}, bf16[32,4096]{1,0:T(8,128)(2,1)S(1)}, bf16[32,4096]{1,0:T(8,128)(2,1)S(1)}, bf16[16,4096]{1,0:T(8,128)(2,1)S(1...) custom-call(bf16[208,2048]{1,0:T(8,128)(2,1)S(1)} %get-tuple-element.41.refs_0_, ...), custom_call_target="tpu_custom_call" | custom-call | flops 1 | bytes 1 | tf_op jit(solution)/shard_map/main/pallas_call | solution.py:301
  35.5 1.1 %collective-permute-start.10 = (bf16[16,4096]{1,0:T(8,128)(2,1)S(1)}, bf16[16,4096]{1,0:T(8,128)(2,1)S(1)}, u32[]{:S(2)}, u32[]{:S(2)}) collective-permute-start(bf16[16,4096]{1,0:T(8,128)(2,1)S(1)} %get-tuple-element.65), channel_id=1, source_target_pairs={{0,12},{1,13},{2,14},{3,15},{4,0},{5,1},{6,2},{7,3},{8,20},{9,21},... | collective-permute-start | bytes 393224 | tf_op jit(solution)/shard_map/ppermute | solution.py:219
  36.6 2.9 %collective-permute-start.14 = (bf16[16,4096]{1,0:T(8,128)(2,1)S(1)}, bf16[16,4096]{1,0:T(8,128)(2,1)S(1)}, u32[]{:S(2)}, u32[]{:S(2)}) collective-permute-start(bf16[16,4096]{1,0:T(8,128)(2,1)S(1)} %get-tuple-element.69), channel_id=1, source_target_pairs={{0,48},{1,49},{2,50},{3,51},{4,52},{5,53},{6,54},{7,55},{8,56},{9,... | collective-permute-start | bytes 393224 | tf_op jit(solution)/shard_map/ppermute | solution.py:27
  39.5 1.9 %collective-permute-start.8 = (bf16[32,4096]{1,0:T(8,128)(2,1)S(1)}, bf16[32,4096]{1,0:T(8,128)(2,1)S(1)}, u32[]{:S(2)}, u32[]{:S(2)}) collective-permute-start(bf16[32,4096]{1,0:T(8,128)(2,1)S(1)} %get-tuple-element.57), channel_id=1, source_target_pairs={{0,1},{1,2},{2,3},{3,4},{4,5},{5,6},{6,7},{7,8},{8,9},{9,10},{10,1... | collective-permute-start | bytes 786440 | tf_op jit(solution)/shard_map/ppermute | solution.py:27
  42.4 2.2 %collective-permute-start.12 = (bf16[16,4096]{1,0:T(8,128)(2,1)S(1)}, bf16[16,4096]{1,0:T(8,128)(2,1)S(1)}, u32[]{:S(2)}, u32[]{:S(2)}) collective-permute-start(bf16[16,4096]{1,0:T(8,128)(2,1)S(1)} %collective-permute-done.10), channel_id=1, source_target_pairs={{12,8},{13,9},{14,10},{15,11},{0,12},{1,13},{2,14},{3,15},{20,16},... | collective-permute-start | bytes 393224 | tf_op jit(solution)/shard_map/ppermute | solution.py:219
  45.4 2.2 %collective-permute-start.11 = (bf16[16,4096]{1,0:T(8,128)(2,1)S(1)}, bf16[16,4096]{1,0:T(8,128)(2,1)S(1)}, u32[]{:S(2)}, u32[]{:S(2)}) collective-permute-start(bf16[16,4096]{1,0:T(8,128)(2,1)S(1)} %slice.9), channel_id=1, source_target_pairs={{0,2},{1,3},{2,4},{3,5},{4,6},{5,7},{6,8},{7,9},{8,10},{9,11},{10,... | collective-permute-start | bytes 393224 | tf_op jit(solution)/shard_map/ppermute | solution.py:27
  47.6 3.0 %collective-permute-start.15 = (bf16[16,4096]{1,0:T(8,128)(2,1)S(1)}, bf16[16,4096]{1,0:T(8,128)(2,1)S(1)}, u32[]{:S(2)}, u32[]{:S(2)}) collective-permute-start(bf16[16,4096]{1,0:T(8,128)(2,1)S(1)} %collective-permute-done.14), channel_id=1, source_target_pairs={{0,48},{1,49},{2,50},{3,51},{4,52},{5,53},{6,54},{7,55},{8,56},{9,... | collective-permute-start | bytes 393224 | tf_op jit(solution)/shard_map/ppermute | solution.py:27
  50.6 2.5 %collective-permute-done.8.refs_0_.refs_6_ = bf16[32,4096]{1,0:T(8,128)(2,1)S(1)} collective-permute-done((bf16[32,4096]{1,0:T(8,128)(2,1)S(1)}, bf16[32,4096]{1,0:T(8,128)(2,1)S(1)}, u32[]{:S(2)}, u32[]{:S(2)}) %collective-permute-start.8) | collective-permute-done | bytes 262176 | tf_op jit(solution)/shard_map/ppermute | solution.py:27
  53.1 1.0 %low.3 = (bf16[208,2048]{1,0:T(8,128)(2,1)S(1)}, f32[8,2048]{1,0:T(8,128)S(1)}, bf16[608,2048]{1,0:T(8,128)(2,1)S(1)}) custom-call(bf16[208,4096]{1,0:T(8,128)(2,1)S(1)} %get-tuple-element.55.near, f32[304,8]{1,0:T(8,128)S(1)} %get-tuple-element.38.columns.refs_12_, bf16[608,304]{1,0:T(8,128)(2,1)S(1)} %get-tuple-element.56.w_in.refs_14_, ...), custom_call_target="tpu_custom_call" | custom-call | flops 1 | bytes 1 | tf_op jit(solution)/shard_map/low/pallas_call | solution.py:291
  54.1 2.3 %collective-permute-done.13.refs_10_ = bf16[16,4096]{1,0:T(8,128)(2,1)S(1)} collective-permute-done((bf16[16,4096]{1,0:T(8,128)(2,1)S(1)}, bf16[16,4096]{1,0:T(8,128)(2,1)S(1)}, u32[]{:S(2)}, u32[]{:S(2)}) %collective-permute-start.13) | collective-permute-done | bytes 131104 | tf_op jit(solution)/shard_map/ppermute | solution.py:27
  56.5 6.7 %main.3 = bf16[304,4096]{1,0:T(8,128)(2,1)} custom-call(bf16[208,2048]{1,0:T(8,128)(2,1)S(1)} %get-tuple-element.58.refs_0_, f32[8,2048]{1,0:T(8,128)S(1)} %get-tuple-element.59.refs_1_, bf16[608,2048]{1,0:T(8,128)(2,1)S(1)} %get-tuple-element.60.refs_2_, bf16[208,2048]{1,0:T(8,128)(2,1)S(1)} %get-tuple-element.61.refs_3_, ...), custom_call_target="tpu_custom_call" | custom-call | flops 1 | bytes 1 | tf_op jit(solution)/shard_map/main/pallas_call | solution.py:301
  (29 shorter events, 1.9 us)
Async XLA Ops:
  0.0 15.1 %copy-start = (bf16[304,4096]{1,0:T(8,128)(2,1)S(1)}, bf16[304,4096]{1,0:T(8,128)(2,1)}, u32[]{:S(2)}) copy-start(bf16[304,4096]{1,0:T(8,128)(2,1)} %near.1) | copy-start | bytes 7471108
  0.0 15.1 %copy-start.5 = (f32[2,304]{1,0:T(2,128)S(1)}, f32[2,304]{1,0:T(2,128)}, u32[]{:S(2)}) copy-start(f32[2,304]{1,0:T(2,128)} %last_bias.1) | copy-start | bytes 7300
  0.0 15.1 %copy-start.3 = (f32[2,608]{1,0:T(2,128)S(1)}, f32[2,608]{1,0:T(2,128)}, u32[]{:S(2)}) copy-start(f32[2,608]{1,0:T(2,128)} %bias.1) | copy-start | bytes 14596
  0.0 15.1 %copy-start.4 = (f32[2,304]{1,0:T(2,128)S(1)}, f32[2,304]{1,0:T(2,128)}, u32[]{:S(2)}) copy-start(f32[2,304]{1,0:T(2,128)} %gain.1) | copy-start | bytes 7300
  2.5 17.7 %collective-permute-start.1 = (bf16[32,4096]{1,0:T(8,128)(2,1)}, bf16[32,4096]{1,0:T(8,128)(2,1)S(1)}, u32[]{:S(2)}, u32[]{:S(2)}) collective-permute-start(bf16[32,4096]{1,0:T(8,128)(2,1)} %get-tuple-element.47), channel_id=1, source_target_pairs={{0,2},{1,3},{2,4},{3,5},{4,6},{5,7},{6,8},{7,9},{8,10},{9,11},{10,... | collective-permute-start | bytes 786440 | tf_op jit(solution)/shard_map/ppermute | solution.py:27
  4.5 14.1 %collective-permute-start.2 = (bf16[16,4096]{1,0:T(8,128)(2,1)}, bf16[16,4096]{1,0:T(8,128)(2,1)S(1)}, u32[]{:S(2)}, u32[]{:S(2)}) collective-permute-start(bf16[16,4096]{1,0:T(8,128)(2,1)} %get-tuple-element.48), channel_id=1, source_target_pairs={{0,12},{1,13},{2,14},{3,15},{4,0},{5,1},{6,2},{7,3},{8,20},{9,21},... | collective-permute-start | bytes 393224 | tf_op jit(solution)/shard_map/ppermute | solution.py:219
  9.9 10.3 %collective-permute-start.6 = (bf16[16,4096]{1,0:T(8,128)(2,1)}, bf16[16,4096]{1,0:T(8,128)(2,1)S(1)}, u32[]{:S(2)}, u32[]{:S(2)}) collective-permute-start(bf16[16,4096]{1,0:T(8,128)(2,1)} %get-tuple-element.52), channel_id=1, source_target_pairs={{0,48},{1,49},{2,50},{3,51},{4,52},{5,53},{6,54},{7,55},{8,56},{9,... | collective-permute-start | bytes 393224 | tf_op jit(solution)/shard_map/ppermute | solution.py:27
  12.9 13.9 %collective-permute-start = (bf16[32,4096]{1,0:T(8,128)(2,1)}, bf16[32,4096]{1,0:T(8,128)(2,1)S(1)}, u32[]{:S(2)}, u32[]{:S(2)}) collective-permute-start(bf16[32,4096]{1,0:T(8,128)(2,1)} %get-tuple-element.40), channel_id=1, source_target_pairs={{0,1},{1,2},{2,3},{3,4},{4,5},{5,6},{6,7},{7,8},{8,9},{9,10},{10,1... | collective-permute-start | bytes 786440 | tf_op jit(solution)/shard_map/ppermute | solution.py:27
  15.1 14.8 %collective-permute-start.5 = (bf16[16,4096]{1,0:T(8,128)(2,1)}, bf16[16,4096]{1,0:T(8,128)(2,1)S(1)}, u32[]{:S(2)}, u32[]{:S(2)}) collective-permute-start(bf16[16,4096]{1,0:T(8,128)(2,1)} %get-tuple-element.51), channel_id=1, source_target_pairs={{0,16},{1,17},{2,18},{3,19},{4,20},{5,21},{6,22},{7,23},{8,24},{9,... | collective-permute-start | bytes 393224 | tf_op jit(solution)/shard_map/ppermute | solution.py:27
  15.1 1.1 %copy-start.2 = (bf16[2,608,304]{1,2,0:T(8,128)(2,1)S(1)}, bf16[2,608,304]{1,2,0:T(8,128)(2,1)}, u32[]{:S(2)}) copy-start(bf16[2,608,304]{1,2,0:T(8,128)(2,1)} %param.8) | copy-start | bytes 2217988
  18.7 11.2 %copy-start.1 = (bf16[2,304,608]{2,1,0:T(8,128)(2,1)S(1)}, bf16[2,304,608]{2,1,0:T(8,128)(2,1)}, u32[]{:S(2)}) copy-start(bf16[2,304,608]{2,1,0:T(8,128)(2,1)} %refs_15_.3) | copy-start | bytes 2217988
  18.7 11.2 %collective-permute-start.4 = (bf16[16,4096]{1,0:T(8,128)(2,1)S(1)}, bf16[16,4096]{1,0:T(8,128)(2,1)S(1)}, u32[]{:S(2)}, u32[]{:S(2)}) collective-permute-start(bf16[16,4096]{1,0:T(8,128)(2,1)S(1)} %collective-permute-done.2), channel_id=1, source_target_pairs={{12,8},{13,9},{14,10},{15,11},{0,12},{1,13},{2,14},{3,15},{20,16},... | collective-permute-start | bytes 393224 | tf_op jit(solution)/shard_map/ppermute | solution.py:219
  20.2 9.7 %collective-permute-start.3 = (bf16[16,4096]{1,0:T(8,128)(2,1)S(1)}, bf16[16,4096]{1,0:T(8,128)(2,1)S(1)}, u32[]{:S(2)}, u32[]{:S(2)}) collective-permute-start(bf16[16,4096]{1,0:T(8,128)(2,1)S(1)} %slice.8), channel_id=1, source_target_pairs={{0,2},{1,3},{2,4},{3,5},{4,6},{5,7},{6,8},{7,9},{8,10},{9,11},{10,... | collective-permute-start | bytes 393224 | tf_op jit(solution)/shard_map/ppermute | solution.py:27
  21.3 8.6 %collective-permute-start.7 = (bf16[16,4096]{1,0:T(8,128)(2,1)S(1)}, bf16[16,4096]{1,0:T(8,128)(2,1)S(1)}, u32[]{:S(2)}, u32[]{:S(2)}) collective-permute-start(bf16[16,4096]{1,0:T(8,128)(2,1)S(1)} %collective-permute-done.6), channel_id=1, source_target_pairs={{0,48},{1,49},{2,50},{3,51},{4,52},{5,53},{6,54},{7,55},{8,56},{9,... | collective-permute-start | bytes 393224 | tf_op jit(solution)/shard_map/ppermute | solution.py:27
  35.5 9.9 %collective-permute-start.9 = (bf16[32,4096]{1,0:T(8,128)(2,1)S(1)}, bf16[32,4096]{1,0:T(8,128)(2,1)S(1)}, u32[]{:S(2)}, u32[]{:S(2)}) collective-permute-start(bf16[32,4096]{1,0:T(8,128)(2,1)S(1)} %get-tuple-element.64), channel_id=1, source_target_pairs={{0,2},{1,3},{2,4},{3,5},{4,6},{5,7},{6,8},{7,9},{8,10},{9,11},{10,... | collective-permute-start | bytes 786440 | tf_op jit(solution)/shard_map/ppermute | solution.py:27
  35.5 6.9 %collective-permute-start.10 = (bf16[16,4096]{1,0:T(8,128)(2,1)S(1)}, bf16[16,4096]{1,0:T(8,128)(2,1)S(1)}, u32[]{:S(2)}, u32[]{:S(2)}) collective-permute-start(bf16[16,4096]{1,0:T(8,128)(2,1)S(1)} %get-tuple-element.65), channel_id=1, source_target_pairs={{0,12},{1,13},{2,14},{3,15},{4,0},{5,1},{6,2},{7,3},{8,20},{9,21},... | collective-permute-start | bytes 393224 | tf_op jit(solution)/shard_map/ppermute | solution.py:219
  36.6 8.0 %collective-permute-start.14 = (bf16[16,4096]{1,0:T(8,128)(2,1)S(1)}, bf16[16,4096]{1,0:T(8,128)(2,1)S(1)}, u32[]{:S(2)}, u32[]{:S(2)}) collective-permute-start(bf16[16,4096]{1,0:T(8,128)(2,1)S(1)} %get-tuple-element.69), channel_id=1, source_target_pairs={{0,48},{1,49},{2,50},{3,51},{4,52},{5,53},{6,54},{7,55},{8,56},{9,... | collective-permute-start | bytes 393224 | tf_op jit(solution)/shard_map/ppermute | solution.py:27
  39.5 13.7 %collective-permute-start.8 = (bf16[32,4096]{1,0:T(8,128)(2,1)S(1)}, bf16[32,4096]{1,0:T(8,128)(2,1)S(1)}, u32[]{:S(2)}, u32[]{:S(2)}) collective-permute-start(bf16[32,4096]{1,0:T(8,128)(2,1)S(1)} %get-tuple-element.57), channel_id=1, source_target_pairs={{0,1},{1,2},{2,3},{3,4},{4,5},{5,6},{6,7},{7,8},{8,9},{9,10},{10,1... | collective-permute-start | bytes 786440 | tf_op jit(solution)/shard_map/ppermute | solution.py:27
  41.4 15.1 %collective-permute-start.13 = (bf16[16,4096]{1,0:T(8,128)(2,1)S(1)}, bf16[16,4096]{1,0:T(8,128)(2,1)S(1)}, u32[]{:S(2)}, u32[]{:S(2)}) collective-permute-start(bf16[16,4096]{1,0:T(8,128)(2,1)S(1)} %get-tuple-element.68), channel_id=1, source_target_pairs={{0,16},{1,17},{2,18},{3,19},{4,20},{5,21},{6,22},{7,23},{8,24},{9,... | collective-permute-start | bytes 393224 | tf_op jit(solution)/shard_map/ppermute | solution.py:27
  42.4 14.0 %collective-permute-start.12 = (bf16[16,4096]{1,0:T(8,128)(2,1)S(1)}, bf16[16,4096]{1,0:T(8,128)(2,1)S(1)}, u32[]{:S(2)}, u32[]{:S(2)}) collective-permute-start(bf16[16,4096]{1,0:T(8,128)(2,1)S(1)} %collective-permute-done.10), channel_id=1, source_target_pairs={{12,8},{13,9},{14,10},{15,11},{0,12},{1,13},{2,14},{3,15},{20,16},... | collective-permute-start | bytes 393224 | tf_op jit(solution)/shard_map/ppermute | solution.py:219
  45.4 11.1 %collective-permute-start.11 = (bf16[16,4096]{1,0:T(8,128)(2,1)S(1)}, bf16[16,4096]{1,0:T(8,128)(2,1)S(1)}, u32[]{:S(2)}, u32[]{:S(2)}) collective-permute-start(bf16[16,4096]{1,0:T(8,128)(2,1)S(1)} %slice.9), channel_id=1, source_target_pairs={{0,2},{1,3},{2,4},{3,5},{4,6},{5,7},{6,8},{7,9},{8,10},{9,11},{10,... | collective-permute-start | bytes 393224 | tf_op jit(solution)/shard_map/ppermute | solution.py:27
  47.6 8.8 %collective-permute-start.15 = (bf16[16,4096]{1,0:T(8,128)(2,1)S(1)}, bf16[16,4096]{1,0:T(8,128)(2,1)S(1)}, u32[]{:S(2)}, u32[]{:S(2)}) collective-permute-start(bf16[16,4096]{1,0:T(8,128)(2,1)S(1)} %collective-permute-done.14), channel_id=1, source_target_pairs={{0,48},{1,49},{2,50},{3,51},{4,52},{5,53},{6,54},{7,55},{8,56},{9,... | collective-permute-start | bytes 393224 | tf_op jit(solution)/shard_map/ppermute | solution.py:27

commit v8 on v7

--- a/solution.py
+++ b/solution.py
@@ -13,6 +13,7 @@
 LANES = 128
 NEAR_TILE = 1024
 TILE = 2048
+LAST_TILE = 1024
 COST = 1
 GELU_A = 0.7978845608028654
 ALPHA = (GELU_A * 0.044715) ** (1.0 / 3.0)
@@ -156,10 +157,11 @@
     gain = columns[near_rows:, block_no : block_no + 1]
     b_out = columns[:, BLOCKS + block_no : BLOCKS + block_no + 1]
     b_in = hidden_columns[:, block_no : block_no + 1] * ALPHA
-    for begin in range(0, local_rows, TILE):
-        end = begin + TILE
+    tile = LAST_TILE if last else TILE
+    for begin in range(0, local_rows, tile):
+        end = begin + tile
         rotated, squares, partial = nears[:3] if begin < half_rows else nears[3:]
-        here = slice(begin % half_rows, begin % half_rows + TILE)
+        here = slice(begin % half_rows, begin % half_rows + tile)
         parts = [pair[TRACK_CH:, begin:end].astype(F32)]
         parts += [ref[:TRACK_CH, begin:end].astype(F32) for ref in far]
         total = squares[:, here]
@@ -237,10 +239,9 @@
     eight = permuted(eight, to_middle)
     duo = shifted(duo, "seq", 2)
     pair = shifted(pair, "seq", 1)
-    back = shifted(thirty_two, "seq", -16)
+    back = shifted(thirty_two, "seq", 32)
     sixteen = shifted(sixteen, "seq", 16)
     four = shifted(after(duo[TRACK_CH:], eight), "seq", 2)
-    back = shifted(after(back, duo), "seq", -16)
     eight = permuted(after(eight, *fill), from_middle)
     return pair, [duo, four, eight, sixteen, back]
 
@@ -297,7 +298,7 @@
         out_specs, scratch = [VMEM] * len(out_shape), []
         if last:
             out_specs = [pl.BlockSpec(memory_space=pltpu.HBM)]
-            scratch = [pltpu.VMEM((width, local_rows), BF16)] + [pltpu.SemaphoreType.DMA] * (local_rows // TILE)
+            scratch = [pltpu.VMEM((width, local_rows), BF16)] + [pltpu.SemaphoreType.DMA] * (local_rows // LAST_TILE)
         outs = call(
             functools.partial(main_kernel, short_count, block_no, last), out_shape, [VMEM] * 16, "main", 24, out_specs, scratch
         )(*low, *high, pair, *moved, columns, hidden_columns, w_ins[block_no], out_weight)

time: 64.5 us -> 67.7 us (1.050); the launches traced: 63.4 us -> 67.6 us
  waiting for transfers between devices: 10.3 us -> 22.4 us
  starting transfers between devices: 31.4 us -> 23.7 us
    ppermute x12 -> x10, waiting for transfers between devices: 10.3 us -> 22.4 us  [shifted(): return lax.ppermute(value, axis, pairs)]
    ppermute x12 -> x10, starting transfers between devices: 21.2 us -> 15.7 us  [shifted(): return lax.ppermute(value, axis, pairs)]
    ppermute x4, starting transfers between devices: 10.2 us -> 8.07 us  [permuted(): return lax.ppermute(value, 'seq', moves)]
  transfers between devices with their start and end apart: 16 -> 14, of which waited for: 5 -> 6; matrix products, arithmetic and copies ran while one was open for 0% -> 0% of each run, Pallas kernels for 9% -> 8%
where the time goes in v8:
time: 67.7 us; the launch traced here: 67.6 us
  starting transfers between devices  23.7 us (35%)
  waiting for transfers between devices  22.4 us (33%)
  Pallas kernels  20.1 us (30%)
  local copies, waits for them, and re-layouts  1.17 us (2%)
    ppermute x10, waiting for transfers between devices, shifted(): return lax.ppermute(value, axis, pairs)  22.4 us
    ppermute x10, starting transfers between devices, shifted(): return lax.ppermute(value, axis, pairs)  15.7 us
    pallas_call x2, Pallas kernels, shards(): call(functools.partial(main_kernel, short_count, block_no, last), out_sha...  12.2 us
    ppermute x4, starting transfers between devices, permuted(): return lax.ppermute(value, 'seq', moves)  8.07 us
    pallas_call x1, Pallas kernels, shards(): pl.pallas_call(functools.partial(first_kernel, short_count), out_shape=[t...  2.5 us
    pallas_call x1, Pallas kernels, shards(): pl.pallas_call(functools.partial(start_kernel, short_count, half_rows), o...  2.41 us
    pallas_call x2, Pallas kernels, shards(): call(functools.partial(near_kernel, short_count, block_no, 0), half_shape...  2 us
  transfers between devices with their start and end apart: 14, of which 6 were waited for; matrix products, arithmetic and copies ran while one was open for 0% of the time, Pallas kernels for 8%

profile of v8, /device:TPU:2, one launch (start us, length us, event | category | flops | bytes accessed | tf_op | source)
XLA Modules:
  0.0 67.6 jit_solution(12095681750219311311)
XLA Ops:
  0.0 2.5 %first.1 = (bf16[32,4096]{1,0:T(8,128)(2,1)}, bf16[32,4096]{1,0:T(8,128)(2,1)}, bf16[16,4096]{1,0:T(8,128)(2,1)}, bf16[16,4096]{1,0:T(8,128)(2,1)}, bf16[16,4096]{1,0:T(8,128)(2,1)}) custom-call(bf16[304,4096]{1,0:T(8,128)(2,1)} %near.1), custom_call_target="tpu_custom_call" | custom-call | tf_op jit(solution)/shard_map/first/pallas_call | solution.py:264
  2.5 2.0 %collective-permute-start.1 = (bf16[32,4096]{1,0:T(8,128)(2,1)}, bf16[32,4096]{1,0:T(8,128)(2,1)S(1)}, u32[]{:S(2)}, u32[]{:S(2)}) collective-permute-start(bf16[32,4096]{1,0:T(8,128)(2,1)} %get-tuple-element.45), channel_id=1, source_target_pairs={{0,2},{1,3},{2,4},{3,5},{4,6},{5,7},{6,8},{7,9},{8,10},{9,11},{10,... | collective-permute-start | bytes 786440 | tf_op jit(solution)/shard_map/ppermute | solution.py:28
  4.5 5.4 %collective-permute-start.2 = (bf16[16,4096]{1,0:T(8,128)(2,1)}, bf16[16,4096]{1,0:T(8,128)(2,1)S(1)}, u32[]{:S(2)}, u32[]{:S(2)}) collective-permute-start(bf16[16,4096]{1,0:T(8,128)(2,1)} %get-tuple-element.46), channel_id=1, source_target_pairs={{0,12},{1,13},{2,14},{3,15},{4,0},{5,1},{6,2},{7,3},{8,20},{9,21},... | collective-permute-start | bytes 393224 | tf_op jit(solution)/shard_map/ppermute | solution.py:221
  9.9 2.1 %collective-permute-start = (bf16[32,4096]{1,0:T(8,128)(2,1)}, bf16[32,4096]{1,0:T(8,128)(2,1)S(1)}, u32[]{:S(2)}, u32[]{:S(2)}) collective-permute-start(bf16[32,4096]{1,0:T(8,128)(2,1)} %get-tuple-element.38), channel_id=1, source_target_pairs={{0,1},{1,2},{2,3},{3,4},{4,5},{5,6},{6,7},{7,8},{8,9},{9,10},{10,1... | collective-permute-start | bytes 786440 | tf_op jit(solution)/shard_map/ppermute | solution.py:28
  12.1 1.6 %collective-permute-start.5 = (bf16[16,4096]{1,0:T(8,128)(2,1)}, bf16[16,4096]{1,0:T(8,128)(2,1)S(1)}, u32[]{:S(2)}, u32[]{:S(2)}) collective-permute-start(bf16[16,4096]{1,0:T(8,128)(2,1)} %get-tuple-element.49), channel_id=1, source_target_pairs={{0,16},{1,17},{2,18},{3,19},{4,20},{5,21},{6,22},{7,23},{8,24},{9,... | collective-permute-start | bytes 393224 | tf_op jit(solution)/shard_map/ppermute | solution.py:28
  13.6 2.9 %collective-permute-start.6 = (bf16[16,4096]{1,0:T(8,128)(2,1)}, bf16[16,4096]{1,0:T(8,128)(2,1)S(1)}, u32[]{:S(2)}, u32[]{:S(2)}) collective-permute-start(bf16[16,4096]{1,0:T(8,128)(2,1)} %get-tuple-element.50), channel_id=1, source_target_pairs={{0,32},{1,33},{2,34},{3,35},{4,36},{5,37},{6,38},{7,39},{8,40},{9,... | collective-permute-start | bytes 393224 | tf_op jit(solution)/shard_map/ppermute | solution.py:28
  16.6 1.1 %copy-done.2 = bf16[2,608,304]{1,2,0:T(8,128)(2,1)S(1)} copy-done((bf16[2,608,304]{1,2,0:T(8,128)(2,1)S(1)}, bf16[2,608,304]{1,2,0:T(8,128)(2,1)}, u32[]{:S(2)}) %copy-start.2) | copy-done | bytes 739352
  17.7 2.4 %start.1 = (bf16[608,304]{1,0:T(8,128)(2,1)S(1)}, bf16[608,304]{1,0:T(8,128)(2,1)S(1)}, f32[304,8]{1,0:T(8,128)S(1)}, f32[608,8]{1,0:T(8,128)S(1)}, bf16[208,204...) custom-call(bf16[2,304,608]{2,1,0:T(8,128)(2,1)S(1)} %bitcast.1, f32[2,608]{1,0:T(2,128)S(1)} %copy-done.3, ...), custom_call_target="tpu_custom_call" | custom-call | tf_op jit(solution)/shard_map/start/pallas_call | solution.py:274
  20.1 1.2 %collective-permute-start.4 = (bf16[16,4096]{1,0:T(8,128)(2,1)S(1)}, bf16[16,4096]{1,0:T(8,128)(2,1)S(1)}, u32[]{:S(2)}, u32[]{:S(2)}) collective-permute-start(bf16[16,4096]{1,0:T(8,128)(2,1)S(1)} %collective-permute-done.2), channel_id=1, source_target_pairs={{12,8},{13,9},{14,10},{15,11},{0,12},{1,13},{2,14},{3,15},{20,16},... | collective-permute-start | bytes 393224 | tf_op jit(solution)/shard_map/ppermute | solution.py:221
  21.3 1.3 %collective-permute-start.3 = (bf16[16,4096]{1,0:T(8,128)(2,1)S(1)}, bf16[16,4096]{1,0:T(8,128)(2,1)S(1)}, u32[]{:S(2)}, u32[]{:S(2)}) collective-permute-start(bf16[16,4096]{1,0:T(8,128)(2,1)S(1)} %slice.8), channel_id=1, source_target_pairs={{0,2},{1,3},{2,4},{3,5},{4,6},{5,7},{6,8},{7,9},{8,10},{9,11},{10,... | collective-permute-start | bytes 393224 | tf_op jit(solution)/shard_map/ppermute | solution.py:28
  22.6 2.1 %collective-permute-done.refs_0_.refs_6_ = bf16[32,4096]{1,0:T(8,128)(2,1)S(1)} collective-permute-done((bf16[32,4096]{1,0:T(8,128)(2,1)}, bf16[32,4096]{1,0:T(8,128)(2,1)S(1)}, u32[]{:S(2)}, u32[]{:S(2)}) %collective-permute-start) | collective-permute-done | bytes 262176 | tf_op jit(solution)/shard_map/ppermute | solution.py:28
  24.7 1.0 %low.2 = (bf16[208,2048]{1,0:T(8,128)(2,1)S(1)}, f32[8,2048]{1,0:T(8,128)S(1)}, bf16[608,2048]{1,0:T(8,128)(2,1)S(1)}) custom-call(bf16[304,4096]{1,0:T(8,128)(2,1)S(1)} %copy-done, f32[304,8]{1,0:T(8,128)S(1)} %get-tuple-element.36.columns.refs_12_, bf16[608,304]{1,0:T(8,128)(2,1)S(1)} %get-tuple-element.37.w_in.refs_14_, ...), custom_call_target="tpu_custom_call" | custom-call | flops 1 | bytes 1 | tf_op jit(solution)/shard_map/low/pallas_call | solution.py:292
  25.7 2.5 %collective-permute-done.5.refs_10_ = bf16[16,4096]{1,0:T(8,128)(2,1)S(1)} collective-permute-done((bf16[16,4096]{1,0:T(8,128)(2,1)}, bf16[16,4096]{1,0:T(8,128)(2,1)S(1)}, u32[]{:S(2)}, u32[]{:S(2)}) %collective-permute-start.5) | collective-permute-done | bytes 131104 | tf_op jit(solution)/shard_map/ppermute | solution.py:28
  28.1 3.5 %collective-permute-done.6.refs_11_ = bf16[16,4096]{1,0:T(8,128)(2,1)S(1)} collective-permute-done((bf16[16,4096]{1,0:T(8,128)(2,1)}, bf16[16,4096]{1,0:T(8,128)(2,1)S(1)}, u32[]{:S(2)}, u32[]{:S(2)}) %collective-permute-start.6) | collective-permute-done | bytes 131104 | tf_op jit(solution)/shard_map/ppermute | solution.py:28
  31.7 5.6 %main.2 = (bf16[208,4096]{1,0:T(8,128)(2,1)S(1)}, bf16[32,4096]{1,0:T(8,128)(2,1)S(1)}, bf16[32,4096]{1,0:T(8,128)(2,1)S(1)}, bf16[16,4096]{1,0:T(8,128)(2,1)S(1...) custom-call(bf16[208,2048]{1,0:T(8,128)(2,1)S(1)} %get-tuple-element.39.refs_0_, ...), custom_call_target="tpu_custom_call" | custom-call | flops 1 | bytes 1 | tf_op jit(solution)/shard_map/main/pallas_call | solution.py:302
  37.4 1.8 %collective-permute-start.7 = (bf16[32,4096]{1,0:T(8,128)(2,1)S(1)}, bf16[32,4096]{1,0:T(8,128)(2,1)S(1)}, u32[]{:S(2)}, u32[]{:S(2)}) collective-permute-start(bf16[32,4096]{1,0:T(8,128)(2,1)S(1)} %get-tuple-element.54), channel_id=1, source_target_pairs={{0,1},{1,2},{2,3},{3,4},{4,5},{5,6},{6,7},{7,8},{8,9},{9,10},{10,1... | collective-permute-start | bytes 786440 | tf_op jit(solution)/shard_map/ppermute | solution.py:28
  39.8 3.0 %collective-permute-start.13 = (bf16[16,4096]{1,0:T(8,128)(2,1)S(1)}, bf16[16,4096]{1,0:T(8,128)(2,1)S(1)}, u32[]{:S(2)}, u32[]{:S(2)}) collective-permute-start(bf16[16,4096]{1,0:T(8,128)(2,1)S(1)} %get-tuple-element.66), channel_id=1, source_target_pairs={{0,32},{1,33},{2,34},{3,35},{4,36},{5,37},{6,38},{7,39},{8,40},{9,... | collective-permute-start | bytes 393224 | tf_op jit(solution)/shard_map/ppermute | solution.py:28
  42.8 1.0 %high.1 = (bf16[208,2048]{1,0:T(8,128)(2,1)S(1)}, f32[8,2048]{1,0:T(8,128)S(1)}, bf16[608,2048]{1,0:T(8,128)(2,1)S(1)}) custom-call(bf16[208,4096]{1,0:T(8,128)(2,1)S(1)} %get-tuple-element.52.near, f32[304,8]{1,0:T(8,128)S(1)} %get-tuple-element.36.columns.refs_12_, bf16[608,304]{1,0:T(8,128)(2,1)S(1)} %get-tuple-element.53.w_in.refs_14_), custom_call_target="tpu_custom_call" | custom-call | flops 1 | bytes 1 | tf_op jit(solution)/shard_map/high/pallas_call | solution.py:288
  43.8 1.4 %collective-permute-start.11 = (bf16[16,4096]{1,0:T(8,128)(2,1)S(1)}, bf16[16,4096]{1,0:T(8,128)(2,1)S(1)}, u32[]{:S(2)}, u32[]{:S(2)}) collective-permute-start(bf16[16,4096]{1,0:T(8,128)(2,1)S(1)} %collective-permute-done.9), channel_id=1, source_target_pairs={{12,8},{13,9},{14,10},{15,11},{0,12},{1,13},{2,14},{3,15},{20,16},... | collective-permute-start | bytes 393224 | tf_op jit(solution)/shard_map/ppermute | solution.py:221
  45.2 5.0 %collective-permute-done.8.refs_7_ = bf16[32,4096]{1,0:T(8,128)(2,1)S(1)} collective-permute-done((bf16[32,4096]{1,0:T(8,128)(2,1)S(1)}, bf16[32,4096]{1,0:T(8,128)(2,1)S(1)}, u32[]{:S(2)}, u32[]{:S(2)}) %collective-permute-start.8) | collective-permute-done | bytes 262176 | tf_op jit(solution)/shard_map/ppermute | solution.py:28
  50.5 3.7 %collective-permute-done.7.refs_0_.refs_6_ = bf16[32,4096]{1,0:T(8,128)(2,1)S(1)} collective-permute-done((bf16[32,4096]{1,0:T(8,128)(2,1)S(1)}, bf16[32,4096]{1,0:T(8,128)(2,1)S(1)}, u32[]{:S(2)}, u32[]{:S(2)}) %collective-permute-start.7) | collective-permute-done | bytes 262176 | tf_op jit(solution)/shard_map/ppermute | solution.py:28
  54.2 1.0 %low.3 = (bf16[208,2048]{1,0:T(8,128)(2,1)S(1)}, f32[8,2048]{1,0:T(8,128)S(1)}, bf16[608,2048]{1,0:T(8,128)(2,1)S(1)}) custom-call(bf16[208,4096]{1,0:T(8,128)(2,1)S(1)} %get-tuple-element.52.near, f32[304,8]{1,0:T(8,128)S(1)} %get-tuple-element.36.columns.refs_12_, bf16[608,304]{1,0:T(8,128)(2,1)S(1)} %get-tuple-element.53.w_in.refs_14_, ...), custom_call_target="tpu_custom_call" | custom-call | flops 1 | bytes 1 | tf_op jit(solution)/shard_map/low/pallas_call | solution.py:292
  55.2 5.6 %collective-permute-done.12.refs_10_ = bf16[16,4096]{1,0:T(8,128)(2,1)S(1)} collective-permute-done((bf16[16,4096]{1,0:T(8,128)(2,1)S(1)}, bf16[16,4096]{1,0:T(8,128)(2,1)S(1)}, u32[]{:S(2)}, u32[]{:S(2)}) %collective-permute-start.12) | collective-permute-done | bytes 131104 | tf_op jit(solution)/shard_map/ppermute | solution.py:28
  60.9 6.6 %main.3 = bf16[304,4096]{1,0:T(8,128)(2,1)} custom-call(bf16[208,2048]{1,0:T(8,128)(2,1)S(1)} %get-tuple-element.55.refs_0_, f32[8,2048]{1,0:T(8,128)S(1)} %get-tuple-element.56.refs_1_, bf16[608,2048]{1,0:T(8,128)(2,1)S(1)} %get-tuple-element.57.refs_2_, bf16[208,2048]{1,0:T(8,128)(2,1)S(1)} %get-tuple-element.58.refs_3_, ...), custom_call_target="tpu_custom_call" | custom-call | flops 1 | bytes 1 | tf_op jit(solution)/shard_map/main/pallas_call | solution.py:302
  (25 shorter events, 1.1 us)
Async XLA Ops:
  0.0 16.5 %copy-start = (bf16[304,4096]{1,0:T(8,128)(2,1)S(1)}, bf16[304,4096]{1,0:T(8,128)(2,1)}, u32[]{:S(2)}) copy-start(bf16[304,4096]{1,0:T(8,128)(2,1)} %near.1) | copy-start | bytes 7471108
  0.0 16.5 %copy-start.5 = (f32[2,304]{1,0:T(2,128)S(1)}, f32[2,304]{1,0:T(2,128)}, u32[]{:S(2)}) copy-start(f32[2,304]{1,0:T(2,128)} %last_bias.1) | copy-start | bytes 7300
  0.0 16.5 %copy-start.3 = (f32[2,608]{1,0:T(2,128)S(1)}, f32[2,608]{1,0:T(2,128)}, u32[]{:S(2)}) copy-start(f32[2,608]{1,0:T(2,128)} %bias.1) | copy-start | bytes 14596
  0.0 16.5 %copy-start.4 = (f32[2,304]{1,0:T(2,128)S(1)}, f32[2,304]{1,0:T(2,128)}, u32[]{:S(2)}) copy-start(f32[2,304]{1,0:T(2,128)} %gain.1) | copy-start | bytes 7300
  2.5 18.8 %collective-permute-start.1 = (bf16[32,4096]{1,0:T(8,128)(2,1)}, bf16[32,4096]{1,0:T(8,128)(2,1)S(1)}, u32[]{:S(2)}, u32[]{:S(2)}) collective-permute-start(bf16[32,4096]{1,0:T(8,128)(2,1)} %get-tuple-element.45), channel_id=1, source_target_pairs={{0,2},{1,3},{2,4},{3,5},{4,6},{5,7},{6,8},{7,9},{8,10},{9,11},{10,... | collective-permute-start | bytes 786440 | tf_op jit(solution)/shard_map/ppermute | solution.py:28
  4.5 15.6 %collective-permute-start.2 = (bf16[16,4096]{1,0:T(8,128)(2,1)}, bf16[16,4096]{1,0:T(8,128)(2,1)S(1)}, u32[]{:S(2)}, u32[]{:S(2)}) collective-permute-start(bf16[16,4096]{1,0:T(8,128)(2,1)} %get-tuple-element.46), channel_id=1, source_target_pairs={{0,12},{1,13},{2,14},{3,15},{4,0},{5,1},{6,2},{7,3},{8,20},{9,21},... | collective-permute-start | bytes 393224 | tf_op jit(solution)/shard_map/ppermute | solution.py:221
  9.9 14.7 %collective-permute-start = (bf16[32,4096]{1,0:T(8,128)(2,1)}, bf16[32,4096]{1,0:T(8,128)(2,1)S(1)}, u32[]{:S(2)}, u32[]{:S(2)}) collective-permute-start(bf16[32,4096]{1,0:T(8,128)(2,1)} %get-tuple-element.38), channel_id=1, source_target_pairs={{0,1},{1,2},{2,3},{3,4},{4,5},{5,6},{6,7},{7,8},{8,9},{9,10},{10,1... | collective-permute-start | bytes 786440 | tf_op jit(solution)/shard_map/ppermute | solution.py:28
  12.1 16.1 %collective-permute-start.5 = (bf16[16,4096]{1,0:T(8,128)(2,1)}, bf16[16,4096]{1,0:T(8,128)(2,1)S(1)}, u32[]{:S(2)}, u32[]{:S(2)}) collective-permute-start(bf16[16,4096]{1,0:T(8,128)(2,1)} %get-tuple-element.49), channel_id=1, source_target_pairs={{0,16},{1,17},{2,18},{3,19},{4,20},{5,21},{6,22},{7,23},{8,24},{9,... | collective-permute-start | bytes 393224 | tf_op jit(solution)/shard_map/ppermute | solution.py:28
  13.6 18.0 %collective-permute-start.6 = (bf16[16,4096]{1,0:T(8,128)(2,1)}, bf16[16,4096]{1,0:T(8,128)(2,1)S(1)}, u32[]{:S(2)}, u32[]{:S(2)}) collective-permute-start(bf16[16,4096]{1,0:T(8,128)(2,1)} %get-tuple-element.50), channel_id=1, source_target_pairs={{0,32},{1,33},{2,34},{3,35},{4,36},{5,37},{6,38},{7,39},{8,40},{9,... | collective-permute-start | bytes 393224 | tf_op jit(solution)/shard_map/ppermute | solution.py:28
  16.5 1.1 %copy-start.2 = (bf16[2,608,304]{1,2,0:T(8,128)(2,1)S(1)}, bf16[2,608,304]{1,2,0:T(8,128)(2,1)}, u32[]{:S(2)}) copy-start(bf16[2,608,304]{1,2,0:T(8,128)(2,1)} %param.8) | copy-start | bytes 2217988
  20.1 11.6 %copy-start.1 = (bf16[2,304,608]{2,1,0:T(8,128)(2,1)S(1)}, bf16[2,304,608]{2,1,0:T(8,128)(2,1)}, u32[]{:S(2)}) copy-start(bf16[2,304,608]{2,1,0:T(8,128)(2,1)} %refs_15_.3) | copy-start | bytes 2217988
  20.1 11.5 %collective-permute-start.4 = (bf16[16,4096]{1,0:T(8,128)(2,1)S(1)}, bf16[16,4096]{1,0:T(8,128)(2,1)S(1)}, u32[]{:S(2)}, u32[]{:S(2)}) collective-permute-start(bf16[16,4096]{1,0:T(8,128)(2,1)S(1)} %collective-permute-done.2), channel_id=1, source_target_pairs={{12,8},{13,9},{14,10},{15,11},{0,12},{1,13},{2,14},{3,15},{20,16},... | collective-permute-start | bytes 393224 | tf_op jit(solution)/shard_map/ppermute | solution.py:221
  21.3 10.3 %collective-permute-start.3 = (bf16[16,4096]{1,0:T(8,128)(2,1)S(1)}, bf16[16,4096]{1,0:T(8,128)(2,1)S(1)}, u32[]{:S(2)}, u32[]{:S(2)}) collective-permute-start(bf16[16,4096]{1,0:T(8,128)(2,1)S(1)} %slice.8), channel_id=1, source_target_pairs={{0,2},{1,3},{2,4},{3,5},{4,6},{5,7},{6,8},{7,9},{8,10},{9,11},{10,... | collective-permute-start | bytes 393224 | tf_op jit(solution)/shard_map/ppermute | solution.py:28
  37.2 12.9 %collective-permute-start.8 = (bf16[32,4096]{1,0:T(8,128)(2,1)S(1)}, bf16[32,4096]{1,0:T(8,128)(2,1)S(1)}, u32[]{:S(2)}, u32[]{:S(2)}) collective-permute-start(bf16[32,4096]{1,0:T(8,128)(2,1)S(1)} %get-tuple-element.61), channel_id=1, source_target_pairs={{0,2},{1,3},{2,4},{3,5},{4,6},{5,7},{6,8},{7,9},{8,10},{9,11},{10,... | collective-permute-start | bytes 786440 | tf_op jit(solution)/shard_map/ppermute | solution.py:28
  37.3 6.5 %collective-permute-start.9 = (bf16[16,4096]{1,0:T(8,128)(2,1)S(1)}, bf16[16,4096]{1,0:T(8,128)(2,1)S(1)}, u32[]{:S(2)}, u32[]{:S(2)}) collective-permute-start(bf16[16,4096]{1,0:T(8,128)(2,1)S(1)} %get-tuple-element.62), channel_id=1, source_target_pairs={{0,12},{1,13},{2,14},{3,15},{4,0},{5,1},{6,2},{7,3},{8,20},{9,21},... | collective-permute-start | bytes 393224 | tf_op jit(solution)/shard_map/ppermute | solution.py:221
  37.4 16.8 %collective-permute-start.7 = (bf16[32,4096]{1,0:T(8,128)(2,1)S(1)}, bf16[32,4096]{1,0:T(8,128)(2,1)S(1)}, u32[]{:S(2)}, u32[]{:S(2)}) collective-permute-start(bf16[32,4096]{1,0:T(8,128)(2,1)S(1)} %get-tuple-element.54), channel_id=1, source_target_pairs={{0,1},{1,2},{2,3},{3,4},{4,5},{5,6},{6,7},{7,8},{8,9},{9,10},{10,1... | collective-permute-start | bytes 786440 | tf_op jit(solution)/shard_map/ppermute | solution.py:28
  39.2 21.7 %collective-permute-start.12 = (bf16[16,4096]{1,0:T(8,128)(2,1)S(1)}, bf16[16,4096]{1,0:T(8,128)(2,1)S(1)}, u32[]{:S(2)}, u32[]{:S(2)}) collective-permute-start(bf16[16,4096]{1,0:T(8,128)(2,1)S(1)} %get-tuple-element.65), channel_id=1, source_target_pairs={{0,16},{1,17},{2,18},{3,19},{4,20},{5,21},{6,22},{7,23},{8,24},{9,... | collective-permute-start | bytes 393224 | tf_op jit(solution)/shard_map/ppermute | solution.py:28
  39.8 21.1 %collective-permute-start.13 = (bf16[16,4096]{1,0:T(8,128)(2,1)S(1)}, bf16[16,4096]{1,0:T(8,128)(2,1)S(1)}, u32[]{:S(2)}, u32[]{:S(2)}) collective-permute-start(bf16[16,4096]{1,0:T(8,128)(2,1)S(1)} %get-tuple-element.66), channel_id=1, source_target_pairs={{0,32},{1,33},{2,34},{3,35},{4,36},{5,37},{6,38},{7,39},{8,40},{9,... | collective-permute-start | bytes 393224 | tf_op jit(solution)/shard_map/ppermute | solution.py:28
  43.8 17.0 %collective-permute-start.11 = (bf16[16,4096]{1,0:T(8,128)(2,1)S(1)}, bf16[16,4096]{1,0:T(8,128)(2,1)S(1)}, u32[]{:S(2)}, u32[]{:S(2)}) collective-permute-start(bf16[16,4096]{1,0:T(8,128)(2,1)S(1)} %collective-permute-done.9), channel_id=1, source_target_pairs={{12,8},{13,9},{14,10},{15,11},{0,12},{1,13},{2,14},{3,15},{20,16},... | collective-permute-start | bytes 393224 | tf_op jit(solution)/shard_map/ppermute | solution.py:221
  50.2 10.7 %collective-permute-start.10 = (bf16[16,4096]{1,0:T(8,128)(2,1)S(1)}, bf16[16,4096]{1,0:T(8,128)(2,1)S(1)}, u32[]{:S(2)}, u32[]{:S(2)}) collective-permute-start(bf16[16,4096]{1,0:T(8,128)(2,1)S(1)} %slice.9), channel_id=1, source_target_pairs={{0,2},{1,3},{2,4},{3,5},{4,6},{5,7},{6,8},{7,9},{8,10},{9,11},{10,... | collective-permute-start | bytes 393224 | tf_op jit(solution)/shard_map/ppermute | solution.py:28

commit v9 on v8

--- a/solution.py
+++ b/solution.py
@@ -100,29 +100,36 @@
 
 
 def start_kernel(short_count, half_rows, transposed, bias, gain, last_bias, tokens, *refs):
-    outs, high, made, sems = refs[:4], refs[4:7], refs[7:11], refs[11:]
+    outs, high, made, sems = refs[:4], refs[4:7], refs[7:11], refs[11:15]
+    loaded, load_sems = refs[15:17], refs[17:19]
     depth, hidden = transposed.shape[1:]
-    copies = []
+    loads, copies = [], []
     for block_no in range(BLOCKS):
-        made[block_no][...] = jnp.transpose(transposed[block_no])
-        copies.append(pltpu.make_async_copy(made[block_no], outs[block_no], sems[block_no]))
+        loads.append(pltpu.make_async_copy(transposed.at[block_no], loaded[block_no], load_sems[block_no]))
+        loads[-1].start()
+
+    def send(at):
+        copies.append(pltpu.make_async_copy(made[at], outs[at], sems[at]))
         copies[-1].start()
+
     columns = [gain[...], last_bias[...], jnp.zeros((8 - 2 * BLOCKS, depth), F32)]
     made[2][...] = jnp.transpose(jnp.concatenate(columns, 0))
     made[3][...] = jnp.transpose(jnp.concatenate([bias[...], jnp.zeros((8 - BLOCKS, hidden), F32)], 0))
-    for at in (2, 3):
-        copies.append(pltpu.make_async_copy(made[at], outs[at], sems[at]))
-        copies[-1].start()
-    near_kernel(short_count, 0, half_rows, tokens, made[2], made[0], *high)
+    send(2)
+    send(3)
+    near_rotate(short_count, half_rows, tokens, None, high[0], high[1])
+    for block_no in range(BLOCKS):
+        loads[block_no].wait()
+        made[block_no][...] = jnp.transpose(loaded[block_no][...])
+        send(block_no)
+        if block_no == 0:
+            near_product(0, made[2], made[0], high[0], high[2])
     for copy in copies:
         copy.wait()
 
 
-def near_kernel(short_count, block_no, first, near, columns, w_in, *refs):
-    halo_in = refs[0]
-    rotated, squares, partial = refs[-3:]
-    near_rows, width = rotated.shape
-    gain = columns[:near_rows, block_no : block_no + 1]
+def near_rotate(short_count, first, near, halo_in, rotated, squares):
+    width = rotated.shape[1]
 
     def track(t, begin, end):
         return near[t * TRACK_CH : (t + 1) * TRACK_CH, begin:end]
@@ -133,18 +140,27 @@
     for at in range(0, width, NEAR_TILE):
         begin, end = first + at, first + at + NEAR_TILE
         total = jnp.zeros((8, NEAR_TILE), F32)
-        scaled = []
         for t in range(1 + short_count):
-            rows = slice(t * TRACK_CH, (t + 1) * TRACK_CH)
             piece = track(0, begin, end) if t == 0 else rotated_piece(track, halo, t - 1, begin, end)
-            rotated[rows, at : at + NEAR_TILE] = piece
+            rotated[t * TRACK_CH : (t + 1) * TRACK_CH, at : at + NEAR_TILE] = piece
             piece = piece.astype(F32)
             total = total + (piece[:8] * piece[:8] + piece[8:] * piece[8:])
-            scaled.append((piece * gain[rows]).astype(BF16))
         squares[:, at : at + NEAR_TILE] = total
-        partial[:, at : at + NEAR_TILE] = jnp.dot(
-            w_in[:, :near_rows], jnp.concatenate(scaled, 0), preferred_element_type=F32
-        ).astype(BF16)
+
+
+def near_product(block_no, columns, w_in, rotated, partial):
+    near_rows, width = rotated.shape
+    gain = columns[:near_rows, block_no : block_no + 1]
+    for at in range(0, width, NEAR_TILE):
+        here = slice(at, at + NEAR_TILE)
+        scaled = (rotated[:, here].astype(F32) * gain).astype(BF16)
+        partial[:, here] = jnp.dot(w_in[:, :near_rows], scaled, preferred_element_type=F32).astype(BF16)
+
+
+def near_kernel(short_count, block_no, first, near, columns, w_in, *refs):
+    rotated, squares, partial = refs[-3:]
+    near_rotate(short_count, first, near, refs[0], rotated, squares)
+    near_product(block_no, columns, w_in, rotated, partial)
 
 
 def main_kernel(short_count, block_no, last, *refs):
@@ -239,9 +255,10 @@
     eight = permuted(eight, to_middle)
     duo = shifted(duo, "seq", 2)
     pair = shifted(pair, "seq", 1)
-    back = shifted(thirty_two, "seq", 32)
+    back = shifted(thirty_two, "seq", -16)
     sixteen = shifted(sixteen, "seq", 16)
     four = shifted(after(duo[TRACK_CH:], eight), "seq", 2)
+    back = shifted(after(back, duo), "seq", -16)
     eight = permuted(after(eight, *fill), from_middle)
     return pair, [duo, four, eight, sixteen, back]
 
@@ -274,12 +291,15 @@
     *w_ins, columns, hidden_columns, rotated, squares, partial = pl.pallas_call(
         functools.partial(start_kernel, short_count, half_rows),
         out_shape=[jax.ShapeDtypeStruct(*entry) for entry in made] + half_shapes,
-        in_specs=[VMEM] * 5,
+        in_specs=[pl.BlockSpec(memory_space=pltpu.HBM)] + [VMEM] * 4,
         out_specs=[pl.BlockSpec(memory_space=pltpu.HBM)] * 4 + [VMEM] * 3,
-        scratch_shapes=[pltpu.VMEM(*entry) for entry in made] + [pltpu.SemaphoreType.DMA] * 4,
+        scratch_shapes=[pltpu.VMEM(*entry) for entry in made]
+        + [pltpu.SemaphoreType.DMA] * 4
+        + [pltpu.VMEM((width, hidden), BF16)] * BLOCKS
+        + [pltpu.SemaphoreType.DMA] * BLOCKS,
         compiler_params=pltpu.CompilerParams(vmem_limit_bytes=16 << 20),
         name="start",
-    )(jnp.swapaxes(in_weight, 1, 2), in_bias, norm_gain, out_bias, tokens)
+    )(pltpu.with_memory_space_constraint(jnp.swapaxes(in_weight, 1, 2), pltpu.HBM), in_bias, norm_gain, out_bias, tokens)
     high = [rotated, squares, partial]
     near = tokens
     for block_no in range(BLOCKS):

time: 67.7 us -> 64.4 us (0.951); the launches traced: 67.6 us -> 63.3 us
  waiting for transfers between devices: 22.4 us -> 11 us
  starting transfers between devices: 23.7 us -> 31 us
  local copies, waits for them, and re-layouts: 1.17 us -> 0.04 us
  Pallas kernels: 20.1 us -> 20.9 us
    ppermute x10 -> x12, waiting for transfers between devices: 22.4 us -> 11 us  [shifted(): return lax.ppermute(value, axis, pairs)]
    ppermute x10 -> x12, starting transfers between devices: 15.7 us -> 20.7 us  [shifted(): return lax.ppermute(value, axis, pairs)]
    ppermute x4, starting transfers between devices: 8.07 us -> 10.3 us  [permuted(): return lax.ppermute(value, 'seq', moves)]
    unnamed x12 -> x10, local copies, waits for them, and re-layouts: 1.15 us -> 0.02 us
  transfers between devices with their start and end apart: 14 -> 16, of which waited for: 6 -> 5; matrix products, arithmetic and copies ran while one was open for 0% -> 0% of each run, Pallas kernels for 8% -> 10%
where the time goes in v9:
time: 64.4 us; the launch traced here: 63.3 us
  starting transfers between devices  31 us (48%)
  Pallas kernels  20.9 us (32%)
  waiting for transfers between devices  11 us (17%)
    ppermute x12, starting transfers between devices, shifted(): return lax.ppermute(value, axis, pairs)  20.7 us
    pallas_call x2, Pallas kernels, shards(): call(functools.partial(main_kernel, short_count, block_no, last), out_sha...  12.2 us
    ppermute x12, waiting for transfers between devices, shifted(): return lax.ppermute(value, axis, pairs)  11 us
    ppermute x4, starting transfers between devices, permuted(): return lax.ppermute(value, 'seq', moves)  10.3 us
    pallas_call x1, Pallas kernels, shards(): pl.pallas_call(functools.partial(start_kernel, short_count, half_rows), o...  2.89 us
    pallas_call x1, Pallas kernels, shards(): pl.pallas_call(functools.partial(first_kernel, short_count), out_shape=[t...  2.51 us
    pallas_call x2, Pallas kernels, shards(): call(functools.partial(near_kernel, short_count, block_no, 0), half_shape...  2.28 us
  transfers between devices with their start and end apart: 16, of which 5 were waited for; matrix products, arithmetic and copies ran while one was open for 0% of the time, Pallas kernels for 10%

profile of v9, /device:TPU:2, one launch (start us, length us, event | category | flops | bytes accessed | tf_op | source)
XLA Modules:
  0.0 63.3 jit_solution(4842779824468520251)
XLA Ops:
  0.0 2.5 %first.1 = (bf16[32,4096]{1,0:T(8,128)(2,1)}, bf16[32,4096]{1,0:T(8,128)(2,1)}, bf16[16,4096]{1,0:T(8,128)(2,1)}, bf16[16,4096]{1,0:T(8,128)(2,1)}, bf16[16,4096]{1,0:T(8,128)(2,1)}) custom-call(bf16[304,4096]{1,0:T(8,128)(2,1)} %near.1), custom_call_target="tpu_custom_call" | custom-call | tf_op jit(solution)/shard_map/first/pallas_call | solution.py:281
  2.5 2.0 %collective-permute-start.1 = (bf16[32,4096]{1,0:T(8,128)(2,1)}, bf16[32,4096]{1,0:T(8,128)(2,1)S(1)}, u32[]{:S(2)}, u32[]{:S(2)}) collective-permute-start(bf16[32,4096]{1,0:T(8,128)(2,1)} %get-tuple-element.47), channel_id=1, source_target_pairs={{0,2},{1,3},{2,4},{3,5},{4,6},{5,7},{6,8},{7,9},{8,10},{9,11},{10,... | collective-permute-start | bytes 786440 | tf_op jit(solution)/shard_map/ppermute | solution.py:28
  4.5 5.4 %collective-permute-start.2 = (bf16[16,4096]{1,0:T(8,128)(2,1)}, bf16[16,4096]{1,0:T(8,128)(2,1)S(1)}, u32[]{:S(2)}, u32[]{:S(2)}) collective-permute-start(bf16[16,4096]{1,0:T(8,128)(2,1)} %get-tuple-element.48), channel_id=1, source_target_pairs={{0,12},{1,13},{2,14},{3,15},{4,0},{5,1},{6,2},{7,3},{8,20},{9,21},... | collective-permute-start | bytes 393224 | tf_op jit(solution)/shard_map/ppermute | solution.py:237
  9.9 3.0 %collective-permute-start.6 = (bf16[16,4096]{1,0:T(8,128)(2,1)}, bf16[16,4096]{1,0:T(8,128)(2,1)S(1)}, u32[]{:S(2)}, u32[]{:S(2)}) collective-permute-start(bf16[16,4096]{1,0:T(8,128)(2,1)} %get-tuple-element.52), channel_id=1, source_target_pairs={{0,48},{1,49},{2,50},{3,51},{4,52},{5,53},{6,54},{7,55},{8,56},{9,... | collective-permute-start | bytes 393224 | tf_op jit(solution)/shard_map/ppermute | solution.py:28
  13.0 2.1 %collective-permute-start = (bf16[32,4096]{1,0:T(8,128)(2,1)}, bf16[32,4096]{1,0:T(8,128)(2,1)S(1)}, u32[]{:S(2)}, u32[]{:S(2)}) collective-permute-start(bf16[32,4096]{1,0:T(8,128)(2,1)} %get-tuple-element.40), channel_id=1, source_target_pairs={{0,1},{1,2},{2,3},{3,4},{4,5},{5,6},{6,7},{7,8},{8,9},{9,10},{10,1... | collective-permute-start | bytes 786440 | tf_op jit(solution)/shard_map/ppermute | solution.py:28
  15.1 2.9 %start.1 = (bf16[608,304]{1,0:T(8,128)(2,1)S(1)}, bf16[608,304]{1,0:T(8,128)(2,1)S(1)}, f32[304,8]{1,0:T(8,128)S(1)}, f32[608,8]{1,0:T(8,128)S(1)}, bf16[208,204...) custom-call(bf16[2,304,608]{2,1,0:T(8,128)(2,1)} %bitcast.1, f32[2,608]{1,0:T(2,128)S(1)} %copy-done.2, ...), custom_call_target="tpu_custom_call" | custom-call | tf_op jit(solution)/shard_map/start/pallas_call | solution.py:291
  18.0 2.0 %collective-permute-start.4 = (bf16[16,4096]{1,0:T(8,128)(2,1)S(1)}, bf16[16,4096]{1,0:T(8,128)(2,1)S(1)}, u32[]{:S(2)}, u32[]{:S(2)}) collective-permute-start(bf16[16,4096]{1,0:T(8,128)(2,1)S(1)} %collective-permute-done.2), channel_id=1, source_target_pairs={{12,8},{13,9},{14,10},{15,11},{0,12},{1,13},{2,14},{3,15},{20,16},... | collective-permute-start | bytes 393224 | tf_op jit(solution)/shard_map/ppermute | solution.py:237
  20.7 2.9 %collective-permute-start.7 = (bf16[16,4096]{1,0:T(8,128)(2,1)S(1)}, bf16[16,4096]{1,0:T(8,128)(2,1)S(1)}, u32[]{:S(2)}, u32[]{:S(2)}) collective-permute-start(bf16[16,4096]{1,0:T(8,128)(2,1)S(1)} %collective-permute-done.6), channel_id=1, source_target_pairs={{0,48},{1,49},{2,50},{3,51},{4,52},{5,53},{6,54},{7,55},{8,56},{9,... | collective-permute-start | bytes 393224 | tf_op jit(solution)/shard_map/ppermute | solution.py:28
  23.6 3.3 %collective-permute-done.refs_0_.refs_6_ = bf16[32,4096]{1,0:T(8,128)(2,1)S(1)} collective-permute-done((bf16[32,4096]{1,0:T(8,128)(2,1)}, bf16[32,4096]{1,0:T(8,128)(2,1)S(1)}, u32[]{:S(2)}, u32[]{:S(2)}) %collective-permute-start) | collective-permute-done | bytes 262176 | tf_op jit(solution)/shard_map/ppermute | solution.py:28
  26.9 1.1 %low.2 = (bf16[208,2048]{1,0:T(8,128)(2,1)S(1)}, f32[8,2048]{1,0:T(8,128)S(1)}, bf16[608,2048]{1,0:T(8,128)(2,1)S(1)}) custom-call(bf16[304,4096]{1,0:T(8,128)(2,1)S(1)} %copy-done, f32[304,8]{1,0:T(8,128)S(1)} %get-tuple-element.38.columns.refs_12_, bf16[608,304]{1,0:T(8,128)(2,1)S(1)} %get-tuple-element.39.w_in.refs_14_, ...), custom_call_target="tpu_custom_call" | custom-call | flops 1 | bytes 1 | tf_op jit(solution)/shard_map/low/pallas_call | solution.py:312
  28.0 1.9 %collective-permute-done.5.refs_10_ = bf16[16,4096]{1,0:T(8,128)(2,1)S(1)} collective-permute-done((bf16[16,4096]{1,0:T(8,128)(2,1)}, bf16[16,4096]{1,0:T(8,128)(2,1)S(1)}, u32[]{:S(2)}, u32[]{:S(2)}) %collective-permute-start.5) | collective-permute-done | bytes 131104 | tf_op jit(solution)/shard_map/ppermute | solution.py:28
  29.9 5.6 %main.2 = (bf16[208,4096]{1,0:T(8,128)(2,1)S(1)}, bf16[32,4096]{1,0:T(8,128)(2,1)S(1)}, bf16[32,4096]{1,0:T(8,128)(2,1)S(1)}, bf16[16,4096]{1,0:T(8,128)(2,1)S(1...) custom-call(bf16[208,2048]{1,0:T(8,128)(2,1)S(1)} %get-tuple-element.41.refs_0_, ...), custom_call_target="tpu_custom_call" | custom-call | flops 1 | bytes 1 | tf_op jit(solution)/shard_map/main/pallas_call | solution.py:322
  35.6 0.8 %collective-permute-start.10 = (bf16[16,4096]{1,0:T(8,128)(2,1)S(1)}, bf16[16,4096]{1,0:T(8,128)(2,1)S(1)}, u32[]{:S(2)}, u32[]{:S(2)}) collective-permute-start(bf16[16,4096]{1,0:T(8,128)(2,1)S(1)} %get-tuple-element.65), channel_id=1, source_target_pairs={{0,12},{1,13},{2,14},{3,15},{4,0},{5,1},{6,2},{7,3},{8,20},{9,21},... | collective-permute-start | bytes 393224 | tf_op jit(solution)/shard_map/ppermute | solution.py:237
  36.4 2.9 %collective-permute-start.14 = (bf16[16,4096]{1,0:T(8,128)(2,1)S(1)}, bf16[16,4096]{1,0:T(8,128)(2,1)S(1)}, u32[]{:S(2)}, u32[]{:S(2)}) collective-permute-start(bf16[16,4096]{1,0:T(8,128)(2,1)S(1)} %get-tuple-element.69), channel_id=1, source_target_pairs={{0,48},{1,49},{2,50},{3,51},{4,52},{5,53},{6,54},{7,55},{8,56},{9,... | collective-permute-start | bytes 393224 | tf_op jit(solution)/shard_map/ppermute | solution.py:28
  39.3 2.1 %collective-permute-start.8 = (bf16[32,4096]{1,0:T(8,128)(2,1)S(1)}, bf16[32,4096]{1,0:T(8,128)(2,1)S(1)}, u32[]{:S(2)}, u32[]{:S(2)}) collective-permute-start(bf16[32,4096]{1,0:T(8,128)(2,1)S(1)} %get-tuple-element.57), channel_id=1, source_target_pairs={{0,1},{1,2},{2,3},{3,4},{4,5},{5,6},{6,7},{7,8},{8,9},{9,10},{10,1... | collective-permute-start | bytes 786440 | tf_op jit(solution)/shard_map/ppermute | solution.py:28
  41.4 1.1 %high.1 = (bf16[208,2048]{1,0:T(8,128)(2,1)S(1)}, f32[8,2048]{1,0:T(8,128)S(1)}, bf16[608,2048]{1,0:T(8,128)(2,1)S(1)}) custom-call(bf16[208,4096]{1,0:T(8,128)(2,1)S(1)} %get-tuple-element.55.near, f32[304,8]{1,0:T(8,128)S(1)} %get-tuple-element.38.columns.refs_12_, bf16[608,304]{1,0:T(8,128)(2,1)S(1)} %get-tuple-element.56.w_in.refs_14_), custom_call_target="tpu_custom_call" | custom-call | flops 1 | bytes 1 | tf_op jit(solution)/shard_map/high/pallas_call | solution.py:308
  42.5 2.0 %collective-permute-start.12 = (bf16[16,4096]{1,0:T(8,128)(2,1)S(1)}, bf16[16,4096]{1,0:T(8,128)(2,1)S(1)}, u32[]{:S(2)}, u32[]{:S(2)}) collective-permute-start(bf16[16,4096]{1,0:T(8,128)(2,1)S(1)} %collective-permute-done.10), channel_id=1, source_target_pairs={{12,8},{13,9},{14,10},{15,11},{0,12},{1,13},{2,14},{3,15},{20,16},... | collective-permute-start | bytes 393224 | tf_op jit(solution)/shard_map/ppermute | solution.py:237
  44.6 0.8 %collective-permute-done.9.refs_7_ = bf16[32,4096]{1,0:T(8,128)(2,1)S(1)} collective-permute-done((bf16[32,4096]{1,0:T(8,128)(2,1)S(1)}, bf16[32,4096]{1,0:T(8,128)(2,1)S(1)}, u32[]{:S(2)}, u32[]{:S(2)}) %collective-permute-start.9) | collective-permute-done | bytes 262176 | tf_op jit(solution)/shard_map/ppermute | solution.py:28
  45.4 2.0 %collective-permute-start.11 = (bf16[16,4096]{1,0:T(8,128)(2,1)S(1)}, bf16[16,4096]{1,0:T(8,128)(2,1)S(1)}, u32[]{:S(2)}, u32[]{:S(2)}) collective-permute-start(bf16[16,4096]{1,0:T(8,128)(2,1)S(1)} %slice.9), channel_id=1, source_target_pairs={{0,2},{1,3},{2,4},{3,5},{4,6},{5,7},{6,8},{7,9},{8,10},{9,11},{10,... | collective-permute-start | bytes 393224 | tf_op jit(solution)/shard_map/ppermute | solution.py:28
  47.4 3.0 %collective-permute-start.15 = (bf16[16,4096]{1,0:T(8,128)(2,1)S(1)}, bf16[16,4096]{1,0:T(8,128)(2,1)S(1)}, u32[]{:S(2)}, u32[]{:S(2)}) collective-permute-start(bf16[16,4096]{1,0:T(8,128)(2,1)S(1)} %collective-permute-done.14), channel_id=1, source_target_pairs={{0,48},{1,49},{2,50},{3,51},{4,52},{5,53},{6,54},{7,55},{8,56},{9,... | collective-permute-start | bytes 393224 | tf_op jit(solution)/shard_map/ppermute | solution.py:28
  50.4 2.0 %collective-permute-done.8.refs_0_.refs_6_ = bf16[32,4096]{1,0:T(8,128)(2,1)S(1)} collective-permute-done((bf16[32,4096]{1,0:T(8,128)(2,1)S(1)}, bf16[32,4096]{1,0:T(8,128)(2,1)S(1)}, u32[]{:S(2)}, u32[]{:S(2)}) %collective-permute-start.8) | collective-permute-done | bytes 262176 | tf_op jit(solution)/shard_map/ppermute | solution.py:28
  52.4 1.1 %low.3 = (bf16[208,2048]{1,0:T(8,128)(2,1)S(1)}, f32[8,2048]{1,0:T(8,128)S(1)}, bf16[608,2048]{1,0:T(8,128)(2,1)S(1)}) custom-call(bf16[208,4096]{1,0:T(8,128)(2,1)S(1)} %get-tuple-element.55.near, f32[304,8]{1,0:T(8,128)S(1)} %get-tuple-element.38.columns.refs_12_, bf16[608,304]{1,0:T(8,128)(2,1)S(1)} %get-tuple-element.56.w_in.refs_14_, ...), custom_call_target="tpu_custom_call" | custom-call | flops 1 | bytes 1 | tf_op jit(solution)/shard_map/low/pallas_call | solution.py:312
  53.6 2.9 %collective-permute-done.13.refs_10_ = bf16[16,4096]{1,0:T(8,128)(2,1)S(1)} collective-permute-done((bf16[16,4096]{1,0:T(8,128)(2,1)S(1)}, bf16[16,4096]{1,0:T(8,128)(2,1)S(1)}, u32[]{:S(2)}, u32[]{:S(2)}) %collective-permute-start.13) | collective-permute-done | bytes 131104 | tf_op jit(solution)/shard_map/ppermute | solution.py:28
  56.5 6.6 %main.3 = bf16[304,4096]{1,0:T(8,128)(2,1)} custom-call(bf16[208,2048]{1,0:T(8,128)(2,1)S(1)} %get-tuple-element.58.refs_0_, f32[8,2048]{1,0:T(8,128)S(1)} %get-tuple-element.59.refs_1_, bf16[608,2048]{1,0:T(8,128)(2,1)S(1)} %get-tuple-element.60.refs_2_, bf16[208,2048]{1,0:T(8,128)(2,1)S(1)} %get-tuple-element.61.refs_3_, ...), custom_call_target="tpu_custom_call" | custom-call | flops 1 | bytes 1 | tf_op jit(solution)/shard_map/main/pallas_call | solution.py:322
  (27 shorter events, 0.8 us)
Async XLA Ops:
  0.0 15.1 %copy-start = (bf16[304,4096]{1,0:T(8,128)(2,1)S(1)}, bf16[304,4096]{1,0:T(8,128)(2,1)}, u32[]{:S(2)}) copy-start(bf16[304,4096]{1,0:T(8,128)(2,1)} %near.1) | copy-start | bytes 7471108
  0.0 15.1 %copy-start.4 = (f32[2,304]{1,0:T(2,128)S(1)}, f32[2,304]{1,0:T(2,128)}, u32[]{:S(2)}) copy-start(f32[2,304]{1,0:T(2,128)} %last_bias.1) | copy-start | bytes 7300
  0.0 15.1 %copy-start.2 = (f32[2,608]{1,0:T(2,128)S(1)}, f32[2,608]{1,0:T(2,128)}, u32[]{:S(2)}) copy-start(f32[2,608]{1,0:T(2,128)} %bias.1) | copy-start | bytes 14596
  0.0 15.1 %copy-start.3 = (f32[2,304]{1,0:T(2,128)S(1)}, f32[2,304]{1,0:T(2,128)}, u32[]{:S(2)}) copy-start(f32[2,304]{1,0:T(2,128)} %gain.1) | copy-start | bytes 7300
  2.5 17.5 %collective-permute-start.1 = (bf16[32,4096]{1,0:T(8,128)(2,1)}, bf16[32,4096]{1,0:T(8,128)(2,1)S(1)}, u32[]{:S(2)}, u32[]{:S(2)}) collective-permute-start(bf16[32,4096]{1,0:T(8,128)(2,1)} %get-tuple-element.47), channel_id=1, source_target_pairs={{0,2},{1,3},{2,4},{3,5},{4,6},{5,7},{6,8},{7,9},{8,10},{9,11},{10,... | collective-permute-start | bytes 786440 | tf_op jit(solution)/shard_map/ppermute | solution.py:28
  4.5 13.5 %collective-permute-start.2 = (bf16[16,4096]{1,0:T(8,128)(2,1)}, bf16[16,4096]{1,0:T(8,128)(2,1)S(1)}, u32[]{:S(2)}, u32[]{:S(2)}) collective-permute-start(bf16[16,4096]{1,0:T(8,128)(2,1)} %get-tuple-element.48), channel_id=1, source_target_pairs={{0,12},{1,13},{2,14},{3,15},{4,0},{5,1},{6,2},{7,3},{8,20},{9,21},... | collective-permute-start | bytes 393224 | tf_op jit(solution)/shard_map/ppermute | solution.py:237
  9.9 10.1 %collective-permute-start.6 = (bf16[16,4096]{1,0:T(8,128)(2,1)}, bf16[16,4096]{1,0:T(8,128)(2,1)S(1)}, u32[]{:S(2)}, u32[]{:S(2)}) collective-permute-start(bf16[16,4096]{1,0:T(8,128)(2,1)} %get-tuple-element.52), channel_id=1, source_target_pairs={{0,48},{1,49},{2,50},{3,51},{4,52},{5,53},{6,54},{7,55},{8,56},{9,... | collective-permute-start | bytes 393224 | tf_op jit(solution)/shard_map/ppermute | solution.py:28
  13.0 13.9 %collective-permute-start = (bf16[32,4096]{1,0:T(8,128)(2,1)}, bf16[32,4096]{1,0:T(8,128)(2,1)S(1)}, u32[]{:S(2)}, u32[]{:S(2)}) collective-permute-start(bf16[32,4096]{1,0:T(8,128)(2,1)} %get-tuple-element.40), channel_id=1, source_target_pairs={{0,1},{1,2},{2,3},{3,4},{4,5},{5,6},{6,7},{7,8},{8,9},{9,10},{10,1... | collective-permute-start | bytes 786440 | tf_op jit(solution)/shard_map/ppermute | solution.py:28
  15.1 14.8 %collective-permute-start.5 = (bf16[16,4096]{1,0:T(8,128)(2,1)}, bf16[16,4096]{1,0:T(8,128)(2,1)S(1)}, u32[]{:S(2)}, u32[]{:S(2)}) collective-permute-start(bf16[16,4096]{1,0:T(8,128)(2,1)} %get-tuple-element.51), channel_id=1, source_target_pairs={{0,16},{1,17},{2,18},{3,19},{4,20},{5,21},{6,22},{7,23},{8,24},{9,... | collective-permute-start | bytes 393224 | tf_op jit(solution)/shard_map/ppermute | solution.py:28
  18.0 11.9 %copy-start.1 = (bf16[2,304,608]{2,1,0:T(8,128)(2,1)S(1)}, bf16[2,304,608]{2,1,0:T(8,128)(2,1)}, u32[]{:S(2)}) copy-start(bf16[2,304,608]{2,1,0:T(8,128)(2,1)} %refs_15_.3) | copy-start | bytes 2217988
  18.0 11.9 %collective-permute-start.4 = (bf16[16,4096]{1,0:T(8,128)(2,1)S(1)}, bf16[16,4096]{1,0:T(8,128)(2,1)S(1)}, u32[]{:S(2)}, u32[]{:S(2)}) collective-permute-start(bf16[16,4096]{1,0:T(8,128)(2,1)S(1)} %collective-permute-done.2), channel_id=1, source_target_pairs={{12,8},{13,9},{14,10},{15,11},{0,12},{1,13},{2,14},{3,15},{20,16},... | collective-permute-start | bytes 393224 | tf_op jit(solution)/shard_map/ppermute | solution.py:237
  20.0 9.9 %collective-permute-start.3 = (bf16[16,4096]{1,0:T(8,128)(2,1)S(1)}, bf16[16,4096]{1,0:T(8,128)(2,1)S(1)}, u32[]{:S(2)}, u32[]{:S(2)}) collective-permute-start(bf16[16,4096]{1,0:T(8,128)(2,1)S(1)} %slice.8), channel_id=1, source_target_pairs={{0,2},{1,3},{2,4},{3,5},{4,6},{5,7},{6,8},{7,9},{8,10},{9,11},{10,... | collective-permute-start | bytes 393224 | tf_op jit(solution)/shard_map/ppermute | solution.py:28
  20.7 9.2 %collective-permute-start.7 = (bf16[16,4096]{1,0:T(8,128)(2,1)S(1)}, bf16[16,4096]{1,0:T(8,128)(2,1)S(1)}, u32[]{:S(2)}, u32[]{:S(2)}) collective-permute-start(bf16[16,4096]{1,0:T(8,128)(2,1)S(1)} %collective-permute-done.6), channel_id=1, source_target_pairs={{0,48},{1,49},{2,50},{3,51},{4,52},{5,53},{6,54},{7,55},{8,56},{9,... | collective-permute-start | bytes 393224 | tf_op jit(solution)/shard_map/ppermute | solution.py:28
  35.5 9.9 %collective-permute-start.9 = (bf16[32,4096]{1,0:T(8,128)(2,1)S(1)}, bf16[32,4096]{1,0:T(8,128)(2,1)S(1)}, u32[]{:S(2)}, u32[]{:S(2)}) collective-permute-start(bf16[32,4096]{1,0:T(8,128)(2,1)S(1)} %get-tuple-element.64), channel_id=1, source_target_pairs={{0,2},{1,3},{2,4},{3,5},{4,6},{5,7},{6,8},{7,9},{8,10},{9,11},{10,... | collective-permute-start | bytes 786440 | tf_op jit(solution)/shard_map/ppermute | solution.py:28
  35.6 6.9 %collective-permute-start.10 = (bf16[16,4096]{1,0:T(8,128)(2,1)S(1)}, bf16[16,4096]{1,0:T(8,128)(2,1)S(1)}, u32[]{:S(2)}, u32[]{:S(2)}) collective-permute-start(bf16[16,4096]{1,0:T(8,128)(2,1)S(1)} %get-tuple-element.65), channel_id=1, source_target_pairs={{0,12},{1,13},{2,14},{3,15},{4,0},{5,1},{6,2},{7,3},{8,20},{9,21},... | collective-permute-start | bytes 393224 | tf_op jit(solution)/shard_map/ppermute | solution.py:237
  36.4 8.2 %collective-permute-start.14 = (bf16[16,4096]{1,0:T(8,128)(2,1)S(1)}, bf16[16,4096]{1,0:T(8,128)(2,1)S(1)}, u32[]{:S(2)}, u32[]{:S(2)}) collective-permute-start(bf16[16,4096]{1,0:T(8,128)(2,1)S(1)} %get-tuple-element.69), channel_id=1, source_target_pairs={{0,48},{1,49},{2,50},{3,51},{4,52},{5,53},{6,54},{7,55},{8,56},{9,... | collective-permute-start | bytes 393224 | tf_op jit(solution)/shard_map/ppermute | solution.py:28
  39.3 13.2 %collective-permute-start.8 = (bf16[32,4096]{1,0:T(8,128)(2,1)S(1)}, bf16[32,4096]{1,0:T(8,128)(2,1)S(1)}, u32[]{:S(2)}, u32[]{:S(2)}) collective-permute-start(bf16[32,4096]{1,0:T(8,128)(2,1)S(1)} %get-tuple-element.57), channel_id=1, source_target_pairs={{0,1},{1,2},{2,3},{3,4},{4,5},{5,6},{6,7},{7,8},{8,9},{9,10},{10,1... | collective-permute-start | bytes 786440 | tf_op jit(solution)/shard_map/ppermute | solution.py:28
  41.4 15.1 %collective-permute-start.13 = (bf16[16,4096]{1,0:T(8,128)(2,1)S(1)}, bf16[16,4096]{1,0:T(8,128)(2,1)S(1)}, u32[]{:S(2)}, u32[]{:S(2)}) collective-permute-start(bf16[16,4096]{1,0:T(8,128)(2,1)S(1)} %get-tuple-element.68), channel_id=1, source_target_pairs={{0,16},{1,17},{2,18},{3,19},{4,20},{5,21},{6,22},{7,23},{8,24},{9,... | collective-permute-start | bytes 393224 | tf_op jit(solution)/shard_map/ppermute | solution.py:28
  42.5 14.0 %collective-permute-start.12 = (bf16[16,4096]{1,0:T(8,128)(2,1)S(1)}, bf16[16,4096]{1,0:T(8,128)(2,1)S(1)}, u32[]{:S(2)}, u32[]{:S(2)}) collective-permute-start(bf16[16,4096]{1,0:T(8,128)(2,1)S(1)} %collective-permute-done.10), channel_id=1, source_target_pairs={{12,8},{13,9},{14,10},{15,11},{0,12},{1,13},{2,14},{3,15},{20,16},... | collective-permute-start | bytes 393224 | tf_op jit(solution)/shard_map/ppermute | solution.py:237
  45.4 11.1 %collective-permute-start.11 = (bf16[16,4096]{1,0:T(8,128)(2,1)S(1)}, bf16[16,4096]{1,0:T(8,128)(2,1)S(1)}, u32[]{:S(2)}, u32[]{:S(2)}) collective-permute-start(bf16[16,4096]{1,0:T(8,128)(2,1)S(1)} %slice.9), channel_id=1, source_target_pairs={{0,2},{1,3},{2,4},{3,5},{4,6},{5,7},{6,8},{7,9},{8,10},{9,11},{10,... | collective-permute-start | bytes 393224 | tf_op jit(solution)/shard_map/ppermute | solution.py:28
  47.4 9.1 %collective-permute-start.15 = (bf16[16,4096]{1,0:T(8,128)(2,1)S(1)}, bf16[16,4096]{1,0:T(8,128)(2,1)S(1)}, u32[]{:S(2)}, u32[]{:S(2)}) collective-permute-start(bf16[16,4096]{1,0:T(8,128)(2,1)S(1)} %collective-permute-done.14), channel_id=1, source_target_pairs={{0,48},{1,49},{2,50},{3,51},{4,52},{5,53},{6,54},{7,55},{8,56},{9,... | collective-permute-start | bytes 393224 | tf_op jit(solution)/shard_map/ppermute | solution.py:28

commit v10 on v9

--- a/solution.py
+++ b/solution.py
@@ -73,13 +73,13 @@
 
 
 def first_kernel(short_count, tokens, *refs):
-    pair, duo, far = refs[0], refs[1], refs[2:5]
-    tail, sems = refs[5], refs[6:]
+    pair, far = refs[0], refs[1:6]
+    tail, sems = refs[6], refs[7:]
     near_rows, half_rows = tail.shape
     local_rows = pair.shape[1]
     base = local_rows - half_rows
     copies = [pltpu.make_async_copy(tokens.at[:near_rows, base:], tail, sems[0])]
-    for at, target in enumerate([pair.at[TRACK_CH:, :], duo.at[:TRACK_CH, :], duo.at[TRACK_CH:, :], *far]):
+    for at, target in enumerate([pair.at[TRACK_CH:, :], *far]):
         top = near_rows + at * TRACK_CH
         copies.append(
             pltpu.make_async_copy(tokens.at[top : top + TRACK_CH, :], target, sems[1 + at])
@@ -204,9 +204,8 @@
         else:
             outs[0][:, begin:end] = near_out
             outs[1][TRACK_CH:, begin:end] = far_out[:TRACK_CH]
-            outs[2][:, begin:end] = far_out[TRACK_CH : 3 * TRACK_CH]
-            for at in range(3):
-                outs[3 + at][:, begin:end] = far_out[(3 + at) * TRACK_CH : (4 + at) * TRACK_CH]
+            for at in range(len(far)):
+                outs[2 + at][:, begin:end] = far_out[(1 + at) * TRACK_CH : (2 + at) * TRACK_CH]
     for copy in copies:
         copy.wait()
     if not last:
@@ -249,18 +248,18 @@
     return first, second
 
 
-def exchange(pair, duo, far, fill):
-    eight, sixteen, thirty_two = far
+def exchange(pair, far, fill):
+    two, four, eight, sixteen, thirty_two = far
     to_middle, from_middle = routes()
     eight = permuted(eight, to_middle)
-    duo = shifted(duo, "seq", 2)
     pair = shifted(pair, "seq", 1)
     back = shifted(thirty_two, "seq", -16)
-    sixteen = shifted(sixteen, "seq", 16)
-    four = shifted(after(duo[TRACK_CH:], eight), "seq", 2)
-    back = shifted(after(back, duo), "seq", -16)
+    four = shifted(four, "seq", 4)
+    two = shifted(two, "seq", 2)
     eight = permuted(after(eight, *fill), from_middle)
-    return pair, [duo, four, eight, sixteen, back]
+    back = shifted(back, "seq", -16)
+    sixteen = shifted(after(sixteen, two), "seq", 16)
+    return pair, [two, four, eight, sixteen, back]
 
 
 def shards(tokens, norm_gain, in_weight, in_bias, out_weight, out_bias):
@@ -278,11 +277,11 @@
         jax.ShapeDtypeStruct((8, half_rows), F32),
         jax.ShapeDtypeStruct((hidden, half_rows), BF16),
     ]
-    pair, duo, *far = pl.pallas_call(
+    pair, *far = pl.pallas_call(
         functools.partial(first_kernel, short_count),
-        out_shape=[two] * 2 + [one] * (far_count - 2),
+        out_shape=[two] + [one] * far_count,
         in_specs=[pl.BlockSpec(memory_space=pl.ANY)],
-        out_specs=[VMEM] * far_count,
+        out_specs=[VMEM] * (1 + far_count),
         scratch_shapes=[pltpu.VMEM((near_rows, local_rows // 2), BF16)]
         + [pltpu.SemaphoreType.DMA] * (2 + far_count),
         name="first",
@@ -308,13 +307,13 @@
             high = call(
                 functools.partial(near_kernel, short_count, block_no, half_rows), half_shapes, [VMEM] * 3, "high", 8
             )(near, columns, w_ins[block_no])
-        pair, moved = exchange(pair, duo, far, [high[1]])
+        pair, moved = exchange(pair, far, [high[1]])
         low = call(functools.partial(near_kernel, short_count, block_no, 0), half_shapes, [VMEM] * 4, "low", 8)(
             near, columns, w_ins[block_no], pair
         )
         out_shape = [jax.ShapeDtypeStruct((width, local_rows), BF16)]
         if not last:
-            out_shape = [near_shape, two, two] + [one] * (far_count - 2)
+            out_shape = [near_shape, two] + [one] * far_count
         out_specs, scratch = [VMEM] * len(out_shape), []
         if last:
             out_specs = [pl.BlockSpec(memory_space=pltpu.HBM)]
@@ -324,7 +323,7 @@
         )(*low, *high, pair, *moved, columns, hidden_columns, w_ins[block_no], out_weight)
         if last:
             return outs[0]
-        near, pair, duo, far = outs[0], outs[1], outs[2], outs[3:]
+        near, pair, far = outs[0], outs[1], outs[2:]
 
 
 def solution(mesh):

time: 64.4 us -> 64.5 us (level)
  starting transfers between devices: 31 us -> 33.7 us
  waiting for transfers between devices: 11 us -> 8.54 us
    ppermute x4, starting transfers between devices: 10.3 us -> 15.7 us  [permuted(): return lax.ppermute(value, 'seq', moves)]
    ppermute x12, waiting for transfers between devices: 11 us -> 8.16 us  [shifted(): return lax.ppermute(value, axis, pairs)]
    ppermute x12, starting transfers between devices: 20.7 us -> 18 us  [shifted(): return lax.ppermute(value, axis, pairs)]
  transfers between devices with their start and end apart: 16 -> 16, of which waited for: 5 -> 7; matrix products, arithmetic and copies ran while one was open for 0% -> 0% of each run, Pallas kernels for 10% -> 10%
where the time goes in v10:
time: 64.5 us; the launch traced here: 63.6 us
  starting transfers between devices  33.7 us (52%)
  Pallas kernels  21 us (33%)
  waiting for transfers between devices  8.54 us (13%)
    ppermute x12, starting transfers between devices, shifted(): return lax.ppermute(value, axis, pairs)  18 us
    ppermute x4, starting transfers between devices, permuted(): return lax.ppermute(value, 'seq', moves)  15.7 us
    pallas_call x2, Pallas kernels, shards(): call(functools.partial(main_kernel, short_count, block_no, last), out_sha...  12.2 us
    ppermute x12, waiting for transfers between devices, shifted(): return lax.ppermute(value, axis, pairs)  8.16 us
    pallas_call x1, Pallas kernels, shards(): pl.pallas_call(functools.partial(start_kernel, short_count, half_rows), o...  2.9 us
    pallas_call x1, Pallas kernels, shards(): pl.pallas_call(functools.partial(first_kernel, short_count), out_shape=[t...  2.48 us
    pallas_call x2, Pallas kernels, shards(): call(functools.partial(near_kernel, short_count, block_no, 0), half_shape...  2.28 us
  transfers between devices with their start and end apart: 16, of which 7 were waited for; matrix products, arithmetic and copies ran while one was open for 0% of the time, Pallas kernels for 10%

profile of v10, /device:TPU:2, one launch (start us, length us, event | category | flops | bytes accessed | tf_op | source)
XLA Modules:
  0.0 63.6 jit_solution(12884029922554084687)
XLA Ops:
  0.0 2.5 %first.1 = (bf16[32,4096]{1,0:T(8,128)(2,1)}, bf16[16,4096]{1,0:T(8,128)(2,1)}, bf16[16,4096]{1,0:T(8,128)(2,1)}, bf16[16,4096]{1,0:T(8,128)(2,1)}, bf16[16,4096]{1,0:T(8,128)(2,1)}, /*index=5*/bf16[16,4096]{1,0:T(8,128)(2,1)}) custom-call(bf16[304,4096]{1,0:T(8,128)(2,1)} %near.1), custom_call_target="tpu_custom_call" | custom-call | tf_op jit(solution)/shard_map/first/pallas_call | solution.py:280
  2.5 2.0 %collective-permute-start.1 = (bf16[16,4096]{1,0:T(8,128)(2,1)}, bf16[16,4096]{1,0:T(8,128)(2,1)S(1)}, u32[]{:S(2)}, u32[]{:S(2)}) collective-permute-start(bf16[16,4096]{1,0:T(8,128)(2,1)} %get-tuple-element.47), channel_id=1, source_target_pairs={{0,2},{1,3},{2,4},{3,5},{4,6},{5,7},{6,8},{7,9},{8,10},{9,11},{10,... | collective-permute-start | bytes 393224 | tf_op jit(solution)/shard_map/ppermute | solution.py:28
  4.5 5.4 %collective-permute-start.3 = (bf16[16,4096]{1,0:T(8,128)(2,1)}, bf16[16,4096]{1,0:T(8,128)(2,1)S(1)}, u32[]{:S(2)}, u32[]{:S(2)}) collective-permute-start(bf16[16,4096]{1,0:T(8,128)(2,1)} %get-tuple-element.49), channel_id=1, source_target_pairs={{0,12},{1,13},{2,14},{3,15},{4,0},{5,1},{6,2},{7,3},{8,20},{9,21},... | collective-permute-start | bytes 393224 | tf_op jit(solution)/shard_map/ppermute | solution.py:236
  9.9 2.1 %collective-permute-start = (bf16[32,4096]{1,0:T(8,128)(2,1)}, bf16[32,4096]{1,0:T(8,128)(2,1)S(1)}, u32[]{:S(2)}, u32[]{:S(2)}) collective-permute-start(bf16[32,4096]{1,0:T(8,128)(2,1)} %get-tuple-element.40), channel_id=1, source_target_pairs={{0,1},{1,2},{2,3},{3,4},{4,5},{5,6},{6,7},{7,8},{8,9},{9,10},{10,1... | collective-permute-start | bytes 786440 | tf_op jit(solution)/shard_map/ppermute | solution.py:28
  12.0 3.0 %collective-permute-start.6 = (bf16[16,4096]{1,0:T(8,128)(2,1)}, bf16[16,4096]{1,0:T(8,128)(2,1)S(1)}, u32[]{:S(2)}, u32[]{:S(2)}) collective-permute-start(bf16[16,4096]{1,0:T(8,128)(2,1)} %get-tuple-element.53), channel_id=1, source_target_pairs={{0,48},{1,49},{2,50},{3,51},{4,52},{5,53},{6,54},{7,55},{8,56},{9,... | collective-permute-start | bytes 393224 | tf_op jit(solution)/shard_map/ppermute | solution.py:28
  15.1 2.9 %start.1 = (bf16[608,304]{1,0:T(8,128)(2,1)S(1)}, bf16[608,304]{1,0:T(8,128)(2,1)S(1)}, f32[304,8]{1,0:T(8,128)S(1)}, f32[608,8]{1,0:T(8,128)S(1)}, bf16[208,204...) custom-call(bf16[2,304,608]{2,1,0:T(8,128)(2,1)} %bitcast.1, f32[2,608]{1,0:T(2,128)S(1)} %copy-done.2, ...), custom_call_target="tpu_custom_call" | custom-call | tf_op jit(solution)/shard_map/start/pallas_call | solution.py:290
  18.1 3.3 %collective-permute-start.7 = (bf16[16,4096]{1,0:T(8,128)(2,1)S(1)}, bf16[16,4096]{1,0:T(8,128)(2,1)S(1)}, u32[]{:S(2)}, u32[]{:S(2)}) collective-permute-start(bf16[16,4096]{1,0:T(8,128)(2,1)S(1)} %collective-permute-done.6), channel_id=1, source_target_pairs={{0,48},{1,49},{2,50},{3,51},{4,52},{5,53},{6,54},{7,55},{8,56},{9,... | collective-permute-start | bytes 393224 | tf_op jit(solution)/shard_map/ppermute | solution.py:28
  21.4 3.6 %collective-permute-start.4 = (bf16[16,4096]{1,0:T(8,128)(2,1)S(1)}, bf16[16,4096]{1,0:T(8,128)(2,1)S(1)}, u32[]{:S(2)}, u32[]{:S(2)}) collective-permute-start(bf16[16,4096]{1,0:T(8,128)(2,1)S(1)} %collective-permute-done.3), channel_id=1, source_target_pairs={{12,8},{13,9},{14,10},{15,11},{0,12},{1,13},{2,14},{3,15},{20,16},... | collective-permute-start | bytes 393224 | tf_op jit(solution)/shard_map/ppermute | solution.py:236
  25.0 1.7 %collective-permute-done.refs_0_.refs_6_ = bf16[32,4096]{1,0:T(8,128)(2,1)S(1)} collective-permute-done((bf16[32,4096]{1,0:T(8,128)(2,1)}, bf16[32,4096]{1,0:T(8,128)(2,1)S(1)}, u32[]{:S(2)}, u32[]{:S(2)}) %collective-permute-start) | collective-permute-done | bytes 262176 | tf_op jit(solution)/shard_map/ppermute | solution.py:28
  26.7 1.1 %low.2 = (bf16[208,2048]{1,0:T(8,128)(2,1)S(1)}, f32[8,2048]{1,0:T(8,128)S(1)}, bf16[608,2048]{1,0:T(8,128)(2,1)S(1)}) custom-call(bf16[304,4096]{1,0:T(8,128)(2,1)S(1)} %copy-done, f32[304,8]{1,0:T(8,128)S(1)} %get-tuple-element.38.columns.refs_12_, bf16[608,304]{1,0:T(8,128)(2,1)S(1)} %get-tuple-element.39.w_in.refs_14_, ...), custom_call_target="tpu_custom_call" | custom-call | flops 1 | bytes 1 | tf_op jit(solution)/shard_map/low/pallas_call | solution.py:311
  27.8 1.1 %collective-permute-done.5.refs_10_ = bf16[16,4096]{1,0:T(8,128)(2,1)S(1)} collective-permute-done((bf16[16,4096]{1,0:T(8,128)(2,1)S(1)}, bf16[16,4096]{1,0:T(8,128)(2,1)S(1)}, u32[]{:S(2)}, u32[]{:S(2)}) %collective-permute-start.5) | collective-permute-done | bytes 131104 | tf_op jit(solution)/shard_map/ppermute | solution.py:28
  29.0 5.6 %main.2 = (bf16[208,4096]{1,0:T(8,128)(2,1)S(1)}, bf16[32,4096]{1,0:T(8,128)(2,1)S(1)}, bf16[16,4096]{1,0:T(8,128)(2,1)S(1)}, bf16[16,4096]{1,0:T(8,128)(2,1)S(1...) custom-call(bf16[208,2048]{1,0:T(8,128)(2,1)S(1)} %get-tuple-element.41.refs_0_, ...), custom_call_target="tpu_custom_call" | custom-call | flops 1 | bytes 1 | tf_op jit(solution)/shard_map/main/pallas_call | solution.py:321
  34.6 1.5 %collective-permute-start.9 = (bf16[16,4096]{1,0:T(8,128)(2,1)S(1)}, bf16[16,4096]{1,0:T(8,128)(2,1)S(1)}, u32[]{:S(2)}, u32[]{:S(2)}) collective-permute-start(bf16[16,4096]{1,0:T(8,128)(2,1)S(1)} %get-tuple-element.64), channel_id=1, source_target_pairs={{0,2},{1,3},{2,4},{3,5},{4,6},{5,7},{6,8},{7,9},{8,10},{9,11},{10,... | collective-permute-start | bytes 393224 | tf_op jit(solution)/shard_map/ppermute | solution.py:28
  36.1 3.1 %collective-permute-start.11 = (bf16[16,4096]{1,0:T(8,128)(2,1)S(1)}, bf16[16,4096]{1,0:T(8,128)(2,1)S(1)}, u32[]{:S(2)}, u32[]{:S(2)}) collective-permute-start(bf16[16,4096]{1,0:T(8,128)(2,1)S(1)} %get-tuple-element.66), channel_id=1, source_target_pairs={{0,12},{1,13},{2,14},{3,15},{4,0},{5,1},{6,2},{7,3},{8,20},{9,21},... | collective-permute-start | bytes 393224 | tf_op jit(solution)/shard_map/ppermute | solution.py:236
  39.2 1.0 %collective-permute-start.8 = (bf16[32,4096]{1,0:T(8,128)(2,1)S(1)}, bf16[32,4096]{1,0:T(8,128)(2,1)S(1)}, u32[]{:S(2)}, u32[]{:S(2)}) collective-permute-start(bf16[32,4096]{1,0:T(8,128)(2,1)S(1)} %get-tuple-element.57), channel_id=1, source_target_pairs={{0,1},{1,2},{2,3},{3,4},{4,5},{5,6},{6,7},{7,8},{8,9},{9,10},{10,1... | collective-permute-start | bytes 786440 | tf_op jit(solution)/shard_map/ppermute | solution.py:28
  40.2 1.0 %collective-permute-start.14 = (bf16[16,4096]{1,0:T(8,128)(2,1)S(1)}, bf16[16,4096]{1,0:T(8,128)(2,1)S(1)}, u32[]{:S(2)}, u32[]{:S(2)}) collective-permute-start(bf16[16,4096]{1,0:T(8,128)(2,1)S(1)} %get-tuple-element.70), channel_id=1, source_target_pairs={{0,48},{1,49},{2,50},{3,51},{4,52},{5,53},{6,54},{7,55},{8,56},{9,... | collective-permute-start | bytes 393224 | tf_op jit(solution)/shard_map/ppermute | solution.py:28
  41.8 1.1 %high.1 = (bf16[208,2048]{1,0:T(8,128)(2,1)S(1)}, f32[8,2048]{1,0:T(8,128)S(1)}, bf16[608,2048]{1,0:T(8,128)(2,1)S(1)}) custom-call(bf16[208,4096]{1,0:T(8,128)(2,1)S(1)} %get-tuple-element.55.near, f32[304,8]{1,0:T(8,128)S(1)} %get-tuple-element.38.columns.refs_12_, bf16[608,304]{1,0:T(8,128)(2,1)S(1)} %get-tuple-element.56.w_in.refs_14_), custom_call_target="tpu_custom_call" | custom-call | flops 1 | bytes 1 | tf_op jit(solution)/shard_map/high/pallas_call | solution.py:307
  43.4 1.1 %collective-permute-start.13 = (bf16[16,4096]{1,0:T(8,128)(2,1)S(1)}, bf16[16,4096]{1,0:T(8,128)(2,1)S(1)}, u32[]{:S(2)}, u32[]{:S(2)}) collective-permute-start(bf16[16,4096]{1,0:T(8,128)(2,1)S(1)} %get-tuple-element.69), channel_id=1, source_target_pairs={{0,16},{1,17},{2,18},{3,19},{4,20},{5,21},{6,22},{7,23},{8,24},{9,... | collective-permute-start | bytes 393224 | tf_op jit(solution)/shard_map/ppermute | solution.py:28
  44.5 0.7 %collective-permute-done.14 = bf16[16,4096]{1,0:T(8,128)(2,1)S(1)} collective-permute-done((bf16[16,4096]{1,0:T(8,128)(2,1)S(1)}, bf16[16,4096]{1,0:T(8,128)(2,1)S(1)}, u32[]{:S(2)}, u32[]{:S(2)}) %collective-permute-start.14) | collective-permute-done | bytes 131104 | tf_op jit(solution)/shard_map/ppermute | solution.py:28
  45.2 2.3 %collective-permute-start.15 = (bf16[16,4096]{1,0:T(8,128)(2,1)S(1)}, bf16[16,4096]{1,0:T(8,128)(2,1)S(1)}, u32[]{:S(2)}, u32[]{:S(2)}) collective-permute-start(bf16[16,4096]{1,0:T(8,128)(2,1)S(1)} %collective-permute-done.14), channel_id=1, source_target_pairs={{0,48},{1,49},{2,50},{3,51},{4,52},{5,53},{6,54},{7,55},{8,56},{9,... | collective-permute-start | bytes 393224 | tf_op jit(solution)/shard_map/ppermute | solution.py:28
  47.4 3.6 %collective-permute-start.12 = (bf16[16,4096]{1,0:T(8,128)(2,1)S(1)}, bf16[16,4096]{1,0:T(8,128)(2,1)S(1)}, u32[]{:S(2)}, u32[]{:S(2)}) collective-permute-start(bf16[16,4096]{1,0:T(8,128)(2,1)S(1)} %collective-permute-done.11), channel_id=1, source_target_pairs={{12,8},{13,9},{14,10},{15,11},{0,12},{1,13},{2,14},{3,15},{20,16},... | collective-permute-start | bytes 393224 | tf_op jit(solution)/shard_map/ppermute | solution.py:236
  51.0 3.6 %collective-permute-done.8.refs_0_.refs_6_ = bf16[32,4096]{1,0:T(8,128)(2,1)S(1)} collective-permute-done((bf16[32,4096]{1,0:T(8,128)(2,1)S(1)}, bf16[32,4096]{1,0:T(8,128)(2,1)S(1)}, u32[]{:S(2)}, u32[]{:S(2)}) %collective-permute-start.8) | collective-permute-done | bytes 262176 | tf_op jit(solution)/shard_map/ppermute | solution.py:28
  54.6 1.1 %low.3 = (bf16[208,2048]{1,0:T(8,128)(2,1)S(1)}, f32[8,2048]{1,0:T(8,128)S(1)}, bf16[608,2048]{1,0:T(8,128)(2,1)S(1)}) custom-call(bf16[208,4096]{1,0:T(8,128)(2,1)S(1)} %get-tuple-element.55.near, f32[304,8]{1,0:T(8,128)S(1)} %get-tuple-element.38.columns.refs_12_, bf16[608,304]{1,0:T(8,128)(2,1)S(1)} %get-tuple-element.56.w_in.refs_14_, ...), custom_call_target="tpu_custom_call" | custom-call | flops 1 | bytes 1 | tf_op jit(solution)/shard_map/low/pallas_call | solution.py:311
  56.8 6.6 %main.3 = bf16[304,4096]{1,0:T(8,128)(2,1)} custom-call(bf16[208,2048]{1,0:T(8,128)(2,1)S(1)} %get-tuple-element.58.refs_0_, f32[8,2048]{1,0:T(8,128)S(1)} %get-tuple-element.59.refs_1_, bf16[608,2048]{1,0:T(8,128)(2,1)S(1)} %get-tuple-element.60.refs_2_, bf16[208,2048]{1,0:T(8,128)(2,1)S(1)} %get-tuple-element.61.refs_3_, ...), custom_call_target="tpu_custom_call" | custom-call | flops 1 | bytes 1 | tf_op jit(solution)/shard_map/main/pallas_call | solution.py:321
  (27 shorter events, 2.1 us)
Async XLA Ops:
  0.0 15.1 %copy-start = (bf16[304,4096]{1,0:T(8,128)(2,1)S(1)}, bf16[304,4096]{1,0:T(8,128)(2,1)}, u32[]{:S(2)}) copy-start(bf16[304,4096]{1,0:T(8,128)(2,1)} %near.1) | copy-start | bytes 7471108
  0.0 15.1 %copy-start.4 = (f32[2,304]{1,0:T(2,128)S(1)}, f32[2,304]{1,0:T(2,128)}, u32[]{:S(2)}) copy-start(f32[2,304]{1,0:T(2,128)} %last_bias.1) | copy-start | bytes 7300
  0.0 15.1 %copy-start.2 = (f32[2,608]{1,0:T(2,128)S(1)}, f32[2,608]{1,0:T(2,128)}, u32[]{:S(2)}) copy-start(f32[2,608]{1,0:T(2,128)} %bias.1) | copy-start | bytes 14596
  0.0 15.1 %copy-start.3 = (f32[2,304]{1,0:T(2,128)S(1)}, f32[2,304]{1,0:T(2,128)}, u32[]{:S(2)}) copy-start(f32[2,304]{1,0:T(2,128)} %gain.1) | copy-start | bytes 7300
  2.5 15.5 %copy-start.5 = (bf16[16,4096]{1,0:T(8,128)(2,1)S(1)}, bf16[16,4096]{1,0:T(8,128)(2,1)}, u32[]{:S(2)}) copy-start(bf16[16,4096]{1,0:T(8,128)(2,1)} %get-tuple-element.52) | copy-start | bytes 393220
  2.5 15.5 %collective-permute-start.1 = (bf16[16,4096]{1,0:T(8,128)(2,1)}, bf16[16,4096]{1,0:T(8,128)(2,1)S(1)}, u32[]{:S(2)}, u32[]{:S(2)}) collective-permute-start(bf16[16,4096]{1,0:T(8,128)(2,1)} %get-tuple-element.47), channel_id=1, source_target_pairs={{0,2},{1,3},{2,4},{3,5},{4,6},{5,7},{6,8},{7,9},{8,10},{9,11},{10,... | collective-permute-start | bytes 393224 | tf_op jit(solution)/shard_map/ppermute | solution.py:28
  4.5 13.6 %collective-permute-start.3 = (bf16[16,4096]{1,0:T(8,128)(2,1)}, bf16[16,4096]{1,0:T(8,128)(2,1)S(1)}, u32[]{:S(2)}, u32[]{:S(2)}) collective-permute-start(bf16[16,4096]{1,0:T(8,128)(2,1)} %get-tuple-element.49), channel_id=1, source_target_pairs={{0,12},{1,13},{2,14},{3,15},{4,0},{5,1},{6,2},{7,3},{8,20},{9,21},... | collective-permute-start | bytes 393224 | tf_op jit(solution)/shard_map/ppermute | solution.py:236
  9.9 16.8 %collective-permute-start = (bf16[32,4096]{1,0:T(8,128)(2,1)}, bf16[32,4096]{1,0:T(8,128)(2,1)S(1)}, u32[]{:S(2)}, u32[]{:S(2)}) collective-permute-start(bf16[32,4096]{1,0:T(8,128)(2,1)} %get-tuple-element.40), channel_id=1, source_target_pairs={{0,1},{1,2},{2,3},{3,4},{4,5},{5,6},{6,7},{7,8},{8,9},{9,10},{10,1... | collective-permute-start | bytes 786440 | tf_op jit(solution)/shard_map/ppermute | solution.py:28
  12.0 6.1 %collective-permute-start.6 = (bf16[16,4096]{1,0:T(8,128)(2,1)}, bf16[16,4096]{1,0:T(8,128)(2,1)S(1)}, u32[]{:S(2)}, u32[]{:S(2)}) collective-permute-start(bf16[16,4096]{1,0:T(8,128)(2,1)} %get-tuple-element.53), channel_id=1, source_target_pairs={{0,48},{1,49},{2,50},{3,51},{4,52},{5,53},{6,54},{7,55},{8,56},{9,... | collective-permute-start | bytes 393224 | tf_op jit(solution)/shard_map/ppermute | solution.py:28
  15.1 12.8 %collective-permute-start.2 = (bf16[16,4096]{1,0:T(8,128)(2,1)}, bf16[16,4096]{1,0:T(8,128)(2,1)S(1)}, u32[]{:S(2)}, u32[]{:S(2)}) collective-permute-start(bf16[16,4096]{1,0:T(8,128)(2,1)} %get-tuple-element.48), channel_id=1, source_target_pairs={{0,4},{1,5},{2,6},{3,7},{4,8},{5,9},{6,10},{7,11},{8,12},{9,13},{1... | collective-permute-start | bytes 393224 | tf_op jit(solution)/shard_map/ppermute | solution.py:28
  18.0 11.0 %copy-start.1 = (bf16[2,304,608]{2,1,0:T(8,128)(2,1)S(1)}, bf16[2,304,608]{2,1,0:T(8,128)(2,1)}, u32[]{:S(2)}) copy-start(bf16[2,304,608]{2,1,0:T(8,128)(2,1)} %refs_15_.3) | copy-start | bytes 2217988
  18.0 10.9 %collective-permute-start.5 = (bf16[16,4096]{1,0:T(8,128)(2,1)S(1)}, bf16[16,4096]{1,0:T(8,128)(2,1)S(1)}, u32[]{:S(2)}, u32[]{:S(2)}) collective-permute-start(bf16[16,4096]{1,0:T(8,128)(2,1)S(1)} %copy-done.5), channel_id=1, source_target_pairs={{0,16},{1,17},{2,18},{3,19},{4,20},{5,21},{6,22},{7,23},{8,24},{9,... | collective-permute-start | bytes 393224 | tf_op jit(solution)/shard_map/ppermute | solution.py:28
  18.1 10.8 %collective-permute-start.7 = (bf16[16,4096]{1,0:T(8,128)(2,1)S(1)}, bf16[16,4096]{1,0:T(8,128)(2,1)S(1)}, u32[]{:S(2)}, u32[]{:S(2)}) collective-permute-start(bf16[16,4096]{1,0:T(8,128)(2,1)S(1)} %collective-permute-done.6), channel_id=1, source_target_pairs={{0,48},{1,49},{2,50},{3,51},{4,52},{5,53},{6,54},{7,55},{8,56},{9,... | collective-permute-start | bytes 393224 | tf_op jit(solution)/shard_map/ppermute | solution.py:28
  21.4 7.5 %collective-permute-start.4 = (bf16[16,4096]{1,0:T(8,128)(2,1)S(1)}, bf16[16,4096]{1,0:T(8,128)(2,1)S(1)}, u32[]{:S(2)}, u32[]{:S(2)}) collective-permute-start(bf16[16,4096]{1,0:T(8,128)(2,1)S(1)} %collective-permute-done.3), channel_id=1, source_target_pairs={{12,8},{13,9},{14,10},{15,11},{0,12},{1,13},{2,14},{3,15},{20,16},... | collective-permute-start | bytes 393224 | tf_op jit(solution)/shard_map/ppermute | solution.py:236
  34.6 8.8 %collective-permute-start.9 = (bf16[16,4096]{1,0:T(8,128)(2,1)S(1)}, bf16[16,4096]{1,0:T(8,128)(2,1)S(1)}, u32[]{:S(2)}, u32[]{:S(2)}) collective-permute-start(bf16[16,4096]{1,0:T(8,128)(2,1)S(1)} %get-tuple-element.64), channel_id=1, source_target_pairs={{0,2},{1,3},{2,4},{3,5},{4,6},{5,7},{6,8},{7,9},{8,10},{9,11},{10,... | collective-permute-start | bytes 393224 | tf_op jit(solution)/shard_map/ppermute | solution.py:28
  36.1 8.4 %collective-permute-start.11 = (bf16[16,4096]{1,0:T(8,128)(2,1)S(1)}, bf16[16,4096]{1,0:T(8,128)(2,1)S(1)}, u32[]{:S(2)}, u32[]{:S(2)}) collective-permute-start(bf16[16,4096]{1,0:T(8,128)(2,1)S(1)} %get-tuple-element.66), channel_id=1, source_target_pairs={{0,12},{1,13},{2,14},{3,15},{4,0},{5,1},{6,2},{7,3},{8,20},{9,21},... | collective-permute-start | bytes 393224 | tf_op jit(solution)/shard_map/ppermute | solution.py:236
  39.2 15.4 %collective-permute-start.8 = (bf16[32,4096]{1,0:T(8,128)(2,1)S(1)}, bf16[32,4096]{1,0:T(8,128)(2,1)S(1)}, u32[]{:S(2)}, u32[]{:S(2)}) collective-permute-start(bf16[32,4096]{1,0:T(8,128)(2,1)S(1)} %get-tuple-element.57), channel_id=1, source_target_pairs={{0,1},{1,2},{2,3},{3,4},{4,5},{5,6},{6,7},{7,8},{8,9},{9,10},{10,1... | collective-permute-start | bytes 786440 | tf_op jit(solution)/shard_map/ppermute | solution.py:28
  40.2 5.0 %collective-permute-start.14 = (bf16[16,4096]{1,0:T(8,128)(2,1)S(1)}, bf16[16,4096]{1,0:T(8,128)(2,1)S(1)}, u32[]{:S(2)}, u32[]{:S(2)}) collective-permute-start(bf16[16,4096]{1,0:T(8,128)(2,1)S(1)} %get-tuple-element.70), channel_id=1, source_target_pairs={{0,48},{1,49},{2,50},{3,51},{4,52},{5,53},{6,54},{7,55},{8,56},{9,... | collective-permute-start | bytes 393224 | tf_op jit(solution)/shard_map/ppermute | solution.py:28
  41.3 14.5 %collective-permute-start.10 = (bf16[16,4096]{1,0:T(8,128)(2,1)S(1)}, bf16[16,4096]{1,0:T(8,128)(2,1)S(1)}, u32[]{:S(2)}, u32[]{:S(2)}) collective-permute-start(bf16[16,4096]{1,0:T(8,128)(2,1)S(1)} %get-tuple-element.65), channel_id=1, source_target_pairs={{0,4},{1,5},{2,6},{3,7},{4,8},{5,9},{6,10},{7,11},{8,12},{9,13},{1... | collective-permute-start | bytes 393224 | tf_op jit(solution)/shard_map/ppermute | solution.py:28
  43.4 13.1 %collective-permute-start.13 = (bf16[16,4096]{1,0:T(8,128)(2,1)S(1)}, bf16[16,4096]{1,0:T(8,128)(2,1)S(1)}, u32[]{:S(2)}, u32[]{:S(2)}) collective-permute-start(bf16[16,4096]{1,0:T(8,128)(2,1)S(1)} %get-tuple-element.69), channel_id=1, source_target_pairs={{0,16},{1,17},{2,18},{3,19},{4,20},{5,21},{6,22},{7,23},{8,24},{9,... | collective-permute-start | bytes 393224 | tf_op jit(solution)/shard_map/ppermute | solution.py:28
  45.2 11.3 %collective-permute-start.15 = (bf16[16,4096]{1,0:T(8,128)(2,1)S(1)}, bf16[16,4096]{1,0:T(8,128)(2,1)S(1)}, u32[]{:S(2)}, u32[]{:S(2)}) collective-permute-start(bf16[16,4096]{1,0:T(8,128)(2,1)S(1)} %collective-permute-done.14), channel_id=1, source_target_pairs={{0,48},{1,49},{2,50},{3,51},{4,52},{5,53},{6,54},{7,55},{8,56},{9,... | collective-permute-start | bytes 393224 | tf_op jit(solution)/shard_map/ppermute | solution.py:28
  47.4 9.4 %collective-permute-start.12 = (bf16[16,4096]{1,0:T(8,128)(2,1)S(1)}, bf16[16,4096]{1,0:T(8,128)(2,1)S(1)}, u32[]{:S(2)}, u32[]{:S(2)}) collective-permute-start(bf16[16,4096]{1,0:T(8,128)(2,1)S(1)} %collective-permute-done.11), channel_id=1, source_target_pairs={{12,8},{13,9},{14,10},{15,11},{0,12},{1,13},{2,14},{3,15},{20,16},... | collective-permute-start | bytes 393224 | tf_op jit(solution)/shard_map/ppermute | solution.py:236
